TPU v7x, 32 devices: a whole 2x2x4 slice. The times are simulated.
32 devices in a mesh: shard: 4 (over y, x), ctx: 4 (over z), tp: 2 (over core).
Axes of the slice: x: 2, y: 2, z: 4, core: 2. Of those that a mesh axis runs over, the one named last changes fastest.
Arguments:
- block_entries: bfloat16 [2, 4, 1024, 1024], P(None, 'shard', 'ctx', 'tp'), may hold values from -6 to 6
- row_extents: int32 [2, 4], P(None, 'shard'), may hold values from 256 to 1024, as said below
- upstream_loss_deriv: bfloat16 [2, 4, 1024, 1024], P(None, 'shard', 'ctx', 'tp'), may hold values from -6 to 6
- earlier_layernorm_scaling: float32 [1024], P('tp'), may hold values from 0.25 to 1.75
- earlier_layernorm_offset: float32 [1024], P('tp'), may hold values from -1.2 to 1.2
- temporal_mix_lookup_fraction: float32 [1024], P('tp'), may hold values from 0.05 to 0.95
- temporal_mix_payload_fraction: float32 [1024], P('tp'), may hold values from 0.05 to 0.95
- temporal_mix_filter_fraction: float32 [1024], P('tp'), may hold values from 0.05 to 0.95
- logarithmic_fading_per_feature: float32 [1024], P('tp'), may hold values from -11 to -2.5
- present_entry_reward: float32 [1024], P('tp'), may hold values from -1 to 1
- filter_projection: bfloat16 [1024, 1024], P('shard', 'tp'), may hold values from -0.1875 to 0.1875
- lookup_projection: bfloat16 [1024, 1024], P('shard', 'tp'), may hold values from -0.1875 to 0.1875
- payload_projection: bfloat16 [1024, 1024], P('shard', 'tp'), may hold values from -0.1875 to 0.1875
- temporal_mix_emit_projection: bfloat16 [1024, 1024], P('tp', 'shard'), may hold values from -0.75 to 0.75
- later_layernorm_scaling: float32 [1024], P('tp'), may hold values from 0.25 to 1.75
- later_layernorm_offset: float32 [1024], P('tp'), may hold values from -1.2 to 1.2
- feature_mix_lookup_fraction: float32 [1024], P('tp'), may hold values from 0.05 to 0.95
- feature_mix_filter_fraction: float32 [1024], P('tp'), may hold values from 0.05 to 0.95
- feature_mix_lookup_proj: bfloat16 [1024, 4096], P('shard', 'tp'), may hold values from -0.1875 to 0.1875
- feature_mix_filter_proj: bfloat16 [1024, 1024], P('shard', 'tp'), may hold values from -0.1875 to 0.1875
- feature_mix_payload_proj: bfloat16 [4096, 1024], P('tp', 'shard'), may hold values from -0.09375 to 0.09375
Outputs:
- block_out: bfloat16 [2, 4, 1024, 1024], P(None, 'shard', 'ctx', 'tp')
- input_grad: float32 [2, 4, 1024, 1024], P(None, 'shard', 'ctx', 'tp')
- first_gain_grad: float32 [1024], P('tp')
- first_bias_grad: float32 [1024], P('tp')
- shift_key_grad: float32 [1024], P('tp')
- shift_value_grad: float32 [1024], P('tp')
- shift_gate_grad: float32 [1024], P('tp')
- decay_log_grad: float32 [1024], P('tp')
- time_bonus_grad: float32 [1024], P('tp')
- gate_weight_grad: float32 [1024, 1024], P(('shard', 'ctx'), 'tp')
- key_weight_grad: float32 [1024, 1024], P(('shard', 'ctx'), 'tp')
- value_weight_grad: float32 [1024, 1024], P(('shard', 'ctx'), 'tp')
- output_weight_grad: float32 [1024, 1024], P('tp', ('shard', 'ctx'))
- second_gain_grad: float32 [1024], P('tp')
- second_bias_grad: float32 [1024], P('tp')
- channel_shift_key_grad: float32 [1024], P('tp')
- channel_shift_gate_grad: float32 [1024], P('tp')
- hidden_weight_grad: float32 [1024, 4096], P(('shard', 'ctx'), 'tp')
- filter_weight_grad: float32 [1024, 1024], P(('shard', 'ctx'), 'tp')
- return_weight_grad: float32 [4096, 1024], P('tp', ('shard', 'ctx'))
Inputs may be any that keep to these rules, and one draw needn't show every extreme that they name: `row_extents`: each row's valid tokens come first; in every draw some row has exactly 1024 valid tokens and some row exactly 256.
All inputs are finite; a program needn't handle non-finite values.
Results may differ from a plain program's by a relative error of at most 0.011.
Values may be sent and summed in bfloat16 or wider, within the bound.
No kernel may reach another device: no remote copies, remote signals or barrier semaphores. Data moves between devices by JAX's collectives and lax.ppermute only.
A program may use at most 192 MiB of HBM per device.

v0:
```python
from functools import partial

import jax
import jax.numpy as jnp
from jax import lax
from jax.sharding import PartitionSpec as P

EMBED_SIZE = 1024


epsilon = 1e-05
lowest = -1e30


def entering(value, axis, join, neutral, backward):
    count, mine = (lax.axis_size(axis), lax.axis_index(axis))
    pieces = jax.tree.map(lambda part: lax.all_gather(part, axis), value)
    if backward:
        pieces = jax.tree.map(lambda part: part[::-1], pieces)
        mine = count - 1 - mine
    so_far = jax.tree.map(
        lambda part, zero: jnp.full_like(part, 0) + jnp.asarray(zero, part.dtype), value, neutral
    )

    def turn(position, so_far):
        longer = join(so_far, jax.tree.map(lambda part: part[position], pieces))
        return jax.tree.map(lambda new, old: jnp.where(position < mine, new, old), longer, so_far)

    return lax.fori_loop(0, count - 1, turn, so_far)


def from_behind(block, axis, distance):
    devices = range(lax.axis_size(axis))
    route = [(i - distance, i) for i in devices if i - distance in devices]
    return lax.ppermute(block, axis, route)


def combine_states(earlier, later):
    earlier_num, earlier_den, earlier_high, earlier_span = earlier
    later_num, later_den, later_high, later_span = later
    shifted = earlier_high + later_span
    utmost_accuracy_level = jnp.maximum(shifted, later_high)
    earlier_part = jnp.exp(shifted - utmost_accuracy_level)
    later_part = jnp.exp(later_high - utmost_accuracy_level)
    return (
        earlier_num * earlier_part + later_num * later_part,
        earlier_den * earlier_part + later_den * later_part,
        utmost_accuracy_level,
        earlier_span + later_span,
    )


def stretch_states(lookup_series, payload_series, feature_fading_factor):
    step_spans = jnp.broadcast_to(-feature_fading_factor, lookup_series.shape)
    unit_weights = jnp.ones_like(lookup_series)
    inclusive = lax.associative_scan(
        combine_states, (payload_series, unit_weights, lookup_series, step_spans), axis=0
    )
    closing = (inclusive[0][-1], inclusive[1][-1], inclusive[2][-1])
    zero_first = jnp.zeros_like(lookup_series[:1])
    low_first = jnp.full_like(lookup_series[:1], lowest)
    prior_value = (
        jnp.concatenate([zero_first, inclusive[0][:-1]], axis=0),
        jnp.concatenate([zero_first, inclusive[1][:-1]], axis=0),
        jnp.concatenate([low_first, inclusive[2][:-1]], axis=0),
    )
    return (prior_value, closing)


def complete_span_pass(
    entering_carry,
    prior_value,
    lookup_series,
    payload_series,
    feature_fading_factor,
    present_entry_reward,
):
    steps_back = jnp.arange(lookup_series.shape[0], dtype=jnp.float32)[:, None, None]
    carried_high = entering_carry[2][None] - steps_back * feature_fading_factor
    utmost_accuracy_level = jnp.maximum(carried_high, prior_value[2])
    carried = jnp.exp(carried_high - utmost_accuracy_level)
    local_part = jnp.exp(prior_value[2] - utmost_accuracy_level)
    state_num = entering_carry[0][None] * carried + prior_value[0] * local_part
    state_den = entering_carry[1][None] * carried + prior_value[1] * local_part
    with_present_reward = present_entry_reward + lookup_series
    largest_power_level = jnp.maximum(utmost_accuracy_level, with_present_reward)
    old_part = jnp.exp(utmost_accuracy_level - largest_power_level)
    newly_added_part = jnp.exp(with_present_reward - largest_power_level)
    denominator = old_part * state_den + newly_added_part
    final_output = (old_part * state_num + newly_added_part * payload_series) / denominator
    return (final_output, (carried_high, largest_power_level, denominator))


def span_forward_pass(
    entering_carry,
    lookup_series,
    payload_series,
    logarithmic_fading_per_feature,
    present_entry_reward,
):
    feature_fading_factor = jnp.exp(logarithmic_fading_per_feature)
    prior_value, closing = stretch_states(lookup_series, payload_series, feature_fading_factor)
    final_output, helper_functions = complete_span_pass(
        entering_carry,
        prior_value,
        lookup_series,
        payload_series,
        feature_fading_factor,
        present_entry_reward,
    )
    return ((final_output, closing[0], closing[1], closing[2]), helper_functions)


def weighted_kv_backward(
    entering_carry,
    lookup_series,
    payload_series,
    logarithmic_fading_per_feature,
    present_entry_reward,
    result_gradient,
):
    primal, pullback, helper_functions = jax.vjp(
        partial(span_forward_pass, entering_carry),
        lookup_series,
        payload_series,
        logarithmic_fading_per_feature,
        present_entry_reward,
        has_aux=True,
    )
    final_output, closing_num, closing_den, closing_high = primal
    carried_high, largest_power_level, denominator = helper_functions
    factor = jnp.exp(carried_high - largest_power_level) / denominator
    direct_num = jnp.sum(result_gradient * factor, axis=0)
    direct_den = -jnp.sum(result_gradient * final_output * factor, axis=0)
    count = lookup_series.shape[0]
    feature_fading_factor = jnp.exp(logarithmic_fading_per_feature)
    stretch_span = jnp.broadcast_to(-count * feature_fading_factor, direct_num.shape)
    adjoint_level = jnp.where(entering_carry[2] < 0.5 * lowest, lowest, -entering_carry[2])
    empty_state = jnp.zeros_like(stretch_span)
    adjoint = entering(
        (direct_num, direct_den, adjoint_level, stretch_span),
        "ctx",
        combine_states,
        (empty_state, empty_state, jnp.full_like(stretch_span, lowest), empty_state),
        True,
    )
    anchor = -adjoint[2]
    closing_part = jnp.exp(closing_high - anchor)
    carried_part = jnp.exp(entering_carry[2] - count * feature_fading_factor - anchor)
    pulled = pullback(
        (
            result_gradient,
            adjoint[0] * closing_part,
            adjoint[1] * closing_part,
            (adjoint[0] * closing_num + adjoint[1] * closing_den) * closing_part,
        )
    )
    decay_extra = (
        -count
        * jnp.sum(
            (adjoint[0] * entering_carry[0] + adjoint[1] * entering_carry[1]) * carried_part, axis=0
        )
        * feature_fading_factor
    )
    return (pulled[0], pulled[1], pulled[2] + decay_extra, pulled[3])


def widen_features(stacked):
    return lax.all_gather(stacked, "tp", axis=2, tiled=True)


def narrow(stacked):
    return lax.psum_scatter(stacked, "tp", scatter_dimension=2, tiled=True)


def channel_sums(first_sum, second_sum):
    return lax.psum((first_sum, second_sum), "tp")


def norm_forward(values, norm_gain, norm_bias):
    row_total, squares = channel_sums(jnp.sum(values, axis=-1), jnp.sum(values * values, axis=-1))
    center = row_total / EMBED_SIZE
    inverse_root = lax.rsqrt(squares / EMBED_SIZE - center * center + epsilon)
    normed = (values - center[:, None]) * inverse_root[:, None]
    return (normed * norm_gain + norm_bias, normed, inverse_root)


def norm_backward(grad_out, normed, inverse_root, norm_gain):
    scaled = grad_out * norm_gain
    first_total, second_total = channel_sums(
        jnp.sum(scaled, axis=-1), jnp.sum(scaled * normed, axis=-1)
    )
    grad_in = inverse_root[:, None] * (
        scaled - first_total[:, None] / EMBED_SIZE - normed * second_total[:, None] / EMBED_SIZE
    )
    return (grad_in, jnp.sum(grad_out * normed, axis=0), jnp.sum(grad_out, axis=0))


def shift_tokens(normed, row_count):
    token_grid = normed.reshape(row_count, -1, normed.shape[-1])
    edge_rows = from_behind(token_grid[:, -1, :], "ctx", 1)
    return jnp.concatenate([edge_rows[:, None, :], token_grid[:, :-1, :]], axis=1).reshape(
        normed.shape
    )


def unshift_tokens(grad_prev, row_count):
    token_grid = grad_prev.reshape(row_count, -1, grad_prev.shape[-1])
    edge_rows = from_behind(token_grid[:, 0, :], "ctx", -1)
    return jnp.concatenate([token_grid[:, 1:, :], edge_rows[:, None, :]], axis=1).reshape(
        grad_prev.shape
    )


def dot_float(left_side, right_side):
    return jnp.dot(left_side, right_side, preferred_element_type=jnp.float32)


def per_device(
    block_entries,
    row_extents,
    upstream_loss_deriv,
    earlier_layernorm_scaling,
    earlier_layernorm_offset,
    temporal_mix_lookup_fraction,
    temporal_mix_payload_fraction,
    temporal_mix_filter_fraction,
    logarithmic_fading_per_feature,
    present_entry_reward,
    filter_projection,
    lookup_projection,
    payload_projection,
    temporal_mix_emit_projection,
    later_layernorm_scaling,
    later_layernorm_offset,
    feature_mix_lookup_fraction,
    feature_mix_filter_fraction,
    feature_mix_lookup_proj,
    feature_mix_filter_proj,
    feature_mix_payload_proj,
):
    row_count = block_entries.shape[1]
    stretch_len = block_entries.shape[2]
    width_half = block_entries.shape[3]
    token_count = row_count * stretch_len
    positions = lax.axis_index("ctx") * stretch_len + jnp.arange(stretch_len, dtype=jnp.int32)
    time_mixes = jnp.stack(
        [temporal_mix_lookup_fraction, temporal_mix_payload_fraction, temporal_mix_filter_fraction]
    )[:, None, :]
    channel_mixes = jnp.stack([feature_mix_lookup_fraction, feature_mix_filter_fraction])[
        :, None, :
    ]

    def into_sequence(tokens):
        return tokens.reshape(row_count, stretch_len, width_half).transpose(1, 0, 2)

    def to_tokens(timed):
        return timed.transpose(1, 0, 2).reshape(token_count, width_half)

    outputs_list = []
    input_list = []
    vector_sums = None
    weight_shares = None
    for batch_index in range(block_entries.shape[0]):
        gate_full = lax.all_gather(filter_projection, "shard", axis=0, tiled=True)
        key_full = lax.all_gather(lookup_projection, "shard", axis=0, tiled=True)
        value_full = lax.all_gather(payload_projection, "shard", axis=0, tiled=True)
        output_full = lax.all_gather(temporal_mix_emit_projection, "shard", axis=1, tiled=True)
        hidden_full = lax.all_gather(feature_mix_lookup_proj, "shard", axis=0, tiled=True)
        filter_full = lax.all_gather(feature_mix_filter_proj, "shard", axis=0, tiled=True)
        return_full = lax.all_gather(feature_mix_payload_proj, "shard", axis=1, tiled=True)
        live_mask = (
            (positions[None, :] < row_extents[batch_index][:, None])
            .astype(jnp.float32)
            .reshape(token_count, 1)
        )
        values = block_entries[batch_index].astype(jnp.float32).reshape(token_count, width_half)
        normed_one, hat_one, root_one = norm_forward(
            values, earlier_layernorm_scaling, earlier_layernorm_offset
        )
        prev_one = shift_tokens(normed_one, row_count)
        time_mixed = (normed_one[None] * time_mixes + prev_one[None] * (1.0 - time_mixes)).astype(
            jnp.bfloat16
        )
        mixed_full = widen_features(time_mixed)
        lookup_mapped = dot_float(mixed_full[0], key_full)
        payload_mapped = dot_float(mixed_full[1], value_full)
        gate_logit = dot_float(mixed_full[2], gate_full)
        lookup_series = into_sequence(lookup_mapped)
        payload_series = into_sequence(payload_mapped)
        feature_fading_factor = jnp.exp(logarithmic_fading_per_feature)
        prior_value, closing = stretch_states(lookup_series, payload_series, feature_fading_factor)
        stretch_span = jnp.broadcast_to(-stretch_len * feature_fading_factor, closing[0].shape)
        empty_state = jnp.zeros_like(stretch_span)
        scanned = entering(
            (closing[0], closing[1], closing[2], stretch_span),
            "ctx",
            combine_states,
            (empty_state, empty_state, jnp.full_like(stretch_span, lowest), empty_state),
            False,
        )
        entering_carry = (scanned[0], scanned[1], scanned[2])
        result_time, helper_functions = complete_span_pass(
            entering_carry,
            prior_value,
            lookup_series,
            payload_series,
            feature_fading_factor,
            present_entry_reward,
        )
        final_output = to_tokens(result_time)
        gate_open = jax.nn.sigmoid(gate_logit)
        gated = (gate_open * final_output).astype(jnp.bfloat16)
        attended = narrow(dot_float(gated, output_full)[None])[0]
        middle = values + attended
        normed_two, hat_two, root_two = norm_forward(
            middle, later_layernorm_scaling, later_layernorm_offset
        )
        prev_two = shift_tokens(normed_two, row_count)
        channel_mixed = (
            normed_two[None] * channel_mixes + prev_two[None] * (1.0 - channel_mixes)
        ).astype(jnp.bfloat16)
        channel_full = widen_features(channel_mixed)
        hidden_pre = dot_float(channel_full[0], hidden_full)
        squared = jnp.square(jax.nn.relu(hidden_pre)).astype(jnp.bfloat16)
        returned = narrow(dot_float(squared, return_full)[None])[0]
        filter_logit = dot_float(channel_full[1], filter_full)
        filter_open = jax.nn.sigmoid(filter_logit)
        output = (live_mask * (middle + filter_open * returned)).astype(jnp.bfloat16)
        grad_out = (
            upstream_loss_deriv[batch_index].astype(jnp.float32).reshape(token_count, width_half)
            * live_mask
        )
        grad_returned = (grad_out * filter_open).astype(jnp.bfloat16)
        grad_filter = (grad_out * returned * filter_open * (1.0 - filter_open)).astype(jnp.bfloat16)
        returned_full = widen_features(grad_returned[None])[0]
        grad_squared = dot_float(returned_full, return_full.T)
        grad_hidden = (grad_squared * 2.0 * jax.nn.relu(hidden_pre)).astype(jnp.bfloat16)
        grad_return_w = dot_float(squared.T, returned_full)
        grad_hidden_w = dot_float(channel_full[0].T, grad_hidden)
        grad_filter_w = dot_float(channel_full[1].T, grad_filter)
        grad_channel = narrow(
            jnp.stack(
                [dot_float(grad_hidden, hidden_full.T), dot_float(grad_filter, filter_full.T)]
            )
        )
        grad_channel_mix = jnp.sum(grad_channel * (normed_two - prev_two)[None], axis=1)
        grad_normed_two = jnp.sum(grad_channel * channel_mixes, axis=0) + unshift_tokens(
            jnp.sum(grad_channel * (1.0 - channel_mixes), axis=0), row_count
        )
        grad_middle_norm, grad_second_gain, grad_second_bias = norm_backward(
            grad_normed_two, hat_two, root_two, later_layernorm_scaling
        )
        grad_middle = grad_out + grad_middle_norm
        middle_full = widen_features(grad_middle.astype(jnp.bfloat16)[None])[0]
        grad_output_w = dot_float(gated.T, middle_full)
        grad_gated = dot_float(middle_full, output_full.T)
        result_gradient = grad_gated * gate_open
        grad_gate = (grad_gated * final_output * gate_open * (1.0 - gate_open)).astype(jnp.bfloat16)
        temporal_lookup_deriv, temporal_payload_deriv, fading_deriv, extra_reward_deriv = (
            weighted_kv_backward(
                entering_carry,
                lookup_series,
                payload_series,
                logarithmic_fading_per_feature,
                present_entry_reward,
                into_sequence(result_gradient),
            )
        )
        grad_key = to_tokens(temporal_lookup_deriv).astype(jnp.bfloat16)
        grad_value = to_tokens(temporal_payload_deriv).astype(jnp.bfloat16)
        grad_key_w = dot_float(mixed_full[0].T, grad_key)
        grad_value_w = dot_float(mixed_full[1].T, grad_value)
        grad_gate_w = dot_float(mixed_full[2].T, grad_gate)
        grad_time = narrow(
            jnp.stack(
                [
                    dot_float(grad_key, key_full.T),
                    dot_float(grad_value, value_full.T),
                    dot_float(grad_gate, gate_full.T),
                ]
            )
        )
        grad_time_mix = jnp.sum(grad_time * (normed_one - prev_one)[None], axis=1)
        grad_normed_one = jnp.sum(grad_time * time_mixes, axis=0) + unshift_tokens(
            jnp.sum(grad_time * (1.0 - time_mixes), axis=0), row_count
        )
        grad_input_norm, grad_first_gain, grad_first_bias = norm_backward(
            grad_normed_one, hat_one, root_one, earlier_layernorm_scaling
        )
        grad_input = (grad_middle + grad_input_norm).reshape(row_count, stretch_len, width_half)
        weight_grads = (
            grad_gate_w,
            grad_key_w,
            grad_value_w,
            grad_output_w,
            grad_hidden_w,
            grad_filter_w,
            grad_return_w,
        )
        vector_parts = (
            grad_first_gain,
            grad_first_bias,
            grad_time_mix[0],
            grad_time_mix[1],
            grad_time_mix[2],
            fading_deriv,
            extra_reward_deriv,
            grad_second_gain,
            grad_second_bias,
            grad_channel_mix[0],
            grad_channel_mix[1],
        )
        output, grad_input, weight_grads, vector_parts = (
            output.reshape(row_count, stretch_len, width_half),
            grad_input,
            weight_grads,
            vector_parts,
        )
        outputs_list.append(output)
        input_list.append(grad_input)
        shares = (
            lax.psum_scatter(weight_grads[0], ("shard", "ctx"), scatter_dimension=0, tiled=True),
            lax.psum_scatter(weight_grads[1], ("shard", "ctx"), scatter_dimension=0, tiled=True),
            lax.psum_scatter(weight_grads[2], ("shard", "ctx"), scatter_dimension=0, tiled=True),
            lax.psum_scatter(weight_grads[3], ("shard", "ctx"), scatter_dimension=1, tiled=True),
            lax.psum_scatter(weight_grads[4], ("shard", "ctx"), scatter_dimension=0, tiled=True),
            lax.psum_scatter(weight_grads[5], ("shard", "ctx"), scatter_dimension=0, tiled=True),
            lax.psum_scatter(weight_grads[6], ("shard", "ctx"), scatter_dimension=1, tiled=True),
        )
        weight_shares = (
            shares if weight_shares is None else jax.tree.map(jnp.add, weight_shares, shares)
        )
        vector_sums = (
            vector_parts
            if vector_sums is None
            else jax.tree.map(jnp.add, vector_sums, vector_parts)
        )
    vectors = lax.psum(
        (
            vector_sums[0],
            vector_sums[1],
            vector_sums[2],
            vector_sums[3],
            vector_sums[4],
            vector_sums[5],
            vector_sums[6],
            vector_sums[7],
            vector_sums[8],
            vector_sums[9],
            vector_sums[10],
        ),
        ("shard", "ctx"),
    )
    block_out = jnp.stack(outputs_list)
    input_grad = jnp.stack(input_list)
    return (
        block_out,
        input_grad,
        vectors[0],
        vectors[1],
        vectors[2],
        vectors[3],
        vectors[4],
        vectors[5],
        vectors[6],
        weight_shares[0],
        weight_shares[1],
        weight_shares[2],
        weight_shares[3],
        vectors[7],
        vectors[8],
        vectors[9],
        vectors[10],
        weight_shares[4],
        weight_shares[5],
        weight_shares[6],
    )


def solution(mesh):
    return jax.shard_map(
        per_device,
        mesh=mesh,
        in_specs=(
            P(None, "shard", "ctx", "tp"),
            P(None, "shard"),
            P(None, "shard", "ctx", "tp"),
            P("tp"),
            P("tp"),
            P("tp"),
            P("tp"),
            P("tp"),
            P("tp"),
            P("tp"),
            P("shard", "tp"),
            P("shard", "tp"),
            P("shard", "tp"),
            P("tp", "shard"),
            P("tp"),
            P("tp"),
            P("tp"),
            P("tp"),
            P("shard", "tp"),
            P("shard", "tp"),
            P("tp", "shard"),
        ),
        out_specs=(
            P(None, "shard", "ctx", "tp"),
            P(None, "shard", "ctx", "tp"),
            P("tp"),
            P("tp"),
            P("tp"),
            P("tp"),
            P("tp"),
            P("tp"),
            P("tp"),
            P(("shard", "ctx"), "tp"),
            P(("shard", "ctx"), "tp"),
            P(("shard", "ctx"), "tp"),
            P("tp", ("shard", "ctx")),
            P("tp"),
            P("tp"),
            P("tp"),
            P("tp"),
            P(("shard", "ctx"), "tp"),
            P(("shard", "ctx"), "tp"),
            P("tp", ("shard", "ctx")),
        ),
        check_vma=False,
    )
```

profile of v0, /device:TPU:0, one launch (start us, length us, event | category | flops | bytes accessed | tf_op | source)
XLA Modules:
  0.0 2127.7 jit_solution(12084722905089830674)
XLA Ops:
  30.2 13.3 all-gather.9
  43.6 7.0 all-gather.46.cloned.1.call-done
  55.6 8.1 all-gather.28.cloned.1.call-done
  68.8 24.4 %all-gather.34.cloned.1.call-done = bf16[1024,512]{1,0:T(8,128)(2,1)} async-done(((bf16[256,512]{1,0:T(8,128)(2,1)}), bf16[1024,512]{1,0:T(8,128)(2,1)}) %all-gather.34.cloned.1.call-update) | async-done | bytes 1048592 | tf_op jit(solution)/shard_map/all_gather | solution.py:267
  378.4 12.4 all_gather.123
  394.1 12.5 all_gather.114
  408.0 12.2 all_gather.122
  421.7 12.5 all_gather.112
  435.8 11.9 all_gather.124
  454.2 12.3 all_gather.115
  491.4 12.1 reduce-scatter.20.cloned.1.call-done
  522.3 7.3 all-gather.48.cloned.1.call-done
  529.6 55.6 %all-gather.42.cloned.1.call-done = bf16[1024,2048]{1,0:T(8,128)(2,1)} async-done(((bf16[256,2048]{1,0:T(8,128)(2,1)}), bf16[1024,2048]{1,0:T(8,128)(2,1)}) %all-gather.42.cloned.1.call-update) | async-done | bytes 4194320 | tf_op jit(solution)/shard_map/all_gather | solution.py:269
  588.8 50.8 %all-gather.44.cloned.1.call-done = bf16[2048,1024]{1,0:T(8,128)(2,1)} async-done(((bf16[2048,256]{1,0:T(8,128)(2,1)}), bf16[2048,1024]{1,0:T(8,128)(2,1)}) %all-gather.44.cloned.1.call-update) | async-done | bytes 4194320 | tf_op jit(solution)/shard_map/all_gather | solution.py:271
  644.5 5.6 all-gather.38.cloned.1.call-done
  660.7 19.1 all-gather.40.cloned.1.call-done
  682.4 8.5 reduce-scatter.22.cloned.1.call-done
  691.0 11.9 reduce-scatter.18.cloned.1.call-done
  729.0 12.1 all-gather.13
  753.1 14.2 all-gather.10
  794.2 12.4 all-gather.14
  808.0 12.6 all-gather.15
  834.8 12.5 all-gather.11
  848.6 12.7 all-gather.12
  866.6 8.2 multiply_reduce_fusion.15
  1388.4 75.0 %all-reduce.374 = (f32[512]{0:T(512)}, f32[512]{0:T(512)}, f32[512]{0:T(512)}, f32[512]{0:T(512)}, f32[512]{0:T(512)}, /*index=5*/f32[512]{0:T(512)}, f32[512]{0...) all-reduce(f32[512]{0:T(512)S(1)} %add.2208, ...), channel_id=1, replica_groups=mesh['shard'=4,'ctx'=4,'tp'=2] {'shard','ctx'}, use_global_device_ids=true, to_apply=%region_62.63 | all-reduce | flops 5632 | bytes 45056 | tf_op jit(solution)/shard_map/psum | solution.py:439
  1467.9 37.8 %reduce-scatter.38.cloned.1.call-done = f32[512,64]{0,1:T(8,128)} async-done(((f32[512,1024]{0,1:T(8,128)}), f32[512,64]{0,1:T(8,128)}) %reduce-scatter.38.cloned.1.call-update) | async-done | bytes 131088 | tf_op jit(solution)/shard_map/reduce_scatter | solution.py:426
  1505.6 83.7 %reduce-scatter.34.cloned.1.call-done = f32[64,512]{1,0:T(8,128)} async-done(((f32[1024,512]{1,0:T(8,128)}), f32[64,512]{1,0:T(8,128)}) %reduce-scatter.34.cloned.1.call-update) | async-done | bytes 131088 | tf_op jit(solution)/shard_map/reduce_scatter | solution.py:424
  1589.3 83.8 %reduce-scatter.36.cloned.1.call-done = f32[64,512]{1,0:T(8,128)} async-done(((f32[1024,512]{1,0:T(8,128)}), f32[64,512]{1,0:T(8,128)}) %reduce-scatter.36.cloned.1.call-update) | async-done | bytes 131088 | tf_op jit(solution)/shard_map/reduce_scatter | solution.py:425
  1673.1 83.4 %reduce-scatter.32.cloned.1.call-done = f32[64,512]{1,0:T(8,128)} async-done(((f32[1024,512]{1,0:T(8,128)}), f32[64,512]{1,0:T(8,128)}) %reduce-scatter.32.cloned.1.call-update) | async-done | bytes 131088 | tf_op jit(solution)/shard_map/reduce_scatter | solution.py:423
  1756.5 181.9 %reduce-scatter.44.cloned.1.call-done = f32[2048,64]{0,1:T(8,128)} async-done(((f32[2048,1024]{0,1:T(8,128)}), f32[2048,64]{0,1:T(8,128)}) %reduce-scatter.44.cloned.1.call-update) | async-done | bytes 524304 | tf_op jit(solution)/shard_map/reduce_scatter | solution.py:429
  1938.4 182.6 %reduce-scatter.40.cloned.1.call-done = f32[64,2048]{1,0:T(8,128)} async-done(((f32[1024,2048]{1,0:T(8,128)}), f32[64,2048]{1,0:T(8,128)}) %reduce-scatter.40.cloned.1.call-update) | async-done | bytes 524304 | tf_op jit(solution)/shard_map/reduce_scatter | solution.py:427
  (2261 shorter events, 1010.6 us)
Async XLA Ops:
  7.2 36.4 %all-gather.32.cloned.1.call-start = ((), (), s32[]{:S(2)}) async-start(), calls=%async_computation.17 | async-start | bytes 1310720 | tf_op jit(solution)/shard_map/all_gather | solution.py:266
  7.9 42.7 %all-gather.46.cloned.1.call-start = ((), (), s32[]{:S(2)}) async-start(), calls=%async_computation.26 | async-start | bytes 2359296 | tf_op jit(solution)/shard_map/all_gather | solution.py:169
  14.4 8.7 collective-permute-start.2
  27.0 36.7 %all-gather.28.cloned.1.call-start = ((), (), s32[]{:S(2)}) async-start(), calls=%async_computation.15 | async-start | bytes 2359296 | tf_op jit(solution)/shard_map/all_gather | solution.py:169
  27.7 65.5 %all-gather.34.cloned.1.call-start = ((), (), s32[]{:S(2)}) async-start(), calls=%async_computation.18 | async-start | bytes 1310720 | tf_op jit(solution)/shard_map/all_gather | solution.py:267
  28.3 438.2 %all-gather.30.cloned.1.call-start = ((), (), s32[]{:S(2)}) async-start(), calls=%async_computation.16 | async-start | bytes 1310720 | tf_op jit(solution)/shard_map/all_gather | solution.py:265
  28.9 453.3 %all-gather.36.cloned.1.call-start = ((), (), s32[]{:S(2)}) async-start(), calls=%async_computation.19 | async-start | bytes 1310720 | tf_op jit(solution)/shard_map/all_gather | solution.py:268
  29.5 462.0 %reduce-scatter.16.cloned.1.call-start = ((), (), s32[]{:S(2)}) async-start(), calls=%async_computation.20 | async-start | bytes 1572864 | tf_op jit(solution)/shard_map/reduce_scatter | solution.py:173
  485.0 18.5 reduce-scatter.20.cloned.1.call-start
  486.6 43.0 %all-gather.48.cloned.1.call-start = ((), (), s32[]{:S(2)}) async-start(), calls=%async_computation.28 | async-start | bytes 1572864 | tf_op jit(solution)/shard_map/all_gather | solution.py:169
  509.0 7.1 collective-permute-start.1
  519.6 65.6 %all-gather.42.cloned.1.call-start = ((), (), s32[]{:S(2)}) async-start(), calls=%async_computation.23 | async-start | bytes 5242880 | tf_op jit(solution)/shard_map/all_gather | solution.py:269
  520.2 119.4 %all-gather.44.cloned.1.call-start = ((), (), s32[]{:S(2)}) async-start(), calls=%async_computation.24 | async-start | bytes 5242880 | tf_op jit(solution)/shard_map/all_gather | solution.py:271
  520.9 129.1 %all-gather.38.cloned.1.call-start = ((), (), s32[]{:S(2)}) async-start(), calls=%async_computation.21 | async-start | bytes 1572864 | tf_op jit(solution)/shard_map/all_gather | solution.py:169
  521.5 158.2 %all-gather.40.cloned.1.call-start = ((), (), s32[]{:S(2)}) async-start(), calls=%async_computation.22 | async-start | bytes 1310720 | tf_op jit(solution)/shard_map/all_gather | solution.py:270
  522.2 168.7 %reduce-scatter.22.cloned.1.call-start = ((), (), s32[]{:S(2)}) async-start(), calls=%async_computation.29 | async-start | bytes 1572864 | tf_op jit(solution)/shard_map/reduce_scatter | solution.py:173
  644.0 58.9 %reduce-scatter.18.cloned.1.call-start = ((), (), s32[]{:S(2)}) async-start(), calls=%async_computation.25 | async-start | bytes 1572864 | tf_op jit(solution)/shard_map/reduce_scatter | solution.py:173
  657.4 88.1 %reduce-scatter.28.cloned.1.call-start = ((), (), s32[]{:S(2)}) async-start(), calls=%async_computation.32 | async-start | bytes 3145728 | tf_op jit(solution)/shard_map/reduce_scatter | solution.py:173
  715.3 30.2 %reduce-scatter.24.cloned.1.call-start = ((), (), s32[]{:S(2)}) async-start(), calls=%async_computation.30 | async-start | bytes 3145728 | tf_op jit(solution)/shard_map/reduce_scatter | solution.py:173
  726.9 647.5 %reduce-scatter.30.cloned.1.call-start = ((), (), s32[]{:S(2)}) async-start(), calls=%async_computation.33 | async-start | bytes 4718592 | tf_op jit(solution)/shard_map/reduce_scatter | solution.py:173
  750.5 22.5 %collective-permute-start.6 = (f32[1,512]{1,0:T(1,128)}, f32[1,512]{1,0:T(1,128)}, u32[]{:S(2)}, u32[]{:S(2)}) collective-permute-start(f32[1,512]{1,0:T(1,128)} %slice_bitcast_fusion.31), channel_id=1, source_target_pairs={{2,0},{4,2},{6,4},{3,1},{5,3},{7,5},{10,8},{12,10},{14,12},{11,9},... | collective-permute-start | bytes 6152 | tf_op jit(solution)/shard_map/ppermute | solution.py:35
  751.7 21.2 collective-permute-start.4
  1301.4 73.0 %reduce-scatter.26.cloned.1.call-start = ((), (), s32[]{:S(2)}) async-start(), calls=%async_computation.31 | async-start | bytes 4718592 | tf_op jit(solution)/shard_map/reduce_scatter | solution.py:173
  1323.3 144.5 %reduce-scatter.42.cloned.1.call-start = ((), (), s32[]{:S(2)}) async-start(), calls=%async_computation.39 | async-start | bytes 2228224 | tf_op jit(solution)/shard_map/reduce_scatter | solution.py:428
  1327.6 178.0 %reduce-scatter.38.cloned.1.call-start = ((), (), s32[]{:S(2)}) async-start(), calls=%async_computation.37 | async-start | bytes 2228224 | tf_op jit(solution)/shard_map/reduce_scatter | solution.py:426
  1332.2 257.1 %reduce-scatter.34.cloned.1.call-start = ((), (), s32[]{:S(2)}) async-start(), calls=%async_computation.35 | async-start | bytes 2228224 | tf_op jit(solution)/shard_map/reduce_scatter | solution.py:424
  1337.5 335.6 %reduce-scatter.36.cloned.1.call-start = ((), (), s32[]{:S(2)}) async-start(), calls=%async_computation.36 | async-start | bytes 2228224 | tf_op jit(solution)/shard_map/reduce_scatter | solution.py:425
  1342.9 413.6 %reduce-scatter.32.cloned.1.call-start = ((), (), s32[]{:S(2)}) async-start(), calls=%async_computation.34 | async-start | bytes 2228224 | tf_op jit(solution)/shard_map/reduce_scatter | solution.py:423
  1348.2 590.2 %reduce-scatter.44.cloned.1.call-start = ((), (), s32[]{:S(2)}) async-start(), calls=%async_computation.40 | async-start | bytes 8912896 | tf_op jit(solution)/shard_map/reduce_scatter | solution.py:429
  1356.0 764.9 %reduce-scatter.40.cloned.1.call-start = ((), (), s32[]{:S(2)}) async-start(), calls=%async_computation.38 | async-start | bytes 8912896 | tf_op jit(solution)/shard_map/reduce_scatter | solution.py:427
  1377.4 5.6 collective-permute-start.7
  1378.9 6.1 collective-permute-start.5
  (613 other events, 10481.6 us)
Sparse Core Ops, SparseCore 0:
  9.9 29.3 all-gather.31
  40.8 9.7 all-gather.45
  52.7 10.9 all-gather.27
  65.4 27.7 all-gather.33
  95.0 26.6 all-gather.29
  123.3 26.4 all-gather.35
  485.2 6.2 reduce-scatter.15
  493.8 9.6 reduce-scatter.19
  519.7 9.7 all-gather.47
  531.2 53.8 all-gather.41
  587.0 52.5 all-gather.43
  641.0 9.0 all-gather.37
  651.9 27.7 all-gather.39
  682.4 8.5 reduce-scatter.21
  693.1 9.6 reduce-scatter.17
  715.4 10.7 reduce-scatter.27
  728.4 10.7 reduce-scatter.23
  1301.5 9.4 reduce-scatter.29
  1323.4 9.3 reduce-scatter.25
  1335.6 85.7 reduce-scatter.41
  1424.2 81.3 reduce-scatter.37
  1508.5 80.7 reduce-scatter.33
  1592.2 80.8 reduce-scatter.35
  1675.8 80.6 reduce-scatter.31
  1759.4 178.9 reduce-scatter.43
  1941.1 179.8 reduce-scatter.39
where the time goes:
time: 2150 us; the launch traced here: 2130 us
  waiting for transfers between devices  879 us (41%)
  local copies, waits for them, and re-layouts  565 us (26%)
  other arithmetic  285 us (13%)
  blocking collectives  259 us (12%)
  matrix products  94.7 us (4%)
  between operations  22.7 us (1%)
  starting transfers between devices  22.3 us (1%)
    pad x273, local copies, waits for them, and re-layouts, stretch_states(): lax.associative_scan(combine_states, (payload_series, unit_weights, looku...  283 us
    slice x232, local copies, waits for them, and re-layouts, stretch_states(): lax.associative_scan(combine_states, (payload_series, unit_weights, looku...  206 us
    reduce_scatter x1, waiting for transfers between devices, per_device(): lax.psum_scatter(weight_grads[4], ('shard', 'ctx'), scatter_dimension=0,...  183 us
    reduce_scatter x1, waiting for transfers between devices, per_device(): lax.psum_scatter(weight_grads[6], ('shard', 'ctx'), scatter_dimension=1,...  182 us
    all_gather x13, blocking collectives, entering(): pieces = jax.tree.map(lambda part: lax.all_gather(part, axis), value)  164 us
    dot_general x42, matrix products, dot_float(): return jnp.dot(left_side, right_side, preferred_element_type=jnp.float32)  94.7 us
    reduce_scatter x1, waiting for transfers between devices, per_device(): lax.psum_scatter(weight_grads[2], ('shard', 'ctx'), scatter_dimension=0,...  83.8 us
    reduce_scatter x1, waiting for transfers between devices, per_device(): lax.psum_scatter(weight_grads[1], ('shard', 'ctx'), scatter_dimension=0,...  83.7 us
  transfers between devices with their start and end apart: 34, of which 22 were waited for; matrix products, arithmetic and copies ran while one was open for 20% of the time, Pallas kernels for 0%

commit v1 on v0

v1 whole, which is shorter than its diff:
```python
import jax
import jax.numpy as jnp
from jax import lax
from jax.experimental import pallas as pl
from jax.experimental.pallas import tpu as pltpu
from jax.sharding import PartitionSpec as P

F32, BF16 = jnp.float32, jnp.bfloat16
WIDTH = 1024
epsilon = 1e-05
lowest = -1e30
CHUNKS = 8

VMEM = pl.BlockSpec(memory_space=pltpu.VMEM)
SMEM = pl.BlockSpec(memory_space=pltpu.SMEM)
HBM = pl.BlockSpec(memory_space=pl.ANY)
KINDS = {"v": VMEM, "s": SMEM, "h": HBM}


def launch(body, kinds, inputs, outs, scratch=()):
    return pl.pallas_call(
        body,
        out_shape=[jax.ShapeDtypeStruct(shape, dtype) for shape, dtype in outs],
        in_specs=[KINDS[kind] for kind in kinds],
        out_specs=[VMEM] * len(outs),
        scratch_shapes=list(scratch),
        name=body.__name__,
    )(*inputs)


def bits_of(count):
    return count.bit_length() - 1


def swap(value, axis, step):
    size = lax.axis_size(axis)
    return lax.ppermute(value, axis, [(i, i ^ step) for i in range(size)])


def along_ctx(value, step, cross):
    count = lax.axis_size("ctx")
    if not cross:
        pairs = [(i, i + step) for i in range(count) if 0 <= i + step < count]
        return lax.ppermute(value, "ctx", pairs)
    pairs = []
    for i in range(count):
        if 0 <= i + step < count:
            for core in range(2):
                pairs.append((2 * i + core, 2 * (i + step) + 1 - core))
    return lax.ppermute(value, ("ctx", "tp"), pairs)


def gather_pieces(matrix, cut):
    half = matrix.shape[cut] // 2
    across_x = swap(matrix, "shard", 1)
    across_y = swap(matrix, "shard", 2)
    first = swap(lax.slice_in_dim(across_x, 0, half, axis=cut), "shard", 2)
    second = swap(lax.slice_in_dim(across_y, half, 2 * half, axis=cut), "shard", 1)
    return [matrix, across_x, across_y, first, second]


def place_rows(idx, pieces, whole, sems):
    base = idx[0]
    rows, cols = pieces[0].shape
    half = cols // 2

    def spot(step):
        return pl.ds(pl.multiple_of((base ^ step) * rows, rows), rows)

    targets = [
        whole.at[spot(0), :],
        whole.at[spot(1), :],
        whole.at[spot(2), :],
        whole.at[spot(3), pl.ds(0, half)],
        whole.at[spot(3), pl.ds(half, half)],
    ]
    return [
        pltpu.make_async_copy(piece, target, sems.at[i])
        for i, (piece, target) in enumerate(zip(pieces, targets))
    ]


def place_blocks(idx, pieces, whole, sems):
    base = idx[0]
    half = pieces[0].shape[0] // 2
    targets = [
        whole.at[base],
        whole.at[base ^ 1],
        whole.at[base ^ 2],
        whole.at[base ^ 3, pl.ds(0, half), :],
        whole.at[base ^ 3, pl.ds(half, half), :],
    ]
    return [
        pltpu.make_async_copy(piece, target, sems.at[i])
        for i, (piece, target) in enumerate(zip(pieces, targets))
    ]


def begin(copies):
    for copy in copies:
        copy.start()


def finish(copies):
    for copy in copies:
        copy.wait()


def dot(left, right):
    return jnp.dot(left, right, preferred_element_type=F32)


def dot_t(left, right):
    return lax.dot_general(left, right, (((1,), (1,)), ((), ())), preferred_element_type=F32)


def norm(values):
    center = jnp.sum(values, axis=-1, keepdims=True) * (1.0 / WIDTH)
    squares = jnp.sum(values * values, axis=-1, keepdims=True) * (1.0 / WIDTH)
    root = lax.rsqrt(squares - center * center + epsilon)
    return (values - center) * root, root


def both(own, other, i):
    return jnp.concatenate([own[i : i + 1, :], other[i : i + 1, :]], axis=1)


def shift_down(values, first):
    row = lax.broadcasted_iota(jnp.int32, values.shape, 0)
    return jnp.where(row == 0, first, pltpu.roll(values, 1, 0))


def shift_up(values, last):
    count = values.shape[0]
    row = lax.broadcasted_iota(jnp.int32, values.shape, 0)
    return jnp.where(row == count - 1, last, pltpu.roll(values, count - 1, 0))


def combine(earlier, later, later_span):
    shifted = earlier[2] - later_span
    high = jnp.maximum(shifted, later[2])
    early = jnp.exp(shifted - high)
    late = jnp.exp(later[2] - high)
    return (earlier[0] * early + later[0] * late, earlier[1] * early + later[1] * late, high)


def get(ref, rows):
    return jnp.concatenate([ref[g, rows, :] for g in range(ref.shape[0])], axis=1)


def put(ref, rows, values):
    for g in range(ref.shape[0]):
        ref[g, rows, :] = values[:, g * 128 : (g + 1) * 128]


def swapped(values):
    half = values.shape[1] // 2
    return jnp.concatenate([values[:, half:], values[:, :half]], axis=1)


def per_device(
    block_entries,
    row_extents,
    upstream_loss_deriv,
    earlier_layernorm_scaling,
    earlier_layernorm_offset,
    temporal_mix_lookup_fraction,
    temporal_mix_payload_fraction,
    temporal_mix_filter_fraction,
    logarithmic_fading_per_feature,
    present_entry_reward,
    filter_projection,
    lookup_projection,
    payload_projection,
    temporal_mix_emit_projection,
    later_layernorm_scaling,
    later_layernorm_offset,
    feature_mix_lookup_fraction,
    feature_mix_filter_fraction,
    feature_mix_lookup_proj,
    feature_mix_filter_proj,
    feature_mix_payload_proj,
):
    batches, rows_local, L, H = block_entries.shape
    R = batches * rows_local
    T = R * L
    S, C = lax.axis_size("shard"), lax.axis_size("ctx")
    FH = feature_mix_lookup_proj.shape[1]
    ST = L // CHUNKS
    TB = min(32, L)
    NT = L // TB
    G = H // 128
    EVERY = slice(None)
    BLOCKS = S * C
    BR = WIDTH // BLOCKS
    SR = WIDTH // S
    assert S == 4 and WIDTH == 2 * H
    s_at, c_at, t_at = lax.axis_index("shard"), lax.axis_index("ctx"), lax.axis_index("tp")
    idx = jnp.concatenate(
        [
            jnp.stack(
                [s_at ^ (2 * t_at), c_at, (s_at * C + c_at) ^ (t_at * (BLOCKS // 2))]
            ).astype(jnp.int32),
            row_extents.reshape(R).astype(jnp.int32),
        ]
    )

    def rows_at(r, i):
        return pl.ds(pl.multiple_of(r * L + i * TB, TB), TB)

    def scan_rows(r, t):
        return pl.ds(pl.multiple_of((r * ST + t) * CHUNKS, CHUNKS), CHUNKS)

    def step_rows(r, t):
        return pl.ds(r * L + t, CHUNKS, stride=ST)

    def chunk_rows(part, i):
        return pl.ds(part * R * CHUNKS + i, R, stride=CHUNKS)

    x_own = block_entries.reshape(T, H)
    up_own = upstream_loss_deriv.reshape(T, H)
    params = jnp.stack(
        [
            earlier_layernorm_scaling,
            earlier_layernorm_offset,
            temporal_mix_lookup_fraction,
            temporal_mix_payload_fraction,
            temporal_mix_filter_fraction,
            later_layernorm_scaling,
            later_layernorm_offset,
            feature_mix_lookup_fraction,
            feature_mix_filter_fraction,
        ]
    )
    fading = logarithmic_fading_per_feature.reshape(1, H)
    bonus = present_entry_reward.reshape(1, H)
    time_pieces = gather_pieces(
        jnp.concatenate([lookup_projection, payload_projection, filter_projection], axis=1), 1
    )
    x_other = swap(x_own, "tp", 1)
    params_other = swap(params, "tp", 1)
    edge_out = block_entries[:, :, L - 1, :].reshape(R, H)
    edge_own = along_ctx(edge_out, 1, False)
    edge_other = along_ctx(edge_out, 1, True)
    emit_pieces = gather_pieces(temporal_mix_emit_projection, 0)
    hidden_pieces = gather_pieces(
        jnp.concatenate([feature_mix_lookup_proj, feature_mix_filter_proj], axis=1), 1
    )
    return_pieces = gather_pieces(feature_mix_payload_proj, 0)
    up_other = swap(up_own, "tp", 1)

    def mix_time(
        idx, xo, xp, eo, ep, po, pp, mixed_key, mixed_value, mixed_gate, hat, diff, root, hat_edge
    ):
        gain, bias = both(po, pp, 0), both(po, pp, 1)
        shares = [both(po, pp, i) for i in (2, 3, 4)]
        flag = jnp.where(idx[1] > 0, 1.0, 0.0).astype(F32)
        edge_hat, _ = norm(jnp.concatenate([eo[...], ep[...]], axis=1).astype(F32))
        hat_edge[...] = edge_hat * flag
        first = (edge_hat * gain + bias) * flag
        for r in range(R):

            def tile(i, last):
                at = rows_at(r, i)
                values = jnp.concatenate([xo[at, :], xp[at, :]], axis=1).astype(F32)
                n, q = norm(values)
                normed = n * gain + bias
                prev = shift_down(normed, last)
                hat[at, :] = n
                root[at, :] = q
                diff[at, :] = normed - prev
                for share, target in zip(shares, (mixed_key, mixed_value, mixed_gate)):
                    target[at, :] = (normed * share + prev * (1.0 - share)).astype(BF16)
                return normed[TB - 1 : TB, :]

            lax.fori_loop(0, NT, tile, first[r : r + 1, :])

    mixed_key, mixed_value, mixed_gate, hat_one, diff_one, root_one, hat_edge_one = launch(
        mix_time,
        "svvvvvv",
        (idx, x_own, x_other, edge_own, edge_other, params, params_other),
        [((T, WIDTH), BF16)] * 3
        + [((T, WIDTH), F32), ((T, WIDTH), F32), ((T, 1), F32), ((R, WIDTH), F32)],
    )

    def project_time(
        idx, mk, mv, mg, ld, p0, p1, p2, p3, p4, key, value, opened, states, closing, w, sems
    ):
        copies = place_rows(idx, [p0, p1, p2, p3, p4], w, sems)
        begin(copies)
        finish(copies)
        put(key, EVERY, dot(mk[...], w[:, :H]))
        put(value, EVERY, dot(mv[...], w[:, H : 2 * H]))
        rate = jnp.exp(ld[...])

        def step(t, carry):
            new = []
            for r in range(R):
                num, den, high = carry[r]
                k_now, v_now = get(key, step_rows(r, t)), get(value, step_rows(r, t))
                faded = high - rate
                top = jnp.maximum(faded, k_now)
                old, fresh = jnp.exp(faded - top), jnp.exp(k_now - top)
                new.append((old * num + fresh * v_now, old * den + fresh, top))
            return tuple(new)

        zero = jnp.zeros((CHUNKS, H), F32)
        ends = lax.fori_loop(0, ST, step, ((zero, zero, zero + lowest),) * R)
        for r in range(R):
            for part in range(3):
                put(states, pl.ds((part * R + r) * CHUNKS, CHUNKS), ends[r][part])
        total = tuple(get(states, chunk_rows(part, 0)) for part in range(3))
        for i in range(1, CHUNKS):
            total = combine(
                total, tuple(get(states, chunk_rows(part, i)) for part in range(3)), ST * rate
            )
        for part in range(3):
            closing[pl.ds(part * R, R), :] = total[part]
        opened[...] = jax.nn.sigmoid(dot(mg[...], w[:, 2 * H : 3 * H]))

    key, value, opened, states, closing = launch(
        project_time,
        "svvvv" + "h" * 5,
        (idx, mixed_key, mixed_value, mixed_gate, fading, *time_pieces),
        [((G, T, 128), F32)] * 2
        + [((T, H), F32), ((G, 3 * R * CHUNKS, 128), F32), ((3 * R, H), F32)],
        [pltpu.VMEM((WIDTH, 3 * H), BF16), pltpu.SemaphoreType.DMA((5,))],
    )

    rate = jnp.exp(fading)
    total = tuple(closing.reshape(3, R, H))
    prefix = (jnp.zeros((R, H), F32), jnp.zeros((R, H), F32), jnp.full((R, H), lowest, F32))
    for bit in range(bits_of(C)):
        other = tuple(swap(jnp.stack(total), "ctx", 1 << bit))
        up = (c_at >> bit) & 1 == 1
        span = rate * (L << bit)
        so_far = rate * (L * (c_at & ((1 << bit) - 1))).astype(F32)
        with_other = combine(other, prefix, so_far)
        prefix = tuple(jnp.where(up, a, b) for a, b in zip(with_other, prefix))
        if bit + 1 < bits_of(C):
            as_later, as_earlier = combine(other, total, span), combine(total, other, span)
            total = tuple(jnp.where(up, a, b) for a, b in zip(as_later, as_earlier))
    entering = jnp.concatenate(prefix, axis=0)

    def sweep_time(
        key, value, opened, ld, un, states, enter,
        gated, out, part_old, part_new, keep, fresh, nums, dens, fade, starts,
    ):
        rate = jnp.exp(ld[...])
        reward = un[...]
        state = tuple(enter[pl.ds(part * R, R), :] for part in range(3))
        for i in range(CHUNKS):
            for part in range(3):
                put(starts, chunk_rows(part, i), state[part])
            state = combine(
                state, tuple(get(states, chunk_rows(part, i)) for part in range(3)), ST * rate
            )

        def step(t, carry):
            new = []
            for r in range(R):
                num, den, high = carry[r]
                k_now, v_now = get(key, step_rows(r, t)), get(value, step_rows(r, t))
                at = scan_rows(r, t)
                now = reward + k_now
                top = jnp.maximum(high, now)
                e_old, e_new = jnp.exp(high - top), jnp.exp(now - top)
                inverse = 1.0 / (e_old * den + e_new)
                e_old, e_new = e_old * inverse, e_new * inverse
                put(out, step_rows(r, t), e_old * num + e_new * v_now)
                part_old[at, :] = e_old
                part_new[at, :] = e_new
                nums[at, :] = num
                dens[at, :] = den
                faded = high - rate
                peak = jnp.maximum(faded, k_now)
                a, b = jnp.exp(faded - peak), jnp.exp(k_now - peak)
                keep[at, :] = a
                fresh[at, :] = b
                new.append((a * num + b * v_now, a * den + b, peak))
            return tuple(new)

        begin_at = tuple(
            tuple(get(starts, pl.ds((part * R + r) * CHUNKS, CHUNKS)) for part in range(3))
            for r in range(R)
        )
        ends = lax.fori_loop(0, ST, step, begin_at)
        for r in range(R):
            put(
                fade,
                pl.ds(r * CHUNKS, CHUNKS),
                jnp.exp(begin_at[r][2] - ST * rate - ends[r][2]),
            )
        gated[...] = (opened[...] * get(out, EVERY)).astype(BF16)

    gated, mixed_out, part_old, part_new, keep, fresh, nums, dens, fade = launch(
        sweep_time,
        "v" * 7,
        (key, value, opened, fading, bonus, states, entering),
        [((T, H), BF16), ((G, T, 128), F32)]
        + [((T, H), F32)] * 6
        + [((G, R * CHUNKS, 128), F32)],
        [pltpu.VMEM((G, 3 * R * CHUNKS, 128), F32)],
    )

    def emit(idx, gated, p0, p1, p2, p3, p4, part, w, sems):
        copies = place_blocks(idx, [p0, p1, p2, p3, p4], w, sems)
        begin(copies)
        finish(copies)
        for p in range(S):
            part[:, p * SR : (p + 1) * SR] = dot(gated[...], w[p])

    (emitted,) = launch(
        emit,
        "sv" + "h" * 5,
        (idx, gated, *emit_pieces),
        [((T, WIDTH), F32)],
        [pltpu.VMEM((S, H, SR), BF16), pltpu.SemaphoreType.DMA((5,))],
    )
    emitted_other = swap(emitted, "tp", 1)

    def middle_norm(xo, xp, mine, theirs, middle, hat, root, last):
        for r in range(R):

            def tile(i, carry):
                at = rows_at(r, i)
                values = jnp.concatenate([xo[at, :], xp[at, :]], axis=1).astype(F32)
                values = values + (mine[at, :] + swapped(theirs[at, :]))
                n, q = norm(values)
                middle[at, :] = values[:, :H]
                hat[at, :] = n
                root[at, :] = q
                return n[TB - 1 : TB, :]

            last[r : r + 1, :] = lax.fori_loop(0, NT, tile, jnp.zeros((1, WIDTH), F32))

    middle, hat_two, root_two, hat_last = launch(
        middle_norm,
        "vvvv",
        (x_own, x_other, emitted, emitted_other),
        [((T, H), F32), ((T, WIDTH), F32), ((T, 1), F32), ((R, WIDTH), F32)],
    )
    hat_edge_two = along_ctx(hat_last, 1, False)

    NF = FH + H
    NB = min(512, FH)

    def channel_forward(
        idx, hat, edge, po, pp, h0, h1, h2, h3, h4, r0, r1, r2, r3, r4,
        ckey, cgate, diff, active, squared, keep_own, send_other, opened, wh, wr, sems_h, sems_r,
    ):
        copies_h = place_rows(idx, [h0, h1, h2, h3, h4], wh, sems_h)
        copies_r = place_blocks(idx, [r0, r1, r2, r3, r4], wr, sems_r)
        begin(copies_h)
        begin(copies_r)
        gain, bias = both(po, pp, 5), both(po, pp, 6)
        shares = [both(po, pp, i) for i in (7, 8)]
        flag = jnp.where(idx[1] > 0, 1.0, 0.0).astype(F32)
        first = (edge[...] * gain + bias) * flag
        for r in range(R):

            def tile(i, last):
                at = rows_at(r, i)
                normed = hat[at, :] * gain + bias
                prev = shift_down(normed, last)
                diff[at, :] = normed - prev
                for share, target in zip(shares, (ckey, cgate)):
                    target[at, :] = (normed * share + prev * (1.0 - share)).astype(BF16)
                return normed[TB - 1 : TB, :]

            lax.fori_loop(0, NT, tile, first[r : r + 1, :])
        finish(copies_h)
        for n in range(0, FH, NB):
            pre = jnp.maximum(dot(ckey[...], wh[:, n : n + NB]), 0.0)
            active[:, n : n + NB] = pre.astype(BF16)
            squared[:, n : n + NB] = (pre * pre).astype(BF16)
        opened[...] = jax.nn.sigmoid(dot(cgate[...], wh[:, FH:NF]))
        finish(copies_r)
        for p in range(S):
            target = keep_own if p < S // 2 else send_other
            at = (p % (S // 2)) * SR
            target[:, at : at + SR] = dot(squared[...], wr[p])

    channel_key, channel_gate, diff_two, active, squared, ret_keep, ret_send, filter_open = launch(
        channel_forward,
        "svvvv" + "h" * 10,
        (idx, hat_two, hat_edge_two, params, params_other, *hidden_pieces, *return_pieces),
        [
            ((T, WIDTH), BF16),
            ((T, WIDTH), BF16),
            ((T, WIDTH), F32),
            ((T, FH), BF16),
            ((T, FH), BF16),
            ((T, H), F32),
            ((T, H), F32),
            ((T, H), F32),
        ],
        [
            pltpu.VMEM((WIDTH, NF), BF16),
            pltpu.VMEM((S, FH, SR), BF16),
            pltpu.SemaphoreType.DMA((5,)),
            pltpu.SemaphoreType.DMA((5,)),
        ],
    )
    ret_other = swap(ret_send, "tp", 1)

    def live_rows(idx, r, i):
        at = lax.broadcasted_iota(jnp.int32, (TB, 1), 0) + (idx[1] * L + i * TB)
        return jnp.where(at < idx[3 + r], 1.0, 0.0).astype(F32)

    def close_block(idx, mine, theirs, opened, middle, up, out, grad_ret, grad_fil):
        for r in range(R):

            def tile(i, carry):
                at = rows_at(r, i)
                live = live_rows(idx, r, i)
                returned = mine[at, :] + theirs[at, :]
                s = opened[at, :]
                out[at, :] = (live * (middle[at, :] + s * returned)).astype(BF16)
                grad = live * up[at, :].astype(F32)
                grad_ret[at, :] = (grad * s).astype(BF16)
                grad_fil[at, :] = (grad * returned * s * (1.0 - s)).astype(BF16)
                return carry

            lax.fori_loop(0, NT, tile, 0)

    block_out, grad_returned, grad_filter = launch(
        close_block,
        "svvvvv",
        (idx, ret_keep, ret_other, filter_open, middle, up_own),
        [((T, H), BF16)] * 3,
    )
    grad_returned_other = swap(grad_returned, "tp", 1)

    def channel_backward(
        idx, gro, grp, gf, active, diff, hat, edge, po, pp,
        h0, h1, h2, h3, h4, r0, r1, r2, r3, r4,
        grad_hidden, grad_normed, first_out, sums, wh, wr, ckey, cgate, sems_h, sems_r,
    ):
        copies_h = place_rows(idx, [h0, h1, h2, h3, h4], wh, sems_h)
        copies_r = place_blocks(idx, [r0, r1, r2, r3, r4], wr, sems_r)
        begin(copies_r)
        begin(copies_h)
        finish(copies_r)
        half = S // 2
        for n in range(0, FH, NB):
            acc = None
            for p in range(S):
                source = gro if p < half else grp
                at = (p % half) * SR
                term = dot_t(source[:, at : at + SR], wr[p, n : n + NB, :])
                acc = term if acc is None else acc + term
            grad_hidden[:, n : n + NB] = (
                acc * 2.0 * active[:, n : n + NB].astype(F32)
            ).astype(BF16)
        finish(copies_h)
        for p in range(S):
            at = slice(p * SR, (p + 1) * SR)
            ckey[:, at] = dot_t(grad_hidden[...], wh[at, :FH])
            cgate[:, at] = dot_t(gf[...], wh[at, FH:NF])
        share_k, share_g = both(po, pp, 7), both(po, pp, 8)
        flag = jnp.where(idx[1] > 0, 1.0, 0.0).astype(F32)
        zero = jnp.zeros((1, WIDTH), F32)
        totals = (zero, zero, zero, zero)
        for r in range(R):

            def tile(j, carry):
                after, gain_sum, bias_sum, key_sum, gate_sum = carry
                at = rows_at(r, NT - 1 - j)
                gk, gg, d = ckey[at, :], cgate[at, :], diff[at, :]
                now = gk * share_k + gg * share_g
                back = gk * (1.0 - share_k) + gg * (1.0 - share_g)
                grad = now + shift_up(back, after)
                grad_normed[at, :] = grad
                return (
                    back[0:1, :],
                    gain_sum + jnp.sum(grad * hat[at, :], axis=0, keepdims=True),
                    bias_sum + jnp.sum(grad, axis=0, keepdims=True),
                    key_sum + jnp.sum(gk * d, axis=0, keepdims=True),
                    gate_sum + jnp.sum(gg * d, axis=0, keepdims=True),
                )

            front, *totals = lax.fori_loop(0, NT, tile, (zero, *totals))
            first_out[r : r + 1, :] = front
            totals[0] = totals[0] + front * (edge[r : r + 1, :] * flag)
            totals[1] = totals[1] + front * flag
        for i in range(4):
            sums[i : i + 1, :] = totals[i]

    grad_hidden, grad_two, first_two, sums_two = launch(
        channel_backward,
        "s" + "v" * 9 + "h" * 10,
        (
            idx,
            grad_returned,
            grad_returned_other,
            grad_filter,
            active,
            diff_two,
            hat_two,
            hat_edge_two,
            params,
            params_other,
            *hidden_pieces,
            *return_pieces,
        ),
        [((T, FH), BF16), ((T, WIDTH), F32), ((R, WIDTH), F32), ((4, WIDTH), F32)],
        [
            pltpu.VMEM((WIDTH, NF), BF16),
            pltpu.VMEM((S, FH, SR), BF16),
            pltpu.VMEM((T, WIDTH), F32),
            pltpu.VMEM((T, WIDTH), F32),
            pltpu.SemaphoreType.DMA((5,)),
            pltpu.SemaphoreType.DMA((5,)),
        ],
    )
    grad_two_other = swap(grad_two, "tp", 1)
    first_two_own = along_ctx(first_two, -1, False)
    first_two_other = along_ctx(first_two, -1, True)

    order = []
    for spot in range(BLOCKS):
        high, low = spot // C, spot % C
        turned = 0
        for bit in range(bits_of(C)):
            turned = turned * 2 + ((low >> bit) & 1)
        order.append(high * C + turned)

    def weight_grads(lefts, rights, jobs):
        count_left = [len(group) for group in lefts]
        flat = [ref for group in lefts for ref in group]
        width = sum(job[3] for job in jobs if job[4] == 0)

        def weight_products(idx, *refs):
            left_refs = list(refs[: len(flat)])
            right_refs = refs[len(flat) : len(flat) + len(rights)]
            send_a, keep_a, send_b, keep_b, tall, turned = refs[len(flat) + len(rights) :]
            groups = []
            for count in count_left:
                groups.append(left_refs[:count])
                left_refs = left_refs[count:]
            half, quarter = WIDTH // 2, WIDTH // 4
            for g, group in enumerate(groups):
                row = 0
                for ref in group:
                    for lane in range(0, ref.shape[1], 128):
                        tall[row : row + 128, :] = ref[:, lane : lane + 128].astype(F32).T
                        row += 128
                for spot in range(BLOCKS):
                    block = order[spot] ^ idx[2]
                    turned[spot * BR : (spot + 1) * BR, :] = tall[
                        pl.ds(pl.multiple_of(block * BR, BR), BR), :
                    ].astype(BF16)
                for left, right, start, size, part, at in jobs:
                    if left != g:
                        continue
                    for n in range(0, size, 256):
                        to = slice(at + n, at + n + 256)
                        acc = dot(
                            turned[...], right_refs[right][:, start + n : start + n + 256]
                        ).astype(BF16)
                        if part == 0:
                            keep_a[:quarter, to] = acc[:quarter]
                            send_a[:quarter, to] = acc[quarter:half]
                            keep_a[quarter:, to] = acc[half : half + quarter]
                            send_a[quarter:, to] = acc[half + quarter :]
                        else:
                            keep_b[:, to] = acc[:half]
                            send_b[:, to] = acc[half:]

        return launch(
            weight_products,
            "s" + "v" * (len(flat) + len(rights)),
            (idx, *flat, *rights),
            [((WIDTH // 2, width), BF16)] * 4,
            [pltpu.VMEM((WIDTH, T), F32), pltpu.VMEM((WIDTH, T), BF16)],
        )

    def add(mine, theirs):
        return mine.astype(F32) + theirs.astype(F32)

    def halves(values):
        half = values.shape[0] // 2
        return values[:half], values[half:]

    def scatter(send_a, keep_a, send_b, keep_b):
        got_a, got_b = swap(send_a, "shard", 1), swap(send_b, "shard", 2)
        keep_a, send_a = halves(add(keep_a, got_a).astype(BF16))
        keep_b, send_b = halves(add(keep_b, got_b).astype(BF16))
        got_a, got_b = swap(send_a, "shard", 2), swap(send_b, "shard", 1)
        joined = jnp.concatenate([add(keep_a, got_a), add(keep_b, got_b)], axis=1)
        for bit in range(bits_of(C)):
            mine, theirs = halves(joined.astype(BF16))
            joined = add(mine, swap(theirs, "ctx", 1 << bit))
        return joined

    return_w = scatter(
        *weight_grads(
            [[grad_returned, grad_returned_other]],
            [squared],
            [(0, 0, 0, FH // 2, 0, 0), (0, 0, FH // 2, FH // 2, 1, 0)],
        )
    )
    part = NF // 2
    hidden_w = scatter(
        *weight_grads(
            [[channel_key], [channel_gate]],
            [grad_hidden, grad_filter],
            [
                (0, 0, 0, part, 0, 0),
                (0, 0, part, FH - part, 1, 0),
                (1, 1, 0, H, 1, FH - part),
            ],
        )
    )

    def middle_backward(
        idx, mine, theirs, e_own, e_other, hat, root, po, pp, uo, upp, opened, out,
        part_old, keep, fade, p0, p1, p2, p3, p4,
        grad_mid, grad_own, grad_res, grad_gate, adjoint, entry, w, gates, sems,
    ):
        copies = place_blocks(idx, [p0, p1, p2, p3, p4], w, sems)
        begin(copies)
        gain = both(po, pp, 5)
        tail = e_own[...] + swapped(e_other[...])
        row = lax.broadcasted_iota(jnp.int32, (TB, 1), 0)
        for r in range(R):

            def tile(i, carry):
                at = rows_at(r, i)
                is_last = jnp.where((row == TB - 1) & (i == NT - 1), 1.0, 0.0).astype(F32)
                grad = mine[at, :] + swapped(theirs[at, :]) + is_last * tail[r : r + 1, :]
                n = hat[at, :]
                scaled = grad * gain
                mean_one = jnp.sum(scaled, axis=-1, keepdims=True) * (1.0 / WIDTH)
                mean_two = jnp.sum(scaled * n, axis=-1, keepdims=True) * (1.0 / WIDTH)
                up = jnp.concatenate([uo[at, :], upp[at, :]], axis=1).astype(F32)
                full = live_rows(idx, r, i) * up + root[at, :] * (scaled - mean_one - n * mean_two)
                grad_mid[at, :] = full.astype(BF16)
                grad_own[at, :] = full[:, :H]
                return carry

            lax.fori_loop(0, NT, tile, 0)
        finish(copies)
        acc = None
        for p in range(S):
            term = dot_t(grad_mid[:, p * SR : (p + 1) * SR], w[p])
            acc = term if acc is None else acc + term
        gates[...] = acc
        for r in range(R):

            def gate_tile(i, carry):
                at = rows_at(r, i)
                g, s = gates[at, :], opened[at, :]
                put(grad_res, at, g * s)
                grad_gate[at, :] = (g * get(out, at) * s * (1.0 - s)).astype(BF16)
                return carry

            lax.fori_loop(0, NT, gate_tile, 0)

        def step(j, carry):
            t = ST - 1 - j
            new = []
            for r in range(R):
                alpha, beta = carry[r]
                at = scan_rows(r, t)
                direct = part_old[at, :] * get(grad_res, step_rows(r, t))
                a = keep[at, :]
                new.append(
                    (direct + a * alpha, a * beta - direct * get(out, step_rows(r, t)))
                )
            return tuple(new)

        zero = jnp.zeros((CHUNKS, H), F32)
        ends = lax.fori_loop(0, ST, step, ((zero, zero),) * R)
        for r in range(R):
            for k in range(2):
                put(adjoint, pl.ds((k * R + r) * CHUNKS, CHUNKS), ends[r][k])
        alpha = beta = jnp.zeros((R, H), F32)
        span = jnp.ones((R, H), F32)
        for i in range(CHUNKS - 1, -1, -1):
            f = get(fade, chunk_rows(0, i))
            alpha = get(adjoint, chunk_rows(0, i)) + f * alpha
            beta = get(adjoint, chunk_rows(1, i)) + f * beta
            span = span * f
        entry[pl.ds(0, R), :] = alpha
        entry[pl.ds(R, R), :] = beta
        entry[pl.ds(2 * R, R), :] = span

    grad_mid, grad_mid_own, grad_res, grad_gate, adjoint, entry = launch(
        middle_backward,
        "s" + "v" * 15 + "h" * 5,
        (
            idx,
            grad_two,
            grad_two_other,
            first_two_own,
            first_two_other,
            hat_two,
            root_two,
            params,
            params_other,
            up_own,
            up_other,
            opened,
            mixed_out,
            part_old,
            keep,
            fade,
            *emit_pieces,
        ),
        [
            ((T, WIDTH), BF16),
            ((T, H), F32),
            ((G, T, 128), F32),
            ((T, H), BF16),
            ((G, 2 * R * CHUNKS, 128), F32),
            ((3 * R, H), F32),
        ],
        [
            pltpu.VMEM((S, H, SR), BF16),
            pltpu.VMEM((T, H), F32),
            pltpu.SemaphoreType.DMA((5,)),
        ],
    )

    alpha, beta, span = entry.reshape(3, R, H)
    late_alpha = late_beta = jnp.zeros((R, H), F32)
    late_span = jnp.ones((R, H), F32)
    for bit in range(bits_of(C)):
        alpha_o, beta_o, span_o = swap(jnp.stack([alpha, beta, span]), "ctx", 1 << bit)
        low = (c_at >> bit) & 1 == 0
        late_alpha, late_beta, late_span = (
            jnp.where(low, late_alpha + late_span * alpha_o, late_alpha),
            jnp.where(low, late_beta + late_span * beta_o, late_beta),
            jnp.where(low, late_span * span_o, late_span),
        )
        if bit + 1 < bits_of(C):
            alpha, beta, span = (
                jnp.where(low, alpha + span * alpha_o, alpha_o + span_o * alpha),
                jnp.where(low, beta + span * beta_o, beta_o + span_o * beta),
                span * span_o,
            )
    late = jnp.concatenate([late_alpha, late_beta], axis=0)

    early_w = scatter(
        *weight_grads(
            [[grad_mid], [mixed_gate]],
            [gated, grad_gate],
            [(0, 0, 0, H, 0, 0), (1, 1, 0, H, 1, 0)],
        )
    )

    def time_backward(
        idx, res, out, value, part_old, part_new, keep, fresh, nums, dens, fade, adjoint, late,
        ld, gate, diff, hat, edge, po, pp, p0, p1, p2, p3, p4,
        grad_key, grad_value, mine_own, send, first_out, sums, sums_own,
        w, dk, dv, gk, gv, gg, starts, sems,
    ):
        copies = place_rows(idx, [p0, p1, p2, p3, p4], w, sems)
        begin(copies)
        late_now = (late[pl.ds(0, R), :], late[pl.ds(R, R), :])
        for i in range(CHUNKS - 1, -1, -1):
            for k in range(2):
                put(starts, chunk_rows(k, i), late_now[k])
            f = get(fade, chunk_rows(0, i))
            late_now = tuple(get(adjoint, chunk_rows(k, i)) + f * late_now[k] for k in range(2))

        def step(j, carry):
            t = ST - 1 - j
            adj, fade_sum, bonus_sum = carry
            new = []
            for r in range(R):
                alpha, beta = adj[r]
                at, spread = scan_rows(r, t), step_rows(r, t)
                g, y, v = get(res, spread), get(out, spread), get(value, spread)
                b, a = fresh[at, :], keep[at, :]
                near = part_new[at, :] * g
                lift = near * (v - y)
                put(dv, spread, b * alpha + near)
                put(dk, spread, b * (v * alpha + beta) + lift)
                bonus_sum = bonus_sum + lift
                fade_sum = fade_sum - a * (nums[at, :] * alpha + dens[at, :] * beta)
                direct = part_old[at, :] * g
                new.append((direct + a * alpha, a * beta - direct * y))
            return (tuple(new), fade_sum, bonus_sum)

        first_adj = tuple(
            tuple(get(starts, pl.ds((k * R + r) * CHUNKS, CHUNKS)) for k in range(2))
            for r in range(R)
        )
        zero = jnp.zeros((CHUNKS, H), F32)
        _, fade_sum, bonus_sum = lax.fori_loop(0, ST, step, (first_adj, zero, zero))
        sums_own[0:1, :] = jnp.sum(fade_sum, axis=0, keepdims=True) * jnp.exp(ld[...])
        sums_own[1:2, :] = jnp.sum(bonus_sum, axis=0, keepdims=True)
        grad_key[...] = get(dk, EVERY).astype(BF16)
        grad_value[...] = get(dv, EVERY).astype(BF16)
        finish(copies)
        gk[...] = dot_t(grad_key[...], w[:, :H])
        gv[...] = dot_t(grad_value[...], w[:, H : 2 * H])
        gg[...] = dot_t(gate[...], w[:, 2 * H : 3 * H])
        gain = both(po, pp, 0)
        shares = [both(po, pp, i) for i in (2, 3, 4)]
        flag = jnp.where(idx[1] > 0, 1.0, 0.0).astype(F32)
        zero = jnp.zeros((1, WIDTH), F32)
        totals = (zero,) * 5
        lane = lax.broadcasted_iota(jnp.int32, (TB, 128), 1)
        for r in range(R):

            def tile(j, carry):
                after, gain_sum, bias_sum, *mix_sums = carry
                at = rows_at(r, NT - 1 - j)
                grads = (gk[at, :], gv[at, :], gg[at, :])
                d, n = diff[at, :], hat[at, :]
                now = back = None
                for share, grad in zip(shares, grads):
                    a, b = grad * share, grad * (1.0 - share)
                    now = a if now is None else now + a
                    back = b if back is None else back + b
                grad = now + shift_up(back, after)
                mine_own[at, :] = grad[:, :H]
                send[at, :H] = grad[:, H:]
                scaled = grad * gain
                one = jnp.sum(scaled, axis=-1, keepdims=True)
                two = jnp.sum(scaled * n, axis=-1, keepdims=True)
                send[at, H:] = jnp.where(lane == 0, one, jnp.where(lane == 1, two, 0.0))
                return (
                    back[0:1, :],
                    gain_sum + jnp.sum(grad * n, axis=0, keepdims=True),
                    bias_sum + jnp.sum(grad, axis=0, keepdims=True),
                    *(
                        total + jnp.sum(one_grad * d, axis=0, keepdims=True)
                        for total, one_grad in zip(mix_sums, grads)
                    ),
                )

            front, *totals = lax.fori_loop(0, NT, tile, (zero, *totals))
            first_out[r : r + 1, :] = front
            totals[0] = totals[0] + front * edge[r : r + 1, :]
            totals[1] = totals[1] + front * flag
        for i in range(5):
            sums[i : i + 1, :] = totals[i]

    grad_key, grad_value, one_own, one_send, first_one, sums_one, sums_own = launch(
        time_backward,
        "s" + "v" * 19 + "h" * 5,
        (
            idx,
            grad_res,
            mixed_out,
            value,
            part_old,
            part_new,
            keep,
            fresh,
            nums,
            dens,
            fade,
            adjoint,
            late,
            fading,
            grad_gate,
            diff_one,
            hat_one,
            hat_edge_one,
            params,
            params_other,
            *time_pieces,
        ),
        [
            ((T, H), BF16),
            ((T, H), BF16),
            ((T, H), F32),
            ((T, H + 128), F32),
            ((R, WIDTH), F32),
            ((5, WIDTH), F32),
            ((2, H), F32),
        ],
        [pltpu.VMEM((WIDTH, 3 * H), BF16)]
        + [pltpu.VMEM((G, T, 128), F32)] * 2
        + [pltpu.VMEM((T, WIDTH), F32)] * 3
        + [pltpu.VMEM((G, 2 * R * CHUNKS, 128), F32), pltpu.SemaphoreType.DMA((5,))],
    )
    one_other = swap(one_send, "tp", 1)
    first_one_own = along_ctx(first_one, -1, False)
    first_one_other = along_ctx(first_one, -1, True)

    late_w = scatter(
        *weight_grads(
            [[mixed_key], [mixed_value]],
            [grad_key, grad_value],
            [(0, 0, 0, H, 0, 0), (1, 1, 0, H, 1, 0)],
        )
    )

    wide = jnp.concatenate([sums_one, sums_two], axis=0)
    own = wide[:, :H] + swap(wide[:, H:], "tp", 1)
    vectors = jnp.concatenate([own, sums_own], axis=0)
    for bit in range(bits_of(S)):
        vectors = vectors + swap(vectors, "shard", 1 << bit)
    for bit in range(bits_of(C)):
        vectors = vectors + swap(vectors, "ctx", 1 << bit)

    def input_backward(mine, sent, theirs, e_own, e_other, hat, root, po, pp, gm, out):
        gain_full = both(po, pp, 0)
        tail = e_own[...] + swapped(e_other[...])
        row = lax.broadcasted_iota(jnp.int32, (TB, 1), 0)
        for r in range(R):
            weighted = tail[r : r + 1, :] * gain_full
            tail_one = jnp.sum(weighted, axis=-1, keepdims=True)
            tail_two = jnp.sum(
                weighted * hat[(r + 1) * L - 1 : (r + 1) * L, :], axis=-1, keepdims=True
            )

            def tile(i, carry):
                at = rows_at(r, i)
                is_last = jnp.where((row == TB - 1) & (i == NT - 1), 1.0, 0.0).astype(F32)
                grad = mine[at, :] + theirs[at, :H] + is_last * tail[r : r + 1, :H]
                stats = sent[at, H:] + theirs[at, H:]
                mean_one = (stats[:, 0:1] + is_last * tail_one) * (1.0 / WIDTH)
                mean_two = (stats[:, 1:2] + is_last * tail_two) * (1.0 / WIDTH)
                scaled = grad * gain_full[:, :H]
                out[at, :] = gm[at, :] + root[at, :] * (
                    scaled - mean_one - hat[at, :H] * mean_two
                )
                return carry

            lax.fori_loop(0, NT, tile, 0)

    (input_grad,) = launch(
        input_backward,
        "v" * 10,
        (
            one_own,
            one_send,
            one_other,
            first_one_own,
            first_one_other,
            hat_one,
            root_one,
            params,
            params_other,
            grad_mid_own,
        ),
        [((T, H), F32)],
    )

    shape = block_entries.shape
    return (
        block_out.reshape(shape),
        input_grad.reshape(shape),
        vectors[0],
        vectors[1],
        vectors[2],
        vectors[3],
        vectors[4],
        vectors[9],
        vectors[10],
        early_w[:, H:],
        late_w[:, :H],
        late_w[:, H:],
        early_w[:, :H].T,
        vectors[5],
        vectors[6],
        vectors[7],
        vectors[8],
        hidden_w[:, :FH],
        hidden_w[:, FH:],
        return_w.T,
    )


def solution(mesh):
    token = P(None, "shard", "ctx", "tp")
    feature = P("tp")
    rows = P("shard", "tp")
    cols = P("tp", "shard")
    rows_out = P(("shard", "ctx"), "tp")
    cols_out = P("tp", ("shard", "ctx"))
    return jax.shard_map(
        per_device,
        mesh=mesh,
        in_specs=(
            (token, P(None, "shard"), token)
            + (feature,) * 7
            + (rows, rows, rows, cols)
            + (feature,) * 4
            + (rows, rows, cols)
        ),
        out_specs=(
            (token, token)
            + (feature,) * 7
            + (rows_out, rows_out, rows_out, cols_out)
            + (feature,) * 4
            + (rows_out, rows_out, cols_out)
        ),
        check_vma=False,
    )
```

time: 2150 us -> 412 us (0.19); the launches traced: 2130 us -> 411 us
  waiting for transfers between devices: 879 us -> 155 us
  local copies, waits for them, and re-layouts: 565 us -> 24.2 us
  other arithmetic: 285 us -> 20.6 us
  blocking collectives: 259 us -> 0 us
  Pallas kernels: 0 us -> 125 us
  matrix products: 94.7 us -> 0 us
  starting transfers between devices: 22.3 us -> 85 us
    reduce_scatter x15 -> x0, waiting for transfers between devices: 690 us -> none  [the longest x1 183 us: per_device(): lax.psum_scatter(weight_grads[4], ('shard', 'ctx'), scatter_dimension=0,...]
    pad x273 -> x0, local copies, waits for them, and re-layouts: 283 us -> none  [stretch_states(): lax.associative_scan(combine_states, (payload_series, unit_weights, looku...]
    slice x243 -> x25, local copies, waits for them, and re-layouts: 220 us -> 10.2 us  [the longest x12 2.87 us: halves(): return (values[:half], values[half:])]
    all_gather x11 -> x0, waiting for transfers between devices: 178 us -> none  [the longest x1 55.6 us: per_device(): lax.all_gather(feature_mix_lookup_proj, 'shard', axis=0, tiled=True)]
    all_gather x17 -> x0, blocking collectives: 173 us -> none  [the longest x13 164 us: entering(): pieces = jax.tree.map(lambda part: lax.all_gather(part, axis), value)]
    ppermute x8 -> x64, waiting for transfers between devices: 5.71 us -> 155 us  [the longest x57 155 us: swap(): return lax.ppermute(value, axis, [(i, i ^ step) for i in range(size)])]
    pallas_call x0 -> x15, Pallas kernels: none -> 125 us  [launch(): pl.pallas_call(body, out_shape=[jax.ShapeDtypeStruct(shape, dtype) for sh...]
    dot_general x42 -> x0, matrix products: 94.7 us -> none  [dot_float(): return jnp.dot(left_side, right_side, preferred_element_type=jnp.float32)]
  transfers between devices with their start and end apart: 34 -> 64, of which waited for: 22 -> 23; matrix products, arithmetic and copies ran while one was open for 20% -> 8% of each run, Pallas kernels for 0% -> 23%
where the time goes in v1:
time: 412 us; the launch traced here: 411 us
  waiting for transfers between devices  155 us (38%)
  Pallas kernels  125 us (30%)
  starting transfers between devices  85 us (21%)
  local copies, waits for them, and re-layouts  24.2 us (6%)
  other arithmetic  20.6 us (5%)
    ppermute x57, waiting for transfers between devices, swap(): return lax.ppermute(value, axis, [(i, i ^ step) for i in range(size)])  155 us
    pallas_call x15, Pallas kernels, launch(): pl.pallas_call(body, out_shape=[jax.ShapeDtypeStruct(shape, dtype) for sh...  125 us
    ppermute x57, starting transfers between devices, swap(): return lax.ppermute(value, axis, [(i, i ^ step) for i in range(size)])  72.8 us
    unnamed x136, local copies, waits for them, and re-layouts  10.5 us
    ppermute x4, starting transfers between devices, along_ctx(): return lax.ppermute(value, 'ctx', pairs)  8.41 us
  transfers between devices with their start and end apart: 64, of which 23 were waited for; matrix products, arithmetic and copies ran while one was open for 8% of the time, Pallas kernels for 23%

profile of v1, /device:TPU:0, one launch (start us, length us, event | category | flops | bytes accessed | tf_op | source)
XLA Modules:
  0.0 411.3 jit_solution(4024151103344596498)
XLA Ops:
  3.8 3.0 collective-permute-start.4
  8.3 16.0 %collective-permute-done.4.p1 = bf16[256,1536]{1,0:T(8,128)(2,1)S(1)} collective-permute-done((bf16[256,1536]{1,0:T(8,128)(2,1)S(1)}, bf16[256,1536]{1,0:T(8,128)(2,1)S(1)}, u32[]{:S(2)}, u32[]{:S(2)}) %collective-permute-start.4) | collective-permute-done | bytes 786464 | tf_op jit(solution)/shard_map/ppermute | solution.py:37
  29.3 3.5 collective-permute-start.1
  39.1 7.5 %mix_time.1 = (bf16[512,1024]{1,0:T(8,128)(2,1)}, bf16[512,1024]{1,0:T(8,128)(2,1)}, bf16[512,1024]{1,0:T(8,128)(2,1)}, f32[512,1024]{1,0:T(8,128)}, f32[512,102...) custom-call(s32[5]{0:T(128)} %pad_add_fusion.idx, bf16[512,512]{1,0:T(8,128)(2,1)} %bitcast.161, ...), custom_call_target="tpu_custom_call" | custom-call | tf_op jit(solution)/shard_map/mix_time/pallas_call | solution.py:21
  46.7 9.0 %project_time.1 = (f32[4,512,128]{2,1,0:T(8,128)}, f32[4,512,128]{2,1,0:T(8,128)}, f32[512,512]{1,0:T(8,128)}, f32[4,48,128]{2,1,0:T(8,128)}, f32[6,512]{1,0:T(8,128)}) custom-call(s32[5]{0:T(128)} %pad_add_fusion.idx, bf16[512,1024]{1,0:T(8,128)(2,1)} %get-tuple-element.89.mk.refs_0_, bf16[512,1024]{1,0:T(8,128)(2,1)} %get-tuple-element.90.mv.refs_1_, ...), custom_call_target="tpu_custom_call" | custom-call | tf_op jit(solution)/shard_map/project_time/pallas_call | solution.py:21
  61.2 3.1 collective-permute-start.9
  69.9 7.9 %sweep_time.1 = (bf16[512,512]{1,0:T(8,128)(2,1)}, f32[4,512,128]{2,1,0:T(8,128)}, f32[512,512]{1,0:T(8,128)}, f32[512,512]{1,0:T(8,128)}, f32[512,512]{1,0:T(8,...) custom-call(f32[4,512,128]{2,1,0:T(8,128)} %get-tuple-element.92.key, ...), custom_call_target="tpu_custom_call" | custom-call | tf_op jit(solution)/shard_map/sweep_time/pallas_call | solution.py:21
  78.5 4.5 %emit.1.mine = f32[512,1024]{1,0:T(8,128)} custom-call(s32[5]{0:T(128)} %pad_add_fusion.idx, bf16[512,512]{1,0:T(8,128)(2,1)} %get-tuple-element.97.gated.refs_2_, bf16[512,256]{1,0:T(8,128)(2,1)} %p0.3, bf16[512,256]{1,0:T(8,128)(2,1)} %collective-permute-done.10.p1, bf16[512,256]{1,0:T(8,128)(2,1)} %collective-permute-done.11.p2, ...), custom_call_target="tpu_custom_call" | custom-call | tf_op jit(solution)/shard_map/emit/pallas_call | solution.py:21
  88.1 27.6 %collective-permute-done.16.h1 = bf16[256,2560]{1,0:T(8,128)(2,1)S(1)} collective-permute-done((bf16[256,2560]{1,0:T(8,128)(2,1)S(1)}, bf16[256,2560]{1,0:T(8,128)(2,1)S(1)}, u32[]{:S(2)}, u32[]{:S(2)}) %collective-permute-start.16) | collective-permute-done | bytes 1310752 | tf_op jit(solution)/shard_map/ppermute | solution.py:37
  117.9 20.3 %collective-permute-done.20.r1 = bf16[2048,256]{1,0:T(8,128)(2,1)S(1)} collective-permute-done((bf16[2048,256]{1,0:T(8,128)(2,1)S(1)}, bf16[2048,256]{1,0:T(8,128)(2,1)S(1)}, u32[]{:S(2)}, u32[]{:S(2)}) %collective-permute-start.20) | collective-permute-done | bytes 1048608 | tf_op jit(solution)/shard_map/ppermute | solution.py:37
  141.2 6.2 %middle_norm.1 = (f32[512,512]{1,0:T(8,128)}, f32[512,1024]{1,0:T(8,128)}, f32[512,1]{1,0:T(8,128)}, f32[2,1024]{1,0:T(2,128)}) custom-call(bf16[512,512]{1,0:T(8,128)(2,1)} %bitcast.162, bf16[512,512]{1,0:T(8,128)(2,1)} %copy-done.20, f32[512,1024]{1,0:T(8,128)} %emit.1.mine, f32[512,1024]{1,0:T(8,128)} %collective-permute-done.14.theirs), custom_call_target="tpu_custom_call" | custom-call | tf_op jit(solution)/shard_map/middle_norm/pallas_call | solution.py:21
  149.5 13.0 %collective-permute-done.22.r3 = bf16[1024,256]{1,0:T(8,128)(2,1)S(1)} collective-permute-done((bf16[1024,256]{1,0:T(8,128)(2,1)S(1)}, bf16[1024,256]{1,0:T(8,128)(2,1)S(1)}, u32[]{:S(2)}, u32[]{:S(2)}) %collective-permute-start.22) | collective-permute-done | bytes 524320 | tf_op jit(solution)/shard_map/ppermute | solution.py:37
  163.7 12.5 %channel_forward.1 = (bf16[512,1024]{1,0:T(8,128)(2,1)}, bf16[512,1024]{1,0:T(8,128)(2,1)}, f32[512,1024]{1,0:T(8,128)}, bf16[512,2048]{1,0:T(8,128)(2,1)}, bf16...) custom-call(s32[5]{0:T(128)} %pad_add_fusion.idx, ...), custom_call_target="tpu_custom_call" | custom-call | tf_op jit(solution)/shard_map/channel_forward/pallas_call | solution.py:21
  176.3 2.9 collective-permute-done.24.theirs
  180.1 4.0 close_block.1
  187.1 5.8 %weight_products.7 = (bf16[512,1024]{1,0:T(8,128)(2,1)}, bf16[512,1024]{1,0:T(8,128)(2,1)}, bf16[512,1024]{1,0:T(8,128)(2,1)}, bf16[512,1024]{1,0:T(8,128)(2,1)}) custom-call(s32[5]{0:T(128)} %pad_add_fusion.idx, bf16[512,512]{1,0:T(8,128)(2,1)} %get-tuple-element.105.gro.refs_0_, bf16[512,512]{1,0:T(8,128)(2,1)} %copy-done.21, ...), custom_call_target="tpu_custom_call" | custom-call | tf_op jit(solution)/shard_map/weight_products/pallas_call | solution.py:21
  194.9 16.3 %channel_backward.1 = (bf16[512,2048]{1,0:T(8,128)(2,1)}, f32[512,1024]{1,0:T(8,128)}, f32[2,1024]{1,0:T(2,128)}, f32[4,1024]{1,0:T(4,128)}) custom-call(s32[5]{0:T(128)} %pad_add_fusion.idx, bf16[512,512]{1,0:T(8,128)(2,1)} %get-tuple-element.105.gro.refs_0_, bf16[512,512]{1,0:T(8,128)(2,1)} %copy-done.21, bf16[512,512]{1,0:T(8,128)(2,1)} %get-tuple-element.106.gf.refs_3_, ...), custom_call_target="tpu_custom_call" | custom-call | tf_op jit(solution)/shard_map/channel_backward/pallas_call | solution.py:21
  211.3 7.6 %weight_products.6 = (bf16[512,1280]{1,0:T(8,128)(2,1)}, bf16[512,1280]{1,0:T(8,128)(2,1)}, bf16[512,1280]{1,0:T(8,128)(2,1)}, bf16[512,1280]{1,0:T(8,128)(2,1)}) custom-call(s32[5]{0:T(128)} %pad_add_fusion.idx, bf16[512,1024]{1,0:T(8,128)(2,1)} %get-tuple-element.146.refs_0_, bf16[512,1024]{1,0:T(8,128)(2,1)} %get-tuple-element.147.refs_1_, ...), custom_call_target="tpu_custom_call" | custom-call | tf_op jit(solution)/shard_map/weight_products/pallas_call | solution.py:21
  226.7 22.8 %collective-permute-done.52 = bf16[512,1280]{1,0:T(8,128)(2,1)} collective-permute-done((bf16[512,1280]{1,0:T(8,128)(2,1)}, bf16[512,1280]{1,0:T(8,128)(2,1)}, u32[]{:S(2)}, u32[]{:S(2)}) %collective-permute-start.52) | collective-permute-done | bytes 1310752 | tf_op jit(solution)/shard_map/ppermute | solution.py:37
  261.0 12.2 %middle_backward.1 = (bf16[512,1024]{1,0:T(8,128)(2,1)}, f32[512,512]{1,0:T(8,128)}, f32[4,512,128]{2,1,0:T(8,128)}, bf16[512,512]{1,0:T(8,128)(2,1)}, f32[4,32,128]{2,1,0:T(8,128)}, /*index=5*/f32[6,512]{1,0:T(8,128)}) custom-call(s32[5]{0:T(128)} %pad_add_fusion.idx, f32[512,1024]{1,0:T(8,128)} %get-tuple-element.109.mine, ...), custom_call_target="tpu_custom_call" | custom-call | tf_op jit(solution)/shard_map/middle_backward/pallas_call | solution.py:21
  283.2 16.7 %time_backward.1 = (bf16[512,512]{1,0:T(8,128)(2,1)}, bf16[512,512]{1,0:T(8,128)(2,1)}, f32[512,512]{1,0:T(8,128)}, f32[512,640]{1,0:T(8,128)}, f32[2,1024]{1,0:...) custom-call(s32[5]{0:T(128)} %pad_add_fusion.idx, f32[4,512,128]{2,1,0:T(8,128)} %get-tuple-element.116.res, ...), custom_call_target="tpu_custom_call" | custom-call | tf_op jit(solution)/shard_map/time_backward/pallas_call | solution.py:21
  311.1 4.6 %collective-permute-done.62 = bf16[128,2048]{1,0:T(8,128)(2,1)S(1)} collective-permute-done((bf16[128,2048]{1,0:T(8,128)(2,1)S(1)}, bf16[128,2048]{1,0:T(8,128)(2,1)S(1)}, u32[]{:S(2)}, u32[]{:S(2)}) %collective-permute-start.62) | collective-permute-done | bytes 524320 | tf_op jit(solution)/shard_map/ppermute | solution.py:37
  320.7 4.5 %weight_products.4 = (bf16[512,512]{1,0:T(8,128)(2,1)}, bf16[512,512]{1,0:T(8,128)(2,1)}, bf16[512,512]{1,0:T(8,128)(2,1)}, bf16[512,512]{1,0:T(8,128)(2,1)}) custom-call(s32[5]{0:T(128)} %pad_add_fusion.idx, bf16[512,1024]{1,0:T(8,128)(2,1)} %get-tuple-element.135.refs_0_, bf16[512,1024]{1,0:T(8,128)(2,1)} %get-tuple-element.91.mg.refs_1_, ...), custom_call_target="tpu_custom_call" | custom-call | tf_op jit(solution)/shard_map/weight_products/pallas_call | solution.py:21
  327.4 4.5 %weight_products.5 = (bf16[512,512]{1,0:T(8,128)(2,1)}, bf16[512,512]{1,0:T(8,128)(2,1)}, bf16[512,512]{1,0:T(8,128)(2,1)}, bf16[512,512]{1,0:T(8,128)(2,1)}) custom-call(s32[5]{0:T(128)} %pad_add_fusion.idx, bf16[512,1024]{1,0:T(8,128)(2,1)} %get-tuple-element.89.mk.refs_0_, bf16[512,1024]{1,0:T(8,128)(2,1)} %get-tuple-element.90.mv.refs_1_, ...), custom_call_target="tpu_custom_call" | custom-call | tf_op jit(solution)/shard_map/weight_products/pallas_call | solution.py:21
  342.9 7.4 %collective-permute-done.46 = bf16[512,512]{1,0:T(8,128)(2,1)S(1)} collective-permute-done((bf16[512,512]{1,0:T(8,128)(2,1)}, bf16[512,512]{1,0:T(8,128)(2,1)S(1)}, u32[]{:S(2)}, u32[]{:S(2)}) %collective-permute-start.46) | collective-permute-done | bytes 524320 | tf_op jit(solution)/shard_map/ppermute | solution.py:37
  361.5 2.5 collective-permute-start.49
  364.3 7.7 %collective-permute-start.57 = (bf16[64,2560]{1,0:T(8,128)(2,1)S(1)}, bf16[64,2560]{1,0:T(8,128)(2,1)S(1)}, u32[]{:S(2)}, u32[]{:S(2)}) collective-permute-start(bf16[64,2560]{1,0:T(8,128)(2,1)S(1)} %slice.294), channel_id=1, source_target_pairs={{0,4},{2,6},{4,0},{6,2},{1,5},{3,7},{5,1},{7,3},{8,12},{10,14},{12... | collective-permute-start | bytes 983048 | tf_op jit(solution)/shard_map/ppermute | solution.py:37
  372.5 12.8 %collective-permute-done.57 = bf16[64,2560]{1,0:T(8,128)(2,1)S(1)} collective-permute-done((bf16[64,2560]{1,0:T(8,128)(2,1)S(1)}, bf16[64,2560]{1,0:T(8,128)(2,1)S(1)}, u32[]{:S(2)}, u32[]{:S(2)}) %collective-permute-start.57) | collective-permute-done | bytes 327712 | tf_op jit(solution)/shard_map/ppermute | solution.py:37
  387.7 3.4 collective-permute-start.45
  391.1 4.2 %collective-permute-done.50 = bf16[128,1024]{1,0:T(8,128)(2,1)S(1)} collective-permute-done((bf16[128,1024]{1,0:T(8,128)(2,1)S(1)}, bf16[128,1024]{1,0:T(8,128)(2,1)S(1)}, u32[]{:S(2)}, u32[]{:S(2)}) %collective-permute-start.50) | collective-permute-done | bytes 262176 | tf_op jit(solution)/shard_map/ppermute | solution.py:37
  398.2 5.6 %collective-permute-done.51 = bf16[64,1024]{1,0:T(8,128)(2,1)S(1)} collective-permute-done((bf16[64,1024]{1,0:T(8,128)(2,1)S(1)}, bf16[64,1024]{1,0:T(8,128)(2,1)S(1)}, u32[]{:S(2)}, u32[]{:S(2)}) %collective-permute-start.51) | collective-permute-done | bytes 131104 | tf_op jit(solution)/shard_map/ppermute | solution.py:37
  405.6 5.7 %input_backward.1 = f32[512,512]{1,0:T(8,128)} custom-call(f32[512,512]{1,0:T(8,128)} %get-tuple-element.127.mine, f32[512,640]{1,0:T(8,128)} %get-tuple-element.128.sent, f32[512,640]{1,0:T(8,128)} %copy-done.24, f32[2,1024]{1,0:T(2,128)} %copy-done.49, f32[2,1024]{1,0:T(2,128)} %copy-done.50, f32[512,1024]{1,0:T(8,128)} %get-tuple-element.125.hat, ...), custom_call_target="tpu_custom_call" | custom-call | tf_op jit(solution)/shard_map/input_backward/pallas_call | solution.py:21
  (325 shorter events, 124.1 us)
Async XLA Ops:
  3.8 20.5 %collective-permute-start.4 = (bf16[256,1536]{1,0:T(8,128)(2,1)S(1)}, bf16[256,1536]{1,0:T(8,128)(2,1)S(1)}, u32[]{:S(2)}, u32[]{:S(2)}) collective-permute-start(bf16[256,1536]{1,0:T(8,128)(2,1)S(1)} %constant_dynamic-update-slice_fusion.p0), channel_id=1, source_target_pairs={{0,8},{8,0},{16,24},{24,16},{1,9},{9,1},{17,25},{25,17},{2,10},{10... | collective-permute-start | bytes 2359304 | tf_op jit(solution)/shard_map/ppermute | solution.py:37
  6.8 20.1 %collective-permute-start.5 = (bf16[256,1536]{1,0:T(8,128)(2,1)S(1)}, bf16[256,1536]{1,0:T(8,128)(2,1)S(1)}, u32[]{:S(2)}, u32[]{:S(2)}) collective-permute-start(bf16[256,1536]{1,0:T(8,128)(2,1)S(1)} %constant_dynamic-update-slice_fusion.p0), channel_id=1, source_target_pairs={{0,16},{8,24},{16,0},{24,8},{1,17},{9,25},{17,1},{25,9},{2,18},{10... | collective-permute-start | bytes 2359304 | tf_op jit(solution)/shard_map/ppermute | solution.py:37
  8.3 29.9 %collective-permute-start = (bf16[512,512]{1,0:T(8,128)(2,1)S(1)}, bf16[512,512]{1,0:T(8,128)(2,1)S(1)}, u32[]{:S(2)}, u32[]{:S(2)}) collective-permute-start(bf16[512,512]{1,0:T(8,128)(2,1)S(1)} %bitcast.163), channel_id=1, source_target_pairs={{0,1},{1,0},{2,3},{3,2},{4,5},{5,4},{6,7},{7,6},{8,9},{9,8},{10,11... | collective-permute-start | bytes 1572872 | tf_op jit(solution)/shard_map/ppermute | solution.py:37
  25.2 21.5 %collective-permute-start.6 = (bf16[256,768]{1,0:T(8,128)(2,1)}, bf16[256,768]{1,0:T(8,128)(2,1)}, u32[]{:S(2)}, u32[]{:S(2)}) collective-permute-start(bf16[256,768]{1,0:T(8,128)(2,1)} %slice.246), channel_id=1, source_target_pairs={{0,16},{8,24},{16,0},{24,8},{1,17},{9,25},{17,1},{25,9},{2,18},{10... | collective-permute-start | bytes 1179656 | tf_op jit(solution)/shard_map/ppermute | solution.py:37
  27.8 18.9 %collective-permute-start.7 = (bf16[256,768]{1,0:T(8,128)(2,1)}, bf16[256,768]{1,0:T(8,128)(2,1)}, u32[]{:S(2)}, u32[]{:S(2)}) collective-permute-start(bf16[256,768]{1,0:T(8,128)(2,1)} %slice.247), channel_id=1, source_target_pairs={{0,8},{8,0},{16,24},{24,16},{1,9},{9,1},{17,25},{25,17},{2,10},{10... | collective-permute-start | bytes 1179656 | tf_op jit(solution)/shard_map/ppermute | solution.py:37
  37.2 27.1 %collective-permute-start.10 = (bf16[512,256]{1,0:T(8,128)(2,1)}, bf16[512,256]{1,0:T(8,128)(2,1)}, u32[]{:S(2)}, u32[]{:S(2)}) collective-permute-start(bf16[512,256]{1,0:T(8,128)(2,1)} %p0.3), channel_id=1, source_target_pairs={{0,8},{8,0},{16,24},{24,16},{1,9},{9,1},{17,25},{25,17},{2,10},{10... | collective-permute-start | bytes 786440 | tf_op jit(solution)/shard_map/ppermute | solution.py:37
  37.8 29.0 %collective-permute-start.11 = (bf16[512,256]{1,0:T(8,128)(2,1)}, bf16[512,256]{1,0:T(8,128)(2,1)}, u32[]{:S(2)}, u32[]{:S(2)}) collective-permute-start(bf16[512,256]{1,0:T(8,128)(2,1)} %p0.3), channel_id=1, source_target_pairs={{0,16},{8,24},{16,0},{24,8},{1,17},{9,25},{17,1},{25,9},{2,18},{10... | collective-permute-start | bytes 786440 | tf_op jit(solution)/shard_map/ppermute | solution.py:37
  83.0 58.2 %collective-permute-start.14 = (f32[512,1024]{1,0:T(8,128)}, f32[512,1024]{1,0:T(8,128)}, u32[]{:S(2)}, u32[]{:S(2)}) collective-permute-start(f32[512,1024]{1,0:T(8,128)} %emit.1.mine), channel_id=1, source_target_pairs={{0,1},{1,0},{2,3},{3,2},{4,5},{5,4},{6,7},{7,6},{8,9},{9,8},{10,11... | collective-permute-start | bytes 6291464 | tf_op jit(solution)/shard_map/ppermute | solution.py:37
  84.0 31.7 %collective-permute-start.16 = (bf16[256,2560]{1,0:T(8,128)(2,1)S(1)}, bf16[256,2560]{1,0:T(8,128)(2,1)S(1)}, u32[]{:S(2)}, u32[]{:S(2)}) collective-permute-start(bf16[256,2560]{1,0:T(8,128)(2,1)S(1)} %constant_dynamic-update-slice_fusion.3.h0), channel_id=1, source_target_pairs={{0,8},{8,0},{16,24},{24,16},{1,9},{9,1},{17,25},{25,17},{2,10},{10... | collective-permute-start | bytes 3932168 | tf_op jit(solution)/shard_map/ppermute | solution.py:37
  84.6 31.8 %collective-permute-start.17 = (bf16[256,2560]{1,0:T(8,128)(2,1)S(1)}, bf16[256,2560]{1,0:T(8,128)(2,1)S(1)}, u32[]{:S(2)}, u32[]{:S(2)}) collective-permute-start(bf16[256,2560]{1,0:T(8,128)(2,1)S(1)} %constant_dynamic-update-slice_fusion.3.h0), channel_id=1, source_target_pairs={{0,16},{8,24},{16,0},{24,8},{1,17},{9,25},{17,1},{25,9},{2,18},{10... | collective-permute-start | bytes 3932168 | tf_op jit(solution)/shard_map/ppermute | solution.py:37
  85.2 53.0 %collective-permute-start.20 = (bf16[2048,256]{1,0:T(8,128)(2,1)S(1)}, bf16[2048,256]{1,0:T(8,128)(2,1)S(1)}, u32[]{:S(2)}, u32[]{:S(2)}) collective-permute-start(bf16[2048,256]{1,0:T(8,128)(2,1)S(1)} %copy-done.12), channel_id=1, source_target_pairs={{0,8},{8,0},{16,24},{24,16},{1,9},{9,1},{17,25},{25,17},{2,10},{10... | collective-permute-start | bytes 3145736 | tf_op jit(solution)/shard_map/ppermute | solution.py:37
  86.6 52.2 %collective-permute-start.21 = (bf16[2048,256]{1,0:T(8,128)(2,1)S(1)}, bf16[2048,256]{1,0:T(8,128)(2,1)S(1)}, u32[]{:S(2)}, u32[]{:S(2)}) collective-permute-start(bf16[2048,256]{1,0:T(8,128)(2,1)S(1)} %copy-done.12), channel_id=1, source_target_pairs={{0,16},{8,24},{16,0},{24,8},{1,17},{9,25},{17,1},{25,9},{2,18},{10... | collective-permute-start | bytes 3145736 | tf_op jit(solution)/shard_map/ppermute | solution.py:37
  115.8 46.7 %collective-permute-start.18 = (bf16[256,1280]{1,0:T(8,128)(2,1)S(1)}, bf16[256,1280]{1,0:T(8,128)(2,1)S(1)}, u32[]{:S(2)}, u32[]{:S(2)}) collective-permute-start(bf16[256,1280]{1,0:T(8,128)(2,1)S(1)} %slice.250), channel_id=1, source_target_pairs={{0,16},{8,24},{16,0},{24,8},{1,17},{9,25},{17,1},{25,9},{2,18},{10... | collective-permute-start | bytes 1966088 | tf_op jit(solution)/shard_map/ppermute | solution.py:37
  116.8 45.7 %collective-permute-start.19 = (bf16[256,1280]{1,0:T(8,128)(2,1)S(1)}, bf16[256,1280]{1,0:T(8,128)(2,1)}, u32[]{:S(2)}, u32[]{:S(2)}) collective-permute-start(bf16[256,1280]{1,0:T(8,128)(2,1)S(1)} %slice.251), channel_id=1, source_target_pairs={{0,8},{8,0},{16,24},{24,16},{1,9},{9,1},{17,25},{25,17},{2,10},{10... | collective-permute-start | bytes 1966088 | tf_op jit(solution)/shard_map/ppermute | solution.py:37
  138.2 24.2 %collective-permute-start.22 = (bf16[1024,256]{1,0:T(8,128)(2,1)S(1)}, bf16[1024,256]{1,0:T(8,128)(2,1)S(1)}, u32[]{:S(2)}, u32[]{:S(2)}) collective-permute-start(bf16[1024,256]{1,0:T(8,128)(2,1)S(1)} %slice.252), channel_id=1, source_target_pairs={{0,16},{8,24},{16,0},{24,8},{1,17},{9,25},{17,1},{25,9},{2,18},{10... | collective-permute-start | bytes 1572872 | tf_op jit(solution)/shard_map/ppermute | solution.py:37
  139.8 22.7 %collective-permute-start.23 = (bf16[1024,256]{1,0:T(8,128)(2,1)}, bf16[1024,256]{1,0:T(8,128)(2,1)S(1)}, u32[]{:S(2)}, u32[]{:S(2)}) collective-permute-start(bf16[1024,256]{1,0:T(8,128)(2,1)} %slice.253), channel_id=1, source_target_pairs={{0,8},{8,0},{16,24},{24,16},{1,9},{9,1},{17,25},{25,17},{2,10},{10... | collective-permute-start | bytes 1572872 | tf_op jit(solution)/shard_map/ppermute | solution.py:37
  192.9 28.0 %collective-permute-start.58 = (bf16[512,1024]{1,0:T(8,128)(2,1)}, bf16[512,1024]{1,0:T(8,128)(2,1)S(1)}, u32[]{:S(2)}, u32[]{:S(2)}) collective-permute-start(bf16[512,1024]{1,0:T(8,128)(2,1)} %get-tuple-element.155), channel_id=1, source_target_pairs={{0,8},{8,0},{16,24},{24,16},{1,9},{9,1},{17,25},{25,17},{2,10},{10... | collective-permute-start | bytes 3145736 | tf_op jit(solution)/shard_map/ppermute | solution.py:37
  194.4 29.5 %collective-permute-start.60 = (bf16[512,1024]{1,0:T(8,128)(2,1)}, bf16[512,1024]{1,0:T(8,128)(2,1)S(1)}, u32[]{:S(2)}, u32[]{:S(2)}) collective-permute-start(bf16[512,1024]{1,0:T(8,128)(2,1)} %get-tuple-element.157), channel_id=1, source_target_pairs={{0,16},{8,24},{16,0},{24,8},{1,17},{9,25},{17,1},{25,9},{2,18},{10... | collective-permute-start | bytes 3145736 | tf_op jit(solution)/shard_map/ppermute | solution.py:37
  218.9 30.6 %collective-permute-start.52 = (bf16[512,1280]{1,0:T(8,128)(2,1)}, bf16[512,1280]{1,0:T(8,128)(2,1)}, u32[]{:S(2)}, u32[]{:S(2)}) collective-permute-start(bf16[512,1280]{1,0:T(8,128)(2,1)} %get-tuple-element.150), channel_id=1, source_target_pairs={{0,8},{8,0},{16,24},{24,16},{1,9},{9,1},{17,25},{25,17},{2,10},{10... | collective-permute-start | bytes 3932168 | tf_op jit(solution)/shard_map/ppermute | solution.py:37
  219.4 41.6 %collective-permute-start.26 = (f32[512,1024]{1,0:T(8,128)}, f32[512,1024]{1,0:T(8,128)}, u32[]{:S(2)}, u32[]{:S(2)}) collective-permute-start(f32[512,1024]{1,0:T(8,128)} %get-tuple-element.109.mine), channel_id=1, source_target_pairs={{0,1},{1,0},{2,3},{3,2},{4,5},{5,4},{6,7},{7,6},{8,9},{9,8},{10,11... | collective-permute-start | bytes 6291464 | tf_op jit(solution)/shard_map/ppermute | solution.py:37
  219.4 33.2 %collective-permute-start.54 = (bf16[512,1280]{1,0:T(8,128)(2,1)}, bf16[512,1280]{1,0:T(8,128)(2,1)}, u32[]{:S(2)}, u32[]{:S(2)}) collective-permute-start(bf16[512,1280]{1,0:T(8,128)(2,1)} %get-tuple-element.152), channel_id=1, source_target_pairs={{0,16},{8,24},{16,0},{24,8},{1,17},{9,25},{17,1},{25,9},{2,18},{10... | collective-permute-start | bytes 3932168 | tf_op jit(solution)/shard_map/ppermute | solution.py:37
  220.9 36.7 %collective-permute-start.29 = (bf16[512,512]{1,0:T(8,128)(2,1)S(1)}, bf16[512,512]{1,0:T(8,128)(2,1)S(1)}, u32[]{:S(2)}, u32[]{:S(2)}) collective-permute-start(bf16[512,512]{1,0:T(8,128)(2,1)S(1)} %bitcast.166), channel_id=1, source_target_pairs={{0,1},{1,0},{2,3},{3,2},{4,5},{5,4},{6,7},{7,6},{8,9},{9,8},{10,11... | collective-permute-start | bytes 1572872 | tf_op jit(solution)/shard_map/ppermute | solution.py:37
  223.9 35.0 %collective-permute-start.27 = (f32[2,1024]{1,0:T(2,128)S(1)}, f32[2,1024]{1,0:T(2,128)S(1)}, u32[]{:S(2)}, u32[]{:S(2)}) collective-permute-start(f32[2,1024]{1,0:T(2,128)S(1)} %copy-done.65), channel_id=1, source_target_pairs={{2,0},{4,2},{6,4},{3,1},{5,3},{7,5},{10,8},{12,10},{14,12},{11,9},... | collective-permute-start | bytes 24584 | tf_op jit(solution)/shard_map/ppermute | solution.py:44
  252.6 22.5 %collective-permute-start.59 = (bf16[256,1024]{1,0:T(8,128)(2,1)S(1)}, bf16[256,1024]{1,0:T(8,128)(2,1)}, u32[]{:S(2)}, u32[]{:S(2)}) collective-permute-start(bf16[256,1024]{1,0:T(8,128)(2,1)S(1)} %slice.298), channel_id=1, source_target_pairs={{0,16},{8,24},{16,0},{24,8},{1,17},{9,25},{17,1},{25,9},{2,18},{10... | collective-permute-start | bytes 1572872 | tf_op jit(solution)/shard_map/ppermute | solution.py:37
  258.4 20.8 %collective-permute-start.61 = (bf16[256,1024]{1,0:T(8,128)(2,1)}, bf16[256,1024]{1,0:T(8,128)(2,1)}, u32[]{:S(2)}, u32[]{:S(2)}) collective-permute-start(bf16[256,1024]{1,0:T(8,128)(2,1)} %slice.300), channel_id=1, source_target_pairs={{0,8},{8,0},{16,24},{24,16},{1,9},{9,1},{17,25},{25,17},{2,10},{10... | collective-permute-start | bytes 1572872 | tf_op jit(solution)/shard_map/ppermute | solution.py:37
  259.0 43.9 %collective-permute-start.53 = (bf16[256,1280]{1,0:T(8,128)(2,1)}, bf16[256,1280]{1,0:T(8,128)(2,1)}, u32[]{:S(2)}, u32[]{:S(2)}) collective-permute-start(bf16[256,1280]{1,0:T(8,128)(2,1)} %slice.288), channel_id=1, source_target_pairs={{0,16},{8,24},{16,0},{24,8},{1,17},{9,25},{17,1},{25,9},{2,18},{10... | collective-permute-start | bytes 1966088 | tf_op jit(solution)/shard_map/ppermute | solution.py:37
  259.5 48.1 %collective-permute-start.55 = (bf16[256,1280]{1,0:T(8,128)(2,1)}, bf16[256,1280]{1,0:T(8,128)(2,1)}, u32[]{:S(2)}, u32[]{:S(2)}) collective-permute-start(bf16[256,1280]{1,0:T(8,128)(2,1)} %slice.290), channel_id=1, source_target_pairs={{0,8},{8,0},{16,24},{24,16},{1,9},{9,1},{17,25},{25,17},{2,10},{10... | collective-permute-start | bytes 1966088 | tf_op jit(solution)/shard_map/ppermute | solution.py:37
  319.8 22.8 %collective-permute-start.56 = (bf16[128,2560]{1,0:T(8,128)(2,1)}, bf16[128,2560]{1,0:T(8,128)(2,1)S(1)}, u32[]{:S(2)}, u32[]{:S(2)}) collective-permute-start(bf16[128,2560]{1,0:T(8,128)(2,1)} %pad_maximum_fusion), channel_id=1, source_target_pairs={{0,2},{2,0},{4,6},{6,4},{1,3},{3,1},{5,7},{7,5},{8,10},{10,8},{12,... | collective-permute-start | bytes 1966088 | tf_op jit(solution)/shard_map/ppermute | solution.py:37
  332.0 72.6 %collective-permute-start.33 = (f32[2,1024]{1,0:T(2,128)S(1)}, f32[2,1024]{1,0:T(2,128)S(1)}, u32[]{:S(2)}, u32[]{:S(2)}) collective-permute-start(f32[2,1024]{1,0:T(2,128)S(1)} %copy-done.64), channel_id=1, source_target_pairs={{2,0},{4,2},{6,4},{3,1},{5,3},{7,5},{10,8},{12,10},{14,12},{11,9},... | collective-permute-start | bytes 24584 | tf_op jit(solution)/shard_map/ppermute | solution.py:44
  334.0 70.5 %collective-permute-start.34 = (f32[2,1024]{1,0:T(2,128)S(1)}, f32[2,1024]{1,0:T(2,128)S(1)}, u32[]{:S(2)}, u32[]{:S(2)}) collective-permute-start(f32[2,1024]{1,0:T(2,128)S(1)} %copy-done.64), channel_id=1, source_target_pairs={{2,1},{3,0},{4,3},{5,2},{6,5},{7,4},{10,9},{11,8},{12,11},{13,10},... | collective-permute-start | bytes 24584 | tf_op jit(solution)/shard_map/ppermute | solution.py:50
  342.6 61.9 %collective-permute-start.32 = (f32[512,640]{1,0:T(8,128)S(1)}, f32[512,640]{1,0:T(8,128)S(1)}, u32[]{:S(2)}, u32[]{:S(2)}) collective-permute-start(f32[512,640]{1,0:T(8,128)S(1)} %copy-done.23), channel_id=1, source_target_pairs={{0,1},{1,0},{2,3},{3,2},{4,5},{5,4},{6,7},{7,6},{8,9},{9,8},{10,11... | collective-permute-start | bytes 3932168 | tf_op jit(solution)/shard_map/ppermute | solution.py:37
  364.3 21.1 %collective-permute-start.57 = (bf16[64,2560]{1,0:T(8,128)(2,1)S(1)}, bf16[64,2560]{1,0:T(8,128)(2,1)S(1)}, u32[]{:S(2)}, u32[]{:S(2)}) collective-permute-start(bf16[64,2560]{1,0:T(8,128)(2,1)S(1)} %slice.294), channel_id=1, source_target_pairs={{0,4},{2,6},{4,0},{6,2},{1,5},{3,7},{5,1},{7,3},{8,12},{10,14},{12... | collective-permute-start | bytes 983048 | tf_op jit(solution)/shard_map/ppermute | solution.py:37
  (98 other events, 986.4 us)

commit v2 on v1

--- a/solution.py
+++ b/solution.py
@@ -10,6 +10,7 @@
 epsilon = 1e-05
 lowest = -1e30
 CHUNKS = 8
+SPARE = 6 * 2**20
 
 VMEM = pl.BlockSpec(memory_space=pltpu.VMEM)
 SMEM = pl.BlockSpec(memory_space=pltpu.SMEM)
@@ -17,15 +18,60 @@
 KINDS = {"v": VMEM, "s": SMEM, "h": HBM}
 
 
-def launch(body, kinds, inputs, outs, scratch=()):
+def padded_bytes(shape, dtype):
+    rows = -(-shape[-2] // 8) * 8
+    lanes = -(-shape[-1] // 128) * 128
+    size = rows * lanes * jnp.dtype(dtype).itemsize
+    for dim in shape[:-2]:
+        size *= dim
+    return size
+
+
+def launch(body, kinds, inputs, outs, scratch=(), after=()):
+    count = len(kinds)
+    room = sum(padded_bytes(x.shape, x.dtype) for x in scratch if len(x.shape) > 1) + SPARE
+
+    def run(*refs):
+        body(*refs[:count], *refs[count + len(after) :])
+
     return pl.pallas_call(
-        body,
-        out_shape=[jax.ShapeDtypeStruct(shape, dtype) for shape, dtype in outs],
-        in_specs=[KINDS[kind] for kind in kinds],
+        run,
+        out_shape=[
+            jax.ShapeDtypeStruct(shape, dtype) for shape, dtype in outs
+        ],
+        in_specs=[KINDS[kind] for kind in kinds] + [HBM] * len(after),
         out_specs=[VMEM] * len(outs),
         scratch_shapes=list(scratch),
         name=body.__name__,
-    )(*inputs)
+        compiler_params=pltpu.CompilerParams(vmem_limit_bytes=room),
+    )(*inputs, *after)
+
+
+def side_by_side(*parts):
+    widths = [part.shape[1] for part in parts]
+
+    def pack(*refs):
+        sources, whole, sems = refs[: len(parts)], refs[-2], refs[-1]
+        copies, at = [], 0
+        for i, source in enumerate(sources):
+            target = whole.at[:, pl.ds(at, widths[i])]
+            copies.append(pltpu.make_async_copy(source, target, sems.at[i]))
+            at += widths[i]
+        begin(copies)
+        finish(copies)
+
+    (whole,) = launch(
+        pack,
+        "h" * len(parts),
+        [pltpu.with_memory_space_constraint(part, pltpu.HBM) for part in parts],
+        [((parts[0].shape[0], sum(widths)), parts[0].dtype)],
+        [pltpu.SemaphoreType.DMA((len(parts),))],
+    )
+    return whole
+
+
+def hold(values, *others):
+    return lax.optimization_barrier((values, others))[0]
 
 
 def bits_of(count):
@@ -50,33 +96,42 @@
     return lax.ppermute(value, ("ctx", "tp"), pairs)
 
 
-def gather_pieces(matrix, cut):
-    half = matrix.shape[cut] // 2
-    across_x = swap(matrix, "shard", 1)
-    across_y = swap(matrix, "shard", 2)
-    first = swap(lax.slice_in_dim(across_x, 0, half, axis=cut), "shard", 2)
-    second = swap(lax.slice_in_dim(across_y, half, 2 * half, axis=cut), "shard", 1)
-    return [matrix, across_x, across_y, first, second]
-
-
-def place_rows(idx, pieces, whole, sems):
+def gather_first(matrix):
+    return swap(matrix, "shard", 1), swap(matrix, "shard", 2)
+
+
+def gather_turn(across, cut):
+    half = across[0].shape[cut] // 2
+    return (
+        lax.slice_in_dim(across[0], 0, half, axis=cut),
+        lax.slice_in_dim(across[1], half, 2 * half, axis=cut),
+    )
+
+
+def gather_cross(turn):
+    return swap(turn[0], "shard", 2), swap(turn[1], "shard", 1)
+
+
+def place_rows(idx, pieces, whole, sems, start=0, stop=None):
     base = idx[0]
     rows, cols = pieces[0].shape
     half = cols // 2
+    stop = cols if stop is None else stop
 
     def spot(step):
         return pl.ds(pl.multiple_of((base ^ step) * rows, rows), rows)
 
-    targets = [
-        whole.at[spot(0), :],
-        whole.at[spot(1), :],
-        whole.at[spot(2), :],
-        whole.at[spot(3), pl.ds(0, half)],
-        whole.at[spot(3), pl.ds(half, half)],
-    ]
+    copies = []
+    for step in range(3):
+        copies.append((pieces[step].at[:, pl.ds(start, stop - start)], whole.at[spot(step), :]))
+    for i in range(2):
+        low, high = max(start, i * half), min(stop, (i + 1) * half)
+        if low < high:
+            source = pieces[3 + i].at[:, pl.ds(low - i * half, high - low)]
+            copies.append((source, whole.at[spot(3), pl.ds(low - start, high - low)]))
     return [
-        pltpu.make_async_copy(piece, target, sems.at[i])
-        for i, (piece, target) in enumerate(zip(pieces, targets))
+        pltpu.make_async_copy(source, target, sems.at[i])
+        for i, (source, target) in enumerate(copies)
     ]
 
 
@@ -151,6 +206,16 @@
 def put(ref, rows, values):
     for g in range(ref.shape[0]):
         ref[g, rows, :] = values[:, g * 128 : (g + 1) * 128]
+
+
+def columns(refs, rows):
+    return jnp.concatenate([ref[rows, :] for ref in refs], axis=1)
+
+
+def swap_parts(parts):
+    half = len(parts) // 2
+    got = [swap(part, "tp", 1) for part in parts]
+    return got[half:] + got[:half]
 
 
 def swapped(values):
@@ -234,28 +299,29 @@
     )
     fading = logarithmic_fading_per_feature.reshape(1, H)
     bonus = present_entry_reward.reshape(1, H)
-    time_pieces = gather_pieces(
-        jnp.concatenate([lookup_projection, payload_projection, filter_projection], axis=1), 1
-    )
+    time_matrix = side_by_side(
+        lookup_projection,
+        payload_projection,
+        filter_projection,
+        temporal_mix_emit_projection.T,
+    )
+    time_first = gather_first(time_matrix)
     x_other = swap(x_own, "tp", 1)
     params_other = swap(params, "tp", 1)
-    edge_out = block_entries[:, :, L - 1, :].reshape(R, H)
-    edge_own = along_ctx(edge_out, 1, False)
-    edge_other = along_ctx(edge_out, 1, True)
-    emit_pieces = gather_pieces(temporal_mix_emit_projection, 0)
-    hidden_pieces = gather_pieces(
-        jnp.concatenate([feature_mix_lookup_proj, feature_mix_filter_proj], axis=1), 1
-    )
-    return_pieces = gather_pieces(feature_mix_payload_proj, 0)
+    last_rows = [
+        part.reshape(batches, rows_local, L, H)[:, :, L - 1, :].reshape(R, H)
+        for part in (x_own, x_other)
+    ]
+    edge = along_ctx(jnp.concatenate(last_rows, axis=1), 1, False)
     up_other = swap(up_own, "tp", 1)
 
     def mix_time(
-        idx, xo, xp, eo, ep, po, pp, mixed_key, mixed_value, mixed_gate, hat, diff, root, hat_edge
+        idx, xo, xp, ed, po, pp, mixed_key, mixed_value, mixed_gate, hat, diff, root, hat_edge
     ):
         gain, bias = both(po, pp, 0), both(po, pp, 1)
         shares = [both(po, pp, i) for i in (2, 3, 4)]
         flag = jnp.where(idx[1] > 0, 1.0, 0.0).astype(F32)
-        edge_hat, _ = norm(jnp.concatenate([eo[...], ep[...]], axis=1).astype(F32))
+        edge_hat, _ = norm(ed[...].astype(F32))
         hat_edge[...] = edge_hat * flag
         first = (edge_hat * gain + bias) * flag
         for r in range(R):
@@ -266,27 +332,39 @@
                 n, q = norm(values)
                 normed = n * gain + bias
                 prev = shift_down(normed, last)
-                hat[at, :] = n
+                hat[at, :] = n.astype(BF16)
                 root[at, :] = q
-                diff[at, :] = normed - prev
+                diff[at, :] = (normed - prev).astype(BF16)
                 for share, target in zip(shares, (mixed_key, mixed_value, mixed_gate)):
                     target[at, :] = (normed * share + prev * (1.0 - share)).astype(BF16)
                 return normed[TB - 1 : TB, :]
 
             lax.fori_loop(0, NT, tile, first[r : r + 1, :])
 
-    mixed_key, mixed_value, mixed_gate, hat_one, diff_one, root_one, hat_edge_one = launch(
-        mix_time,
-        "svvvvvv",
-        (idx, x_own, x_other, edge_own, edge_other, params, params_other),
-        [((T, WIDTH), BF16)] * 3
-        + [((T, WIDTH), F32), ((T, WIDTH), F32), ((T, 1), F32), ((R, WIDTH), F32)],
-    )
+    def mixes(*tokens):
+        return launch(
+            mix_time,
+            "svvvvv",
+            (idx, *tokens, edge, params, params_other),
+            [((T, WIDTH), BF16)] * 5 + [((T, 1), F32), ((R, WIDTH), F32)],
+        )
+
+    mixed_key, mixed_value, mixed_gate, *_, hat_edge_one = mixes(x_own, x_other)
+    time_turn = gather_turn(hold(time_first, hat_edge_one), 1)
+    time_across = gather_cross(time_turn)
+    time_pieces = [time_matrix, *time_first, *time_across]
+    hidden_matrix = side_by_side(feature_mix_lookup_proj, feature_mix_filter_proj)
+    hidden_first = gather_first(hold(hidden_matrix, time_across))
+    return_matrix = hold(feature_mix_payload_proj, time_across)
+    return_first = gather_first(return_matrix)
+    return_turn_in = gather_turn(return_first, 0)
+    return_across = gather_cross(return_turn_in)
+    return_pieces = [return_matrix, *return_first, *return_across]
 
     def project_time(
         idx, mk, mv, mg, ld, p0, p1, p2, p3, p4, key, value, opened, states, closing, w, sems
     ):
-        copies = place_rows(idx, [p0, p1, p2, p3, p4], w, sems)
+        copies = place_rows(idx, [p0, p1, p2, p3, p4], w, sems, 0, 3 * H)
         begin(copies)
         finish(copies)
         put(key, EVERY, dot(mk[...], w[:, :H]))
@@ -325,27 +403,64 @@
         [((G, T, 128), F32)] * 2
         + [((T, H), F32), ((G, 3 * R * CHUNKS, 128), F32), ((3 * R, H), F32)],
         [pltpu.VMEM((WIDTH, 3 * H), BF16), pltpu.SemaphoreType.DMA((5,))],
-    )
-
-    rate = jnp.exp(fading)
-    total = tuple(closing.reshape(3, R, H))
-    prefix = (jnp.zeros((R, H), F32), jnp.zeros((R, H), F32), jnp.full((R, H), lowest, F32))
-    for bit in range(bits_of(C)):
-        other = tuple(swap(jnp.stack(total), "ctx", 1 << bit))
-        up = (c_at >> bit) & 1 == 1
-        span = rate * (L << bit)
-        so_far = rate * (L * (c_at & ((1 << bit) - 1))).astype(F32)
-        with_other = combine(other, prefix, so_far)
-        prefix = tuple(jnp.where(up, a, b) for a, b in zip(with_other, prefix))
-        if bit + 1 < bits_of(C):
-            as_later, as_earlier = combine(other, total, span), combine(total, other, span)
-            total = tuple(jnp.where(up, a, b) for a, b in zip(as_later, as_earlier))
-    entering = jnp.concatenate(prefix, axis=0)
-
-    def sweep_time(
-        key, value, opened, ld, un, states, enter,
-        gated, out, part_old, part_new, keep, fresh, nums, dens, fade, starts,
-    ):
+        after=(up_other,),
+    )
+
+    def parts_of(ref):
+        return tuple(ref[pl.ds(part * R, R), :] for part in range(3))
+
+    def put_parts(ref, values):
+        for part in range(3):
+            ref[pl.ds(part * R, R), :] = values[part]
+
+    def scan_rounds(first_total, empty, join):
+        total, so_far = first_total, None
+        for bit in range(bits_of(C)):
+            other = swap(total, "ctx", 1 << bit)
+            last = bit + 1 == bits_of(C)
+
+            def join_round(idx, ld, total, other, *refs):
+                if so_far is None:
+                    before = empty()
+                else:
+                    before, refs = parts_of(refs[0]), refs[1:]
+                new_total, new_before = join(
+                    idx, ld, bit, parts_of(total), parts_of(other), before
+                )
+                put_parts(refs[0], new_before)
+                if not last:
+                    put_parts(refs[1], new_total)
+
+            inputs = [idx, fading, total, other] + ([] if so_far is None else [so_far])
+            so_far, *rest = launch(
+                join_round, "s" + "v" * (len(inputs) - 1), inputs, [((3 * R, H), F32)] * (2 - last)
+            )
+            total = None if last else rest[0]
+        return so_far
+
+    def no_state():
+        zero = jnp.zeros((R, H), F32)
+        return (zero, zero, zero + lowest)
+
+    def join_states(idx, ld, bit, total, other, before):
+        up = (idx[1] >> bit) & 1 == 1
+        rate = jnp.exp(ld[...])
+        span = rate * float(L << bit)
+        passed = (L * (idx[1] & ((1 << bit) - 1))).astype(F32)
+        with_other = combine(other, before, rate * passed)
+        as_later, as_earlier = combine(other, total, span), combine(total, other, span)
+        return (
+            tuple(jnp.where(up, a, b) for a, b in zip(as_later, as_earlier)),
+            tuple(jnp.where(up, a, b) for a, b in zip(with_other, before)),
+        )
+
+    entering = scan_rounds(closing, no_state, join_states)
+
+    hidden_turn = gather_turn(hold(hidden_first, entering), 1)
+    hidden_across = gather_cross(hidden_turn)
+    hidden_pieces = [hidden_matrix, *hidden_first, *hidden_across]
+
+    def sweep(key, value, opened, ld, un, states, enter, gated, out, starts, saved=None):
         rate = jnp.exp(ld[...])
         reward = un[...]
         state = tuple(enter[pl.ds(part * R, R), :] for part in range(3))
@@ -368,15 +483,18 @@
                 inverse = 1.0 / (e_old * den + e_new)
                 e_old, e_new = e_old * inverse, e_new * inverse
                 put(out, step_rows(r, t), e_old * num + e_new * v_now)
-                part_old[at, :] = e_old
-                part_new[at, :] = e_new
-                nums[at, :] = num
-                dens[at, :] = den
+                if saved:
+                    part_old, part_new, keep, fresh, nums, dens, fade = saved
+                    part_old[at, :] = e_old
+                    part_new[at, :] = e_new
+                    nums[at, :] = num
+                    dens[at, :] = den
                 faded = high - rate
                 peak = jnp.maximum(faded, k_now)
                 a, b = jnp.exp(faded - peak), jnp.exp(k_now - peak)
-                keep[at, :] = a
-                fresh[at, :] = b
+                if saved:
+                    keep[at, :] = a
+                    fresh[at, :] = b
                 new.append((a * num + b * v_now, a * den + b, peak))
             return tuple(new)
 
@@ -385,47 +503,50 @@
             for r in range(R)
         )
         ends = lax.fori_loop(0, ST, step, begin_at)
-        for r in range(R):
-            put(
-                fade,
-                pl.ds(r * CHUNKS, CHUNKS),
-                jnp.exp(begin_at[r][2] - ST * rate - ends[r][2]),
-            )
+        if saved:
+            for r in range(R):
+                put(
+                    saved[-1],
+                    pl.ds(r * CHUNKS, CHUNKS),
+                    jnp.exp(begin_at[r][2] - ST * rate - ends[r][2]),
+                )
         gated[...] = (opened[...] * get(out, EVERY)).astype(BF16)
 
-    gated, mixed_out, part_old, part_new, keep, fresh, nums, dens, fade = launch(
+    def sweep_time(
+        idx, key, value, opened, ld, un, states, enter, p0, p1, p2, p3, p4,
+        e0, e1, e2, e3, gated, out, starts, w, sems,
+    ):
+        copies = place_rows(idx, [p0, p1, p2, p3, p4], w, sems, 3 * H, 4 * H)
+        begin(copies)
+        sweep(key, value, opened, ld, un, states, enter, gated, out, starts)
+        finish(copies)
+        for p, part in enumerate((e0, e1, e2, e3)):
+            part[...] = dot_t(gated[...], w[p * SR : (p + 1) * SR, :])
+
+    emitted = launch(
         sweep_time,
-        "v" * 7,
-        (key, value, opened, fading, bonus, states, entering),
-        [((T, H), BF16), ((G, T, 128), F32)]
-        + [((T, H), F32)] * 6
-        + [((G, R * CHUNKS, 128), F32)],
-        [pltpu.VMEM((G, 3 * R * CHUNKS, 128), F32)],
-    )
-
-    def emit(idx, gated, p0, p1, p2, p3, p4, part, w, sems):
-        copies = place_blocks(idx, [p0, p1, p2, p3, p4], w, sems)
-        begin(copies)
-        finish(copies)
-        for p in range(S):
-            part[:, p * SR : (p + 1) * SR] = dot(gated[...], w[p])
-
-    (emitted,) = launch(
-        emit,
-        "sv" + "h" * 5,
-        (idx, gated, *emit_pieces),
-        [((T, WIDTH), F32)],
-        [pltpu.VMEM((S, H, SR), BF16), pltpu.SemaphoreType.DMA((5,))],
-    )
-    emitted_other = swap(emitted, "tp", 1)
-
-    def middle_norm(xo, xp, mine, theirs, middle, hat, root, last):
+        "s" + "v" * 7 + "h" * 5,
+        (idx, key, value, opened, fading, bonus, states, entering, *time_pieces),
+        [((T, SR), F32)] * S,
+        [
+            pltpu.VMEM((T, H), BF16),
+            pltpu.VMEM((G, T, 128), F32),
+            pltpu.VMEM((G, 3 * R * CHUNKS, 128), F32),
+            pltpu.VMEM((WIDTH, H), BF16),
+            pltpu.SemaphoreType.DMA((5,)),
+        ],
+        after=hidden_turn,
+    )
+    emitted_other = swap_parts(emitted)
+
+    def middle_norm(xo, xp, *refs):
+        mine, theirs, (middle, hat, root, last) = refs[:S], refs[S : 2 * S], refs[2 * S :]
         for r in range(R):
 
             def tile(i, carry):
                 at = rows_at(r, i)
                 values = jnp.concatenate([xo[at, :], xp[at, :]], axis=1).astype(F32)
-                values = values + (mine[at, :] + swapped(theirs[at, :]))
+                values = values + (columns(mine, at) + columns(theirs, at))
                 n, q = norm(values)
                 middle[at, :] = values[:, :H]
                 hat[at, :] = n
@@ -436,23 +557,21 @@
 
     middle, hat_two, root_two, hat_last = launch(
         middle_norm,
-        "vvvv",
-        (x_own, x_other, emitted, emitted_other),
+        "vv" + "v" * (2 * S),
+        (x_own, x_other, *emitted, *emitted_other),
         [((T, H), F32), ((T, WIDTH), F32), ((T, 1), F32), ((R, WIDTH), F32)],
+        after=return_turn_in,
     )
     hat_edge_two = along_ctx(hat_last, 1, False)
-
     NF = FH + H
     NB = min(512, FH)
 
     def channel_forward(
-        idx, hat, edge, po, pp, h0, h1, h2, h3, h4, r0, r1, r2, r3, r4,
-        ckey, cgate, diff, active, squared, keep_own, send_other, opened, wh, wr, sems_h, sems_r,
+        idx, hat, edge, po, pp, h0, h1, h2, h3, h4,
+        ckey, cgate, diff, hat_low, active, squared, opened, wh, sems_h,
     ):
         copies_h = place_rows(idx, [h0, h1, h2, h3, h4], wh, sems_h)
-        copies_r = place_blocks(idx, [r0, r1, r2, r3, r4], wr, sems_r)
         begin(copies_h)
-        begin(copies_r)
         gain, bias = both(po, pp, 5), both(po, pp, 6)
         shares = [both(po, pp, i) for i in (7, 8)]
         flag = jnp.where(idx[1] > 0, 1.0, 0.0).astype(F32)
@@ -461,9 +580,11 @@
 
             def tile(i, last):
                 at = rows_at(r, i)
-                normed = hat[at, :] * gain + bias
+                n = hat[at, :]
+                hat_low[at, :] = n.astype(BF16)
+                normed = n * gain + bias
                 prev = shift_down(normed, last)
-                diff[at, :] = normed - prev
+                diff[at, :] = (normed - prev).astype(BF16)
                 for share, target in zip(shares, (ckey, cgate)):
                     target[at, :] = (normed * share + prev * (1.0 - share)).astype(BF16)
                 return normed[TB - 1 : TB, :]
@@ -475,46 +596,44 @@
             active[:, n : n + NB] = pre.astype(BF16)
             squared[:, n : n + NB] = (pre * pre).astype(BF16)
         opened[...] = jax.nn.sigmoid(dot(cgate[...], wh[:, FH:NF]))
+
+    channel_key, channel_gate, diff_two, hat_two, active, squared, filter_open = launch(
+        channel_forward,
+        "svvvv" + "h" * 5,
+        (idx, hat_two, hat_edge_two, params, params_other, *hidden_pieces),
+        [((T, WIDTH), BF16)] * 4 + [((T, FH), BF16)] * 2 + [((T, H), F32)],
+        [pltpu.VMEM((WIDTH, NF), BF16), pltpu.SemaphoreType.DMA((5,))],
+    )
+
+    def channel_return(idx, squared, r0, r1, r2, r3, r4, *rest):
+        parts, (wr, sems_r) = rest[:S], rest[S:]
+        copies_r = place_blocks(idx, [r0, r1, r2, r3, r4], wr, sems_r)
+        begin(copies_r)
         finish(copies_r)
         for p in range(S):
-            target = keep_own if p < S // 2 else send_other
-            at = (p % (S // 2)) * SR
-            target[:, at : at + SR] = dot(squared[...], wr[p])
-
-    channel_key, channel_gate, diff_two, active, squared, ret_keep, ret_send, filter_open = launch(
-        channel_forward,
-        "svvvv" + "h" * 10,
-        (idx, hat_two, hat_edge_two, params, params_other, *hidden_pieces, *return_pieces),
-        [
-            ((T, WIDTH), BF16),
-            ((T, WIDTH), BF16),
-            ((T, WIDTH), F32),
-            ((T, FH), BF16),
-            ((T, FH), BF16),
-            ((T, H), F32),
-            ((T, H), F32),
-            ((T, H), F32),
-        ],
-        [
-            pltpu.VMEM((WIDTH, NF), BF16),
-            pltpu.VMEM((S, FH, SR), BF16),
-            pltpu.SemaphoreType.DMA((5,)),
-            pltpu.SemaphoreType.DMA((5,)),
-        ],
-    )
-    ret_other = swap(ret_send, "tp", 1)
+            parts[p][...] = dot(squared[...], wr[p])
+
+    returned = launch(
+        channel_return,
+        "sv" + "h" * 5,
+        (idx, squared, *return_pieces),
+        [((T, SR), F32)] * S,
+        [pltpu.VMEM((S, FH, SR), BF16), pltpu.SemaphoreType.DMA((5,))],
+    )
+    ret_keep = returned[: S // 2]
+    ret_other = [swap(part, "tp", 1) for part in returned[S // 2 :]]
 
     def live_rows(idx, r, i):
         at = lax.broadcasted_iota(jnp.int32, (TB, 1), 0) + (idx[1] * L + i * TB)
         return jnp.where(at < idx[3 + r], 1.0, 0.0).astype(F32)
 
-    def close_block(idx, mine, theirs, opened, middle, up, out, grad_ret, grad_fil):
+    def close_block(idx, m0, m1, t0, t1, opened, middle, up, out, grad_ret, grad_fil):
         for r in range(R):
 
             def tile(i, carry):
                 at = rows_at(r, i)
                 live = live_rows(idx, r, i)
-                returned = mine[at, :] + theirs[at, :]
+                returned = columns((m0, m1), at) + columns((t0, t1), at)
                 s = opened[at, :]
                 out[at, :] = (live * (middle[at, :] + s * returned)).astype(BF16)
                 grad = live * up[at, :].astype(F32)
@@ -526,16 +645,200 @@
 
     block_out, grad_returned, grad_filter = launch(
         close_block,
-        "svvvvv",
-        (idx, ret_keep, ret_other, filter_open, middle, up_own),
-        [((T, H), BF16)] * 3,
+        "svvvvvvv",
+        (idx, *ret_keep, *ret_other, filter_open, middle, up_own),
+        [((T, H), BF16), ((T, H), BF16), ((T, H), BF16)],
     )
     grad_returned_other = swap(grad_returned, "tp", 1)
+
+    order = []
+    for spot in range(BLOCKS):
+        high, low = spot // C, spot % C
+        turned = 0
+        for bit in range(bits_of(C)):
+            turned = turned * 2 + ((low >> bit) & 1)
+        order.append(high * C + turned)
+
+    VR = 16
+
+    def weight_grads(lefts, rights, jobs, after=(), riders=()):
+        count_left = [len(group) for group in lefts]
+        flat = [ref for group in lefts for ref in group]
+        width = sum(job[3] for job in jobs if job[4] == 0)
+        half, quarter = WIDTH // 2, WIDTH // 4
+
+        def weight_products(idx, *refs):
+            left_refs, refs = list(refs[: len(flat)]), refs[len(flat) :]
+            right_refs, refs = refs[: len(rights)], refs[len(rights) :]
+            rider_refs, refs = refs[: len(riders)], refs[len(riders) :]
+            send_a, keep_a, send_b, keep_b, *mine, tall, turned = refs
+            if riders:
+                one, two, other, own = rider_refs
+                total = mine[0]
+                total[...] = jnp.zeros((VR, H), F32)
+                total[0:5, :] = one[:, :H] + other[0:5, :]
+                total[5:9, :] = two[:, :H] + other[5:9, :]
+                total[9:11, :] = own[...]
+                total[...] = write_pair(send_a, half, total[...])
+            for g, count in enumerate(count_left):
+                group, left_refs = left_refs[:count], left_refs[count:]
+                row = 0
+                for ref in group:
+                    for lane in range(0, ref.shape[1], 128):
+                        tall[row : row + 128, :] = ref[:, lane : lane + 128].astype(F32).T
+                        row += 128
+                for spot in range(BLOCKS):
+                    block = order[spot] ^ idx[2]
+                    turned[spot * BR : (spot + 1) * BR, :] = tall[
+                        pl.ds(pl.multiple_of(block * BR, BR), BR), :
+                    ].astype(BF16)
+                for left, right, start, size, part, at in jobs:
+                    if left != g:
+                        continue
+                    for n in range(0, size, 256):
+                        to = slice(at + n, at + n + 256)
+                        acc = dot(
+                            turned[...], right_refs[right][:, start + n : start + n + 256]
+                        ).astype(BF16)
+                        if part == 0:
+                            keep_a[:quarter, to] = acc[:quarter]
+                            send_a[:quarter, to] = acc[quarter:half]
+                            keep_a[quarter:, to] = acc[half : half + quarter]
+                            send_a[quarter:half, to] = acc[half + quarter :]
+                        else:
+                            keep_b[:, to] = acc[:half]
+                            send_b[:, to] = acc[half:]
+
+        extra = VR if riders else 0
+        return launch(
+            weight_products,
+            "s" + "v" * (len(flat) + len(rights) + len(riders)),
+            (idx, *flat, *rights, *riders),
+            [((half + extra, width), BF16)]
+            + [((half, width), BF16)] * 3
+            + ([((VR, H), F32)] if riders else []),
+            [pltpu.VMEM((WIDTH, T), F32), pltpu.VMEM((WIDTH, T), BF16)],
+            after=after,
+        )
+
+    def write_pair(ref, row, values):
+        high = values.astype(BF16)
+        low = (values - high.astype(F32)).astype(BF16)
+        ref[row:, :H] = high
+        ref[row:, H : 2 * H] = low
+        if ref.shape[1] > 2 * H:
+            ref[row:, 2 * H :] = jnp.zeros((VR, ref.shape[1] - 2 * H), BF16)
+        return high.astype(F32) + low.astype(F32)
+
+    def read_pair(ref, row):
+        return ref[row:, :H].astype(F32) + ref[row:, H : 2 * H].astype(F32)
+
+    def add(mine, theirs):
+        return mine.astype(F32) + theirs.astype(F32)
+
+    def square_start(send_a, keep_a, send_b, keep_b, *mine):
+        return [keep_a, swap(send_a, "shard", 1), keep_b, swap(send_b, "shard", 2), *mine]
+
+    def square_turn(state):
+        rows, width = state[0].shape
+        half = rows // 2
+        extra = VR if len(state) > 4 else 0
+
+        def turn_square(keep_a, got_a, keep_b, got_b, *refs):
+            if extra:
+                mine, refs = refs[0], refs[1:]
+            send_a, new_a, send_b, new_b, *total = refs
+            low, high = slice(0, half), slice(half, rows)
+            new_a[...] = add(keep_a[low, :], got_a[low, :]).astype(BF16)
+            send_a[:half, :] = add(keep_a[high, :], got_a[high, :]).astype(BF16)
+            new_b[...] = add(keep_b[low, :], got_b[low, :]).astype(BF16)
+            send_b[...] = add(keep_b[high, :], got_b[high, :]).astype(BF16)
+            if extra:
+                total[0][...] = write_pair(send_a, half, mine[...] + read_pair(got_a, rows))
+
+        return launch(
+            turn_square,
+            "v" * len(state),
+            state,
+            [((half + extra, width), BF16)]
+            + [((half, width), BF16)] * 3
+            + ([((VR, H), F32)] if extra else []),
+        )
+
+    def square_cross(send_a, keep_a, send_b, keep_b, *mine):
+        return [keep_a, swap(send_a, "shard", 2), keep_b, swap(send_b, "shard", 1), *mine]
+
+    def square_end(state):
+        rows, width = state[0].shape
+        half = rows // 2
+        extra = VR if len(state) > 4 else 0
+
+        def end_square(keep_a, got_a, keep_b, got_b, *refs):
+            if extra:
+                mine, refs = refs[0], refs[1:]
+            send, new, *total = refs
+            for part, (keep, got) in enumerate(((keep_a, got_a), (keep_b, got_b))):
+                at = slice(part * width, (part + 1) * width)
+                new[:, at] = add(keep[:half, :], got[:half, :]).astype(BF16)
+                send[:half, at] = add(keep[half:, :], got[half:rows, :]).astype(BF16)
+            if extra:
+                total[0][...] = write_pair(send, half, mine[...] + read_pair(got_a, rows))
+
+        return launch(
+            end_square,
+            "v" * len(state),
+            state,
+            [((half + extra, 2 * width), BF16), ((half, 2 * width), BF16)]
+            + ([((VR, H), F32)] if extra else []),
+        )
+
+    def scatter_line(send, keep, *mine, seen=None):
+        extra = VR if mine else 0
+        for bit in range(bits_of(C)):
+            got = swap(send, "ctx", 1 << bit)
+            if seen is not None:
+                seen.append(got)
+            rows, width = keep.shape
+            last = bit + 1 == bits_of(C)
+            half = rows if last else rows // 2
+
+            def turn_line(keep, got, *refs):
+                if extra:
+                    own, refs = refs[0], refs[1:]
+                new, *refs = refs
+                if last:
+                    new[...] = add(keep[...], got[:rows, :])
+                else:
+                    send = refs.pop(0)
+                    new[...] = add(keep[:half, :], got[:half, :]).astype(BF16)
+                    send[:half, :] = add(keep[half:, :], got[half:rows, :]).astype(BF16)
+                if extra:
+                    total = own[...] + read_pair(got, rows)
+                    refs[0][...] = total if last else write_pair(send, half, total)
+
+            outs = [((half, width), F32 if last else BF16)]
+            if not last:
+                outs.append(((half + extra, width), BF16))
+            if extra:
+                outs.append(((VR, H), F32))
+            result = launch(turn_line, "v" * (2 + len(mine)), (keep, got, *mine), outs)
+            keep, result = result[0], result[1:]
+            if not last:
+                send, result = result[0], result[1:]
+            mine = tuple(result)
+        return (keep, *mine)
+
+    return_parts = weight_grads(
+        [[grad_returned, grad_returned_other]],
+        [squared],
+        [(0, 0, 0, FH // 2, 0, 0), (0, 0, FH // 2, FH // 2, 1, 0)],
+    )
+    return_state = square_start(*return_parts)
 
     def channel_backward(
         idx, gro, grp, gf, active, diff, hat, edge, po, pp,
         h0, h1, h2, h3, h4, r0, r1, r2, r3, r4,
-        grad_hidden, grad_normed, first_out, sums, wh, wr, ckey, cgate, sems_h, sems_r,
+        grad_hidden, n0, n1, n2, n3, first_out, sums, wh, wr, ckey, cgate, sems_h, sems_r,
     ):
         copies_h = place_rows(idx, [h0, h1, h2, h3, h4], wh, sems_h)
         copies_r = place_blocks(idx, [r0, r1, r2, r3, r4], wr, sems_r)
@@ -567,14 +870,15 @@
             def tile(j, carry):
                 after, gain_sum, bias_sum, key_sum, gate_sum = carry
                 at = rows_at(r, NT - 1 - j)
-                gk, gg, d = ckey[at, :], cgate[at, :], diff[at, :]
+                gk, gg, d = ckey[at, :], cgate[at, :], diff[at, :].astype(F32)
                 now = gk * share_k + gg * share_g
                 back = gk * (1.0 - share_k) + gg * (1.0 - share_g)
                 grad = now + shift_up(back, after)
-                grad_normed[at, :] = grad
+                for p, part in enumerate((n0, n1, n2, n3)):
+                    part[at, :] = grad[:, p * SR : (p + 1) * SR]
                 return (
                     back[0:1, :],
-                    gain_sum + jnp.sum(grad * hat[at, :], axis=0, keepdims=True),
+                    gain_sum + jnp.sum(grad * hat[at, :].astype(F32), axis=0, keepdims=True),
                     bias_sum + jnp.sum(grad, axis=0, keepdims=True),
                     key_sum + jnp.sum(gk * d, axis=0, keepdims=True),
                     gate_sum + jnp.sum(gg * d, axis=0, keepdims=True),
@@ -587,7 +891,7 @@
         for i in range(4):
             sums[i : i + 1, :] = totals[i]
 
-    grad_hidden, grad_two, first_two, sums_two = launch(
+    grad_hidden, *grad_two, first_two, sums_two = launch(
         channel_backward,
         "s" + "v" * 9 + "h" * 10,
         (
@@ -604,7 +908,9 @@
             *hidden_pieces,
             *return_pieces,
         ),
-        [((T, FH), BF16), ((T, WIDTH), F32), ((R, WIDTH), F32), ((4, WIDTH), F32)],
+        [((T, FH), BF16)]
+        + [((T, SR), F32)] * S
+        + [((R, WIDTH), F32), ((4, WIDTH), F32)],
         [
             pltpu.VMEM((WIDTH, NF), BF16),
             pltpu.VMEM((S, FH, SR), BF16),
@@ -613,113 +919,54 @@
             pltpu.SemaphoreType.DMA((5,)),
             pltpu.SemaphoreType.DMA((5,)),
         ],
-    )
-    grad_two_other = swap(grad_two, "tp", 1)
+        after=(return_parts[0],),
+    )
+    grad_two, first_two, return_state = lax.optimization_barrier(
+        (grad_two, first_two, return_state)
+    )
+    grad_two_other = swap_parts(grad_two)
     first_two_own = along_ctx(first_two, -1, False)
     first_two_other = along_ctx(first_two, -1, True)
 
-    order = []
-    for spot in range(BLOCKS):
-        high, low = spot // C, spot % C
-        turned = 0
-        for bit in range(bits_of(C)):
-            turned = turned * 2 + ((low >> bit) & 1)
-        order.append(high * C + turned)
-
-    def weight_grads(lefts, rights, jobs):
-        count_left = [len(group) for group in lefts]
-        flat = [ref for group in lefts for ref in group]
-        width = sum(job[3] for job in jobs if job[4] == 0)
-
-        def weight_products(idx, *refs):
-            left_refs = list(refs[: len(flat)])
-            right_refs = refs[len(flat) : len(flat) + len(rights)]
-            send_a, keep_a, send_b, keep_b, tall, turned = refs[len(flat) + len(rights) :]
-            groups = []
-            for count in count_left:
-                groups.append(left_refs[:count])
-                left_refs = left_refs[count:]
-            half, quarter = WIDTH // 2, WIDTH // 4
-            for g, group in enumerate(groups):
-                row = 0
-                for ref in group:
-                    for lane in range(0, ref.shape[1], 128):
-                        tall[row : row + 128, :] = ref[:, lane : lane + 128].astype(F32).T
-                        row += 128
-                for spot in range(BLOCKS):
-                    block = order[spot] ^ idx[2]
-                    turned[spot * BR : (spot + 1) * BR, :] = tall[
-                        pl.ds(pl.multiple_of(block * BR, BR), BR), :
-                    ].astype(BF16)
-                for left, right, start, size, part, at in jobs:
-                    if left != g:
-                        continue
-                    for n in range(0, size, 256):
-                        to = slice(at + n, at + n + 256)
-                        acc = dot(
-                            turned[...], right_refs[right][:, start + n : start + n + 256]
-                        ).astype(BF16)
-                        if part == 0:
-                            keep_a[:quarter, to] = acc[:quarter]
-                            send_a[:quarter, to] = acc[quarter:half]
-                            keep_a[quarter:, to] = acc[half : half + quarter]
-                            send_a[quarter:, to] = acc[half + quarter :]
-                        else:
-                            keep_b[:, to] = acc[:half]
-                            send_b[:, to] = acc[half:]
-
-        return launch(
-            weight_products,
-            "s" + "v" * (len(flat) + len(rights)),
-            (idx, *flat, *rights),
-            [((WIDTH // 2, width), BF16)] * 4,
-            [pltpu.VMEM((WIDTH, T), F32), pltpu.VMEM((WIDTH, T), BF16)],
-        )
-
-    def add(mine, theirs):
-        return mine.astype(F32) + theirs.astype(F32)
-
-    def halves(values):
-        half = values.shape[0] // 2
-        return values[:half], values[half:]
-
-    def scatter(send_a, keep_a, send_b, keep_b):
-        got_a, got_b = swap(send_a, "shard", 1), swap(send_b, "shard", 2)
-        keep_a, send_a = halves(add(keep_a, got_a).astype(BF16))
-        keep_b, send_b = halves(add(keep_b, got_b).astype(BF16))
-        got_a, got_b = swap(send_a, "shard", 2), swap(send_b, "shard", 1)
-        joined = jnp.concatenate([add(keep_a, got_a), add(keep_b, got_b)], axis=1)
-        for bit in range(bits_of(C)):
-            mine, theirs = halves(joined.astype(BF16))
-            joined = add(mine, swap(theirs, "ctx", 1 << bit))
-        return joined
-
-    return_w = scatter(
-        *weight_grads(
-            [[grad_returned, grad_returned_other]],
-            [squared],
-            [(0, 0, 0, FH // 2, 0, 0), (0, 0, FH // 2, FH // 2, 1, 0)],
-        )
-    )
+    def sweep_again(*refs):
+        inputs, (gated, out, *saved, starts) = refs[:7], refs[7:]
+        sweep(*inputs, gated, out, starts, saved)
+
+    gated, mixed_out, part_old, part_new, keep, fresh, nums, dens, fade = launch(
+        sweep_again,
+        "v" * 7,
+        (key, value, opened, fading, bonus, states, hold(entering, grad_returned_other)),
+        [((T, H), BF16), ((G, T, 128), F32)]
+        + [((T, H), F32)] * 6
+        + [((G, R * CHUNKS, 128), F32)],
+        [pltpu.VMEM((G, 3 * R * CHUNKS, 128), F32)],
+    )
+
+    mixed_key, mixed_value, mixed_gate, hat_one, diff_one, root_one, _ = mixes(
+        *hold((x_own, x_other), grad_returned_other)
+    )
+
     part = NF // 2
-    hidden_w = scatter(
-        *weight_grads(
-            [[channel_key], [channel_gate]],
-            [grad_hidden, grad_filter],
-            [
-                (0, 0, 0, part, 0, 0),
-                (0, 0, part, FH - part, 1, 0),
-                (1, 1, 0, H, 1, FH - part),
-            ],
-        )
-    )
+    hidden_parts = weight_grads(
+        [[channel_key], [channel_gate]],
+        [grad_hidden, grad_filter],
+        [
+            (0, 0, 0, part, 0, 0),
+            (0, 0, part, FH - part, 1, 0),
+            (1, 1, 0, H, 1, FH - part),
+        ],
+        after=(gated, root_one),
+    )
+    hidden_state = square_start(*hidden_parts)
+    return_turn = square_turn(return_state)
+    return_cross = square_cross(*return_turn)
 
     def middle_backward(
-        idx, mine, theirs, e_own, e_other, hat, root, po, pp, uo, upp, opened, out,
+        idx, m0, m1, m2, m3, t0, t1, t2, t3, e_own, e_other, hat, root, po, pp, uo, upp, opened, out,
         part_old, keep, fade, p0, p1, p2, p3, p4,
         grad_mid, grad_own, grad_res, grad_gate, adjoint, entry, w, gates, sems,
     ):
-        copies = place_blocks(idx, [p0, p1, p2, p3, p4], w, sems)
+        copies = place_rows(idx, [p0, p1, p2, p3, p4], w, sems, 3 * H, 4 * H)
         begin(copies)
         gain = both(po, pp, 5)
         tail = e_own[...] + swapped(e_other[...])
@@ -729,8 +976,9 @@
             def tile(i, carry):
                 at = rows_at(r, i)
                 is_last = jnp.where((row == TB - 1) & (i == NT - 1), 1.0, 0.0).astype(F32)
-                grad = mine[at, :] + swapped(theirs[at, :]) + is_last * tail[r : r + 1, :]
-                n = hat[at, :]
+                grad = columns((m0, m1, m2, m3), at) + columns((t0, t1, t2, t3), at)
+                grad = grad + is_last * tail[r : r + 1, :]
+                n = hat[at, :].astype(F32)
                 scaled = grad * gain
                 mean_one = jnp.sum(scaled, axis=-1, keepdims=True) * (1.0 / WIDTH)
                 mean_two = jnp.sum(scaled * n, axis=-1, keepdims=True) * (1.0 / WIDTH)
@@ -742,11 +990,7 @@
 
             lax.fori_loop(0, NT, tile, 0)
         finish(copies)
-        acc = None
-        for p in range(S):
-            term = dot_t(grad_mid[:, p * SR : (p + 1) * SR], w[p])
-            acc = term if acc is None else acc + term
-        gates[...] = acc
+        gates[...] = dot(grad_mid[...], w[...])
         for r in range(R):
 
             def gate_tile(i, carry):
@@ -789,11 +1033,11 @@
 
     grad_mid, grad_mid_own, grad_res, grad_gate, adjoint, entry = launch(
         middle_backward,
-        "s" + "v" * 15 + "h" * 5,
+        "s" + "v" * 21 + "h" * 5,
         (
             idx,
-            grad_two,
-            grad_two_other,
+            *grad_two,
+            *grad_two_other,
             first_two_own,
             first_two_other,
             hat_two,
@@ -807,7 +1051,7 @@
             part_old,
             keep,
             fade,
-            *emit_pieces,
+            *time_pieces,
         ),
         [
             ((T, WIDTH), BF16),
@@ -818,46 +1062,38 @@
             ((3 * R, H), F32),
         ],
         [
-            pltpu.VMEM((S, H, SR), BF16),
+            pltpu.VMEM((WIDTH, H), BF16),
             pltpu.VMEM((T, H), F32),
             pltpu.SemaphoreType.DMA((5,)),
         ],
-    )
-
-    alpha, beta, span = entry.reshape(3, R, H)
-    late_alpha = late_beta = jnp.zeros((R, H), F32)
-    late_span = jnp.ones((R, H), F32)
-    for bit in range(bits_of(C)):
-        alpha_o, beta_o, span_o = swap(jnp.stack([alpha, beta, span]), "ctx", 1 << bit)
-        low = (c_at >> bit) & 1 == 0
-        late_alpha, late_beta, late_span = (
-            jnp.where(low, late_alpha + late_span * alpha_o, late_alpha),
-            jnp.where(low, late_beta + late_span * beta_o, late_beta),
-            jnp.where(low, late_span * span_o, late_span),
+        after=(hidden_parts[1],),
+    )
+
+    def no_adjoint():
+        zero = jnp.zeros((R, H), F32)
+        return (zero, zero, zero + 1.0)
+
+    def join_adjoints(idx, ld, bit, total, other, before):
+        low = (idx[1] >> bit) & 1 == 0
+
+        def follow(near, far):
+            return (near[0] + near[2] * far[0], near[1] + near[2] * far[1], near[2] * far[2])
+
+        as_near, as_far, with_other = follow(total, other), follow(other, total), follow(before, other)
+        return (
+            tuple(jnp.where(low, a, b) for a, b in zip(as_near, as_far)),
+            tuple(jnp.where(low, a, b) for a, b in zip(with_other, before)),
         )
-        if bit + 1 < bits_of(C):
-            alpha, beta, span = (
-                jnp.where(low, alpha + span * alpha_o, alpha_o + span_o * alpha),
-                jnp.where(low, beta + span * beta_o, beta_o + span_o * beta),
-                span * span_o,
-            )
-    late = jnp.concatenate([late_alpha, late_beta], axis=0)
-
-    early_w = scatter(
-        *weight_grads(
-            [[grad_mid], [mixed_gate]],
-            [gated, grad_gate],
-            [(0, 0, 0, H, 0, 0), (1, 1, 0, H, 1, 0)],
-        )
-    )
+
+    late = scan_rounds(entry, no_adjoint, join_adjoints)
 
     def time_backward(
         idx, res, out, value, part_old, part_new, keep, fresh, nums, dens, fade, adjoint, late,
         ld, gate, diff, hat, edge, po, pp, p0, p1, p2, p3, p4,
-        grad_key, grad_value, mine_own, send, first_out, sums, sums_own,
+        grad_key, grad_value, mine_own, s0, s1, stats, first_out, sums, sums_own,
         w, dk, dv, gk, gv, gg, starts, sems,
     ):
-        copies = place_rows(idx, [p0, p1, p2, p3, p4], w, sems)
+        copies = place_rows(idx, [p0, p1, p2, p3, p4], w, sems, 0, 3 * H)
         begin(copies)
         late_now = (late[pl.ds(0, R), :], late[pl.ds(R, R), :])
         for i in range(CHUNKS - 1, -1, -1):
@@ -911,7 +1147,7 @@
                 after, gain_sum, bias_sum, *mix_sums = carry
                 at = rows_at(r, NT - 1 - j)
                 grads = (gk[at, :], gv[at, :], gg[at, :])
-                d, n = diff[at, :], hat[at, :]
+                d, n = diff[at, :].astype(F32), hat[at, :].astype(F32)
                 now = back = None
                 for share, grad in zip(shares, grads):
                     a, b = grad * share, grad * (1.0 - share)
@@ -919,11 +1155,12 @@
                     back = b if back is None else back + b
                 grad = now + shift_up(back, after)
                 mine_own[at, :] = grad[:, :H]
-                send[at, :H] = grad[:, H:]
+                s0[at, :] = grad[:, H : H + SR]
+                s1[at, :] = grad[:, H + SR :]
                 scaled = grad * gain
                 one = jnp.sum(scaled, axis=-1, keepdims=True)
                 two = jnp.sum(scaled * n, axis=-1, keepdims=True)
-                send[at, H:] = jnp.where(lane == 0, one, jnp.where(lane == 1, two, 0.0))
+                stats[at, :] = jnp.where(lane == 0, one, jnp.where(lane == 1, two, 0.0))
                 return (
                     back[0:1, :],
                     gain_sum + jnp.sum(grad * n, axis=0, keepdims=True),
@@ -941,7 +1178,9 @@
         for i in range(5):
             sums[i : i + 1, :] = totals[i]
 
-    grad_key, grad_value, one_own, one_send, first_one, sums_one, sums_own = launch(
+    hidden_turn_out = square_turn(hidden_state)
+    hidden_cross = square_cross(*hidden_turn_out)
+    grad_key, grad_value, one_own, *one_send, first_one, sums_one, sums_own = launch(
         time_backward,
         "s" + "v" * 19 + "h" * 5,
         (
@@ -971,7 +1210,9 @@
             ((T, H), BF16),
             ((T, H), BF16),
             ((T, H), F32),
-            ((T, H + 128), F32),
+            ((T, SR), F32),
+            ((T, SR), F32),
+            ((T, 128), F32),
             ((R, WIDTH), F32),
             ((5, WIDTH), F32),
             ((2, H), F32),
@@ -980,28 +1221,34 @@
         + [pltpu.VMEM((G, T, 128), F32)] * 2
         + [pltpu.VMEM((T, WIDTH), F32)] * 3
         + [pltpu.VMEM((G, 2 * R * CHUNKS, 128), F32), pltpu.SemaphoreType.DMA((5,))],
-    )
-    one_other = swap(one_send, "tp", 1)
+        after=(hidden_turn_out[0], hidden_turn_out[2]),
+    )
+    one_other = [swap(part, "tp", 1) for part in one_send]
     first_one_own = along_ctx(first_one, -1, False)
     first_one_other = along_ctx(first_one, -1, True)
 
-    late_w = scatter(
-        *weight_grads(
-            [[mixed_key], [mixed_value]],
-            [grad_key, grad_value],
-            [(0, 0, 0, H, 0, 0), (1, 1, 0, H, 1, 0)],
-        )
-    )
-
-    wide = jnp.concatenate([sums_one, sums_two], axis=0)
-    own = wide[:, :H] + swap(wide[:, H:], "tp", 1)
-    vectors = jnp.concatenate([own, sums_own], axis=0)
-    for bit in range(bits_of(S)):
-        vectors = vectors + swap(vectors, "shard", 1 << bit)
-    for bit in range(bits_of(C)):
-        vectors = vectors + swap(vectors, "ctx", 1 << bit)
-
-    def input_backward(mine, sent, theirs, e_own, e_other, hat, root, po, pp, gm, out):
+    sums_other = swap(jnp.concatenate([sums_one[:, H:], sums_two[:, H:]], axis=0), "tp", 1)
+    late_parts = weight_grads(
+        [[grad_mid], [mixed_gate], [mixed_key], [mixed_value]],
+        [gated, grad_gate, grad_key, grad_value],
+        [(0, 0, 0, H, 0, 0), (1, 1, 0, H, 0, H), (2, 2, 0, H, 1, 0), (3, 3, 0, H, 1, H)],
+        after=(
+            return_cross[1],
+            return_cross[3],
+            first_one_own,
+            first_one_other,
+            *one_other,
+        ),
+        riders=(sums_one, sums_two, sums_other, sums_own),
+    )
+    late_state = square_start(*late_parts)
+
+    return_seen = []
+    (return_w,) = scatter_line(*square_end(hold(return_cross, first_one_other)), seen=return_seen)
+
+    def input_backward(
+        mine, sent, t0, t1, theirs, e_own, e_other, hat, root, po, pp, gm, out
+    ):
         gain_full = both(po, pp, 0)
         tail = e_own[...] + swapped(e_other[...])
         row = lax.broadcasted_iota(jnp.int32, (TB, 1), 0)
@@ -1009,19 +1256,21 @@
             weighted = tail[r : r + 1, :] * gain_full
             tail_one = jnp.sum(weighted, axis=-1, keepdims=True)
             tail_two = jnp.sum(
-                weighted * hat[(r + 1) * L - 1 : (r + 1) * L, :], axis=-1, keepdims=True
+                weighted * hat[(r + 1) * L - TB : (r + 1) * L, :].astype(F32)[TB - 1 :],
+                axis=-1,
+                keepdims=True,
             )
 
             def tile(i, carry):
                 at = rows_at(r, i)
                 is_last = jnp.where((row == TB - 1) & (i == NT - 1), 1.0, 0.0).astype(F32)
-                grad = mine[at, :] + theirs[at, :H] + is_last * tail[r : r + 1, :H]
-                stats = sent[at, H:] + theirs[at, H:]
+                grad = mine[at, :] + columns((t0, t1), at) + is_last * tail[r : r + 1, :H]
+                stats = sent[at, :] + theirs[at, :]
                 mean_one = (stats[:, 0:1] + is_last * tail_one) * (1.0 / WIDTH)
                 mean_two = (stats[:, 1:2] + is_last * tail_two) * (1.0 / WIDTH)
                 scaled = grad * gain_full[:, :H]
                 out[at, :] = gm[at, :] + root[at, :] * (
-                    scaled - mean_one - hat[at, :H] * mean_two
+                    scaled - mean_one - hat[at, :H].astype(F32) * mean_two
                 )
                 return carry
 
@@ -1029,11 +1278,11 @@
 
     (input_grad,) = launch(
         input_backward,
-        "v" * 10,
+        "v" * 12,
         (
             one_own,
-            one_send,
-            one_other,
+            one_send[2],
+            *one_other,
             first_one_own,
             first_one_other,
             hat_one,
@@ -1043,8 +1292,12 @@
             grad_mid_own,
         ),
         [((T, H), F32)],
-    )
-
+        after=(late_parts[1], return_seen[0]),
+    )
+    hidden_seen = []
+    (hidden_w,) = scatter_line(*square_end(hold(hidden_cross, late_parts[1])), seen=hidden_seen)
+    late_cross = square_cross(*square_turn(hold(late_state, hidden_seen[0], return_seen[-1])))
+    late_w, vectors = scatter_line(*square_end(hold(late_cross, input_grad)))
     shape = block_entries.shape
     return (
         block_out.reshape(shape),
@@ -1056,10 +1309,10 @@
         vectors[4],
         vectors[9],
         vectors[10],
-        early_w[:, H:],
-        late_w[:, :H],
-        late_w[:, H:],
-        early_w[:, :H].T,
+        late_w[:, H : 2 * H],
+        late_w[:, 2 * H : 3 * H],
+        late_w[:, 3 * H :],
+        late_w[:, :H].T,
         vectors[5],
         vectors[6],
         vectors[7],

time: 412 us -> 308 us (0.75)
  Pallas kernels: 125 us -> 87.4 us
  starting transfers between devices: 85 us -> 58.9 us
  other arithmetic: 20.6 us -> 0.1 us
  local copies, waits for them, and re-layouts: 24.2 us -> 9.57 us
  waiting for transfers between devices: 155 us -> 150 us
    pallas_call x15 -> x34, Pallas kernels: 125 us -> 87.4 us  [launch(): pl.pallas_call(run, out_shape=[jax.ShapeDtypeStruct(shape, dtype) for sha...]
    ppermute x57 -> x52, starting transfers between devices: 72.8 us -> 46.3 us  [swap(): return lax.ppermute(value, axis, [(i, i ^ step) for i in range(size)])]
    ppermute x57 -> x52, waiting for transfers between devices: 155 us -> 135 us  [swap(): return lax.ppermute(value, axis, [(i, i ^ step) for i in range(size)])]
    ppermute x4, waiting for transfers between devices: 0.01 us -> 9.31 us  [along_ctx(): return lax.ppermute(value, 'ctx', pairs)]
    convert_element_type x12 -> x0, other arithmetic: 8.83 us -> none  [the longest x4 5.04 us: scatter(): keep_a, send_a = halves(add(keep_a, got_a).astype(BF16))]
    slice x22 -> x10, local copies, waits for them, and re-layouts: 8.08 us -> 1.68 us  [the longest x2 1.45 us: per_device(): part.reshape(batches, rows_local, L, H)[:, :, L - 1, :].reshape(R, H)]
    another operation x14 -> x0, other arithmetic: 6.1 us -> none
    unnamed x136 -> x51, local copies, waits for them, and re-layouts: 10.5 us -> 4.92 us
  transfers between devices with their start and end apart: 64 -> 58, of which waited for: 23 -> 38; matrix products, arithmetic and copies ran while one was open for 8% -> 1% of each run, Pallas kernels for 23% -> 25%
where the time goes in v2:
time: 308 us; the launch traced here: 307 us
  waiting for transfers between devices  150 us (49%)
  Pallas kernels  87.4 us (28%)
  starting transfers between devices  58.9 us (19%)
  local copies, waits for them, and re-layouts  9.57 us (3%)
    ppermute x52, waiting for transfers between devices, swap(): return lax.ppermute(value, axis, [(i, i ^ step) for i in range(size)])  135 us
    pallas_call x34, Pallas kernels, launch(): pl.pallas_call(run, out_shape=[jax.ShapeDtypeStruct(shape, dtype) for sha...  87.4 us
    ppermute x52, starting transfers between devices, swap(): return lax.ppermute(value, axis, [(i, i ^ step) for i in range(size)])  46.3 us
    ppermute x4, starting transfers between devices, along_ctx(): return lax.ppermute(value, 'ctx', pairs)  9.97 us
    ppermute x4, waiting for transfers between devices, along_ctx(): return lax.ppermute(value, 'ctx', pairs)  9.31 us
  transfers between devices with their start and end apart: 58, of which 38 were waited for; matrix products, arithmetic and copies ran while one was open for 1% of the time, Pallas kernels for 25%

profile of v2, /device:TPU:0, one launch (start us, length us, event | category | flops | bytes accessed | tf_op | source)
XLA Modules:
  0.0 307.2 jit_solution(11326126095218093717)
XLA Ops:
  3.8 3.0 collective-permute-start.3
  11.4 3.5 %collective-permute-start.1 = (bf16[2,1024]{1,0:T(2,128)(2,1)S(1)}, bf16[2,1024]{1,0:T(2,128)(2,1)S(1)}, u32[]{:S(2)}, u32[]{:S(2)}) collective-permute-start(bf16[2,1024]{1,0:T(2,128)(2,1)S(1)} %pad_maximum_fusion.1), channel_id=1, source_target_pairs={{0,2},{2,4},{4,6},{1,3},{3,5},{5,7},{8,10},{10,12},{12,14},{9,11},... | collective-permute-start | bytes 12296 | tf_op jit(solution)/shard_map/ppermute | solution.py:90
  16.2 5.8 %mix_time.2 = (bf16[512,1024]{1,0:T(8,128)(2,1)S(1)}, bf16[512,1024]{1,0:T(8,128)(2,1)S(1)}, bf16[512,1024]{1,0:T(8,128)(2,1)S(1)}, bf16[512,1024]{1,0:T(8,128)(...) custom-call(s32[5]{0:T(128)S(1)} %pad_add_fusion.refs_0_, ...), custom_call_target="tpu_custom_call" | custom-call | tf_op jit(solution)/shard_map/mix_time/pallas_call | solution.py:37
  22.0 8.0 %collective-permute-done.3.refs_6_.refs_9_.refs_23_.refs_21_ = bf16[256,2048]{1,0:T(8,128)(2,1)S(1)} collective-permute-done((bf16[256,2048]{1,0:T(8,128)(2,1)S(1)}, bf16[256,2048]{1,0:T(8,128)(2,1)S(1)}, u32[]{:S(2)}, u32[]{:S(2)}) %collective-permute-start.3) | collective-permute-done | bytes 1048608 | tf_op jit(solution)/shard_map/ppermute | solution.py:83
  35.1 9.0 %collective-permute-done.5.refs_8_.refs_11_.refs_25_.refs_23_ = bf16[256,1024]{1,0:T(8,128)(2,1)S(1)} collective-permute-done((bf16[256,1024]{1,0:T(8,128)(2,1)S(1)}, bf16[256,1024]{1,0:T(8,128)(2,1)S(1)}, u32[]{:S(2)}, u32[]{:S(2)}) %collective-permute-start.5) | collective-permute-done | bytes 524320 | tf_op jit(solution)/shard_map/ppermute | solution.py:83
  51.4 5.1 %project_time.1 = (f32[4,512,128]{2,1,0:T(8,128)S(1)}, f32[4,512,128]{2,1,0:T(8,128)S(1)}, f32[512,512]{1,0:T(8,128)S(1)}, f32[4,48,128]{2,1,0:T(8,128)S(1)}, f32[6,512]{1,0:T(8,128)S(1)}) custom-call(s32[5]{0:T(128)S(1)} %pad_add_fusion.refs_0_, bf16[512,1024]{1,0:T(8,128)(2,1)S(1)} %get-tuple-element.170.refs_1_, ...), custom_call_target="tpu_custom_call" | custom-call | tf_op jit(solution)/shard_map/project_time/pallas_call | solution.py:37
  66.2 10.9 %collective-permute-done.10.refs_6_.refs_11_ = bf16[256,2560]{1,0:T(8,128)(2,1)S(1)} collective-permute-done((bf16[256,2560]{1,0:T(8,128)(2,1)S(1)}, bf16[256,2560]{1,0:T(8,128)(2,1)S(1)}, u32[]{:S(2)}, u32[]{:S(2)}) %collective-permute-start.10) | collective-permute-done | bytes 1310752 | tf_op jit(solution)/shard_map/ppermute | solution.py:83
  77.9 4.7 %sweep_time.1 = (f32[512,256]{1,0:T(8,128)S(1)}, f32[512,256]{1,0:T(8,128)S(1)}, f32[512,256]{1,0:T(8,128)S(1)}, f32[512,256]{1,0:T(8,128)S(1)}) custom-call(s32[5]{0:T(128)S(1)} %pad_add_fusion.refs_0_, f32[4,512,128]{2,1,0:T(8,128)S(1)} %get-tuple-element.176.refs_1_.refs_0_, f32[4,512,128]{2,1,0:T(8,128)S(1)} %get-tuple-element.177.refs_2_.refs_1_.refs_3_, ...), custom_call_target="tpu_custom_call" | custom-call | tf_op jit(solution)/shard_map/sweep_time/pallas_call | solution.py:37
  83.2 13.4 %collective-permute-done.16.refs_3_.refs_16_ = bf16[2048,256]{1,0:T(8,128)(2,1)S(1)} collective-permute-done((bf16[2048,256]{1,0:T(8,128)(2,1)S(1)}, bf16[2048,256]{1,0:T(8,128)(2,1)S(1)}, u32[]{:S(2)}, u32[]{:S(2)}) %collective-permute-start.16) | collective-permute-done | bytes 1048608 | tf_op jit(solution)/shard_map/ppermute | solution.py:83
  101.5 3.2 %middle_norm.1 = (f32[512,512]{1,0:T(8,128)S(1)}, f32[512,1024]{1,0:T(8,128)S(1)}, f32[512,1]{1,0:T(8,128)S(1)}, f32[2,1024]{1,0:T(2,128)S(1)}) custom-call(bf16[512,512]{1,0:T(8,128)(2,1)} %bitcast.4.refs_1_.refs_0_, bf16[512,512]{1,0:T(8,128)(2,1)} %collective-permute-done.refs_2_.refs_1_, f32[512,256]{1,0:T(8,128)S(1)} %get-tuple-element.186.refs_2_, ...), custom_call_target="tpu_custom_call" | custom-call | tf_op jit(solution)/shard_map/middle_norm/pallas_call | solution.py:37
  104.7 3.7 %collective-permute-start.18 = (f32[2,1024]{1,0:T(2,128)S(1)}, f32[2,1024]{1,0:T(2,128)S(1)}, u32[]{:S(2)}, u32[]{:S(2)}) collective-permute-start(f32[2,1024]{1,0:T(2,128)S(1)} %get-tuple-element.192), channel_id=1, source_target_pairs={{0,2},{2,4},{4,6},{1,3},{3,5},{5,7},{8,10},{10,12},{12,14},{9,11},... | collective-permute-start | bytes 24584 | tf_op jit(solution)/shard_map/ppermute | solution.py:90
  109.6 4.7 %collective-permute-done.19.refs_8_.refs_13_ = bf16[256,1280]{1,0:T(8,128)(2,1)S(1)} collective-permute-done((bf16[256,1280]{1,0:T(8,128)(2,1)S(1)}, bf16[256,1280]{1,0:T(8,128)(2,1)S(1)}, u32[]{:S(2)}, u32[]{:S(2)}) %collective-permute-start.19) | collective-permute-done | bytes 655392 | tf_op jit(solution)/shard_map/ppermute | solution.py:83
  115.3 5.0 %channel_forward.1 = (bf16[512,1024]{1,0:T(8,128)(2,1)S(1)}, bf16[512,1024]{1,0:T(8,128)(2,1)S(1)}, bf16[512,1024]{1,0:T(8,128)(2,1)S(1)}, bf16[512,1024]{1,0:T(...) custom-call(s32[5]{0:T(128)S(1)} %pad_add_fusion.refs_0_, ...), custom_call_target="tpu_custom_call" | custom-call | tf_op jit(solution)/shard_map/channel_forward/pallas_call | solution.py:37
  121.7 3.2 %channel_return.1 = (f32[512,256]{1,0:T(8,128)S(1)}, f32[512,256]{1,0:T(8,128)S(1)}, f32[512,256]{1,0:T(8,128)S(1)}, f32[512,256]{1,0:T(8,128)S(1)}) custom-call(s32[5]{0:T(128)S(1)} %pad_add_fusion.refs_0_, bf16[512,2048]{1,0:T(8,128)(2,1)S(1)} %get-tuple-element.193.refs_1_.refs_3_, bf16[2048,256]{1,0:T(8,128)(2,1)S(1)} %copy-done, ...), custom_call_target="tpu_custom_call" | custom-call | tf_op jit(solution)/shard_map/channel_return/pallas_call | solution.py:37
  131.6 4.2 %weight_products.3 = (bf16[512,1024]{1,0:T(8,128)(2,1)S(1)}, bf16[512,1024]{1,0:T(8,128)(2,1)S(1)}, bf16[512,1024]{1,0:T(8,128)(2,1)}, bf16[512,1024]{1,0:T(8,128)(2,1)S(1)}) custom-call(s32[5]{0:T(128)S(1)} %pad_add_fusion.refs_0_, bf16[512,512]{1,0:T(8,128)(2,1)S(1)} %get-tuple-element.201.refs_1_, bf16[512,512]{1,0:T(8,128)(2,1)S(1)} %collective-permute-done.25.refs_2_, ...), custom_call_target="tpu_custom_call" | custom-call | tf_op jit(solution)/shard_map/weight_products/pallas_call | solution.py:37
  137.6 3.1 sweep_again.1
  140.7 4.9 %mix_time.3 = (bf16[512,1024]{1,0:T(8,128)(2,1)S(1)}, bf16[512,1024]{1,0:T(8,128)(2,1)S(1)}, bf16[512,1024]{1,0:T(8,128)(2,1)S(1)}, bf16[512,1024]{1,0:T(8,128)(...) custom-call(s32[5]{0:T(128)S(1)} %pad_add_fusion.refs_0_, ...), custom_call_target="tpu_custom_call" | custom-call | tf_op jit(solution)/shard_map/mix_time/pallas_call | solution.py:37
  148.5 9.0 %channel_backward.1 = (bf16[512,2048]{1,0:T(8,128)(2,1)S(1)}, f32[512,256]{1,0:T(8,128)S(1)}, f32[512,256]{1,0:T(8,128)S(1)}, f32[512,256]{1,0:T(8,128)S(1)}, f3...) custom-call(s32[5]{0:T(128)S(1)} %pad_add_fusion.refs_0_, ...), custom_call_target="tpu_custom_call" | custom-call | tf_op jit(solution)/shard_map/channel_backward/pallas_call | solution.py:37
  157.6 3.8 %weight_products.4 = (bf16[512,1280]{1,0:T(8,128)(2,1)S(1)}, bf16[512,1280]{1,0:T(8,128)(2,1)S(1)}, bf16[512,1280]{1,0:T(8,128)(2,1)S(1)}, bf16[512,1280]{1,0:T(8,128)(2,1)S(1)}) custom-call(s32[5]{0:T(128)S(1)} %pad_add_fusion.refs_0_, bf16[512,1024]{1,0:T(8,128)(2,1)S(1)} %copy-done.3, bf16[512,1024]{1,0:T(8,128)(2,1)S(1)} %copy-done.5, ...), custom_call_target="tpu_custom_call" | custom-call | tf_op jit(solution)/shard_map/weight_products/pallas_call | solution.py:37
  166.2 2.9 collective-permute-done.32.refs_9_
  174.8 6.6 %middle_backward.1 = (bf16[512,1024]{1,0:T(8,128)(2,1)S(1)}, f32[512,512]{1,0:T(8,128)S(1)}, f32[4,512,128]{2,1,0:T(8,128)S(1)}, bf16[512,512]{1,0:T(8,128)(2,1)...) custom-call(s32[5]{0:T(128)S(1)} %pad_add_fusion.refs_0_, f32[512,256]{1,0:T(8,128)S(1)} %get-tuple-element.215.refs_1_, ...), custom_call_target="tpu_custom_call" | custom-call | tf_op jit(solution)/shard_map/middle_backward/pallas_call | solution.py:37
  188.7 4.4 %collective-permute-done.36.refs_1_ = bf16[512,1280]{1,0:T(8,128)(2,1)S(1)} collective-permute-done((bf16[512,1280]{1,0:T(8,128)(2,1)S(1)}, bf16[512,1280]{1,0:T(8,128)(2,1)S(1)}, u32[]{:S(2)}, u32[]{:S(2)}) %collective-permute-start.36) | collective-permute-done | bytes 1310752 | tf_op jit(solution)/shard_map/ppermute | solution.py:83
  195.3 10.7 %time_backward.1 = (bf16[512,512]{1,0:T(8,128)(2,1)S(1)}, bf16[512,512]{1,0:T(8,128)(2,1)S(1)}, f32[512,512]{1,0:T(8,128)S(1)}, f32[512,256]{1,0:T(8,128)S(1)}, ...) custom-call(s32[5]{0:T(128)S(1)} %pad_add_fusion.refs_0_, ...), custom_call_target="tpu_custom_call" | custom-call | tf_op jit(solution)/shard_map/time_backward/pallas_call | solution.py:37
  208.5 3.7 %collective-permute-done.42.refs_16_.refs_6_ = f32[2,1024]{1,0:T(2,128)S(1)} collective-permute-done((f32[2,1024]{1,0:T(2,128)S(1)}, f32[2,1024]{1,0:T(2,128)S(1)}, u32[]{:S(2)}, u32[]{:S(2)}) %collective-permute-start.42) | collective-permute-done | bytes 8224 | tf_op jit(solution)/shard_map/ppermute | solution.py:96
  213.7 4.0 %collective-permute-done.41.refs_15_.refs_5_ = f32[2,1024]{1,0:T(2,128)S(1)} collective-permute-done((f32[2,1024]{1,0:T(2,128)S(1)}, f32[2,1024]{1,0:T(2,128)S(1)}, u32[]{:S(2)}, u32[]{:S(2)}) %collective-permute-start.41) | collective-permute-done | bytes 8224 | tf_op jit(solution)/shard_map/ppermute | solution.py:90
  220.3 3.8 %weight_products.5 = (bf16[528,1024]{1,0:T(8,128)(2,1)S(1)}, bf16[512,1024]{1,0:T(8,128)(2,1)S(1)}, bf16[512,1024]{1,0:T(8,128)(2,1)S(1)}, bf16[512,1024]{1,0:T(8,128)(2,1)S(1)}, f32[16,512]{1,0:T(8,128)S(1)}) custom-call(s32[5]{0:T(128)S(1)} %pad_add_fusion.refs_0_, bf16[512,1024]{1,0:T(8,128)(2,1)S(1)} %get-tuple-element.257.refs_1_, ...), custom_call_target="tpu_custom_call" | custom-call | tf_op jit(solution)/shard_map/weight_products/pallas_call | solution.py:37
  227.2 8.1 %collective-permute-done.49.refs_1_ = bf16[256,1280]{1,0:T(8,128)(2,1)S(1)} collective-permute-done((bf16[256,1280]{1,0:T(8,128)(2,1)S(1)}, bf16[256,1280]{1,0:T(8,128)(2,1)S(1)}, u32[]{:S(2)}, u32[]{:S(2)}) %collective-permute-start.49) | collective-permute-done | bytes 655392 | tf_op jit(solution)/shard_map/ppermute | solution.py:83
  238.5 4.6 %collective-permute-done.46.refs_13_.refs_1_ = bf16[128,2048]{1,0:T(8,128)(2,1)S(1)} collective-permute-done((bf16[128,2048]{1,0:T(8,128)(2,1)S(1)}, bf16[128,2048]{1,0:T(8,128)(2,1)S(1)}, u32[]{:S(2)}, u32[]{:S(2)}) %collective-permute-start.46) | collective-permute-done | bytes 524320 | tf_op jit(solution)/shard_map/ppermute | solution.py:83
  243.2 12.8 %collective-permute-done.52.refs_1_ = bf16[64,2048]{1,0:T(8,128)(2,1)S(1)} collective-permute-done((bf16[64,2048]{1,0:T(8,128)(2,1)S(1)}, bf16[64,2048]{1,0:T(8,128)(2,1)S(1)}, u32[]{:S(2)}, u32[]{:S(2)}) %collective-permute-start.52) | collective-permute-done | bytes 262176 | tf_op jit(solution)/shard_map/ppermute | solution.py:83
  263.0 7.0 %collective-permute-done.54.refs_3_ = bf16[256,1024]{1,0:T(8,128)(2,1)S(1)} collective-permute-done((bf16[256,1024]{1,0:T(8,128)(2,1)S(1)}, bf16[256,1024]{1,0:T(8,128)(2,1)S(1)}, u32[]{:S(2)}, u32[]{:S(2)}) %collective-permute-start.54) | collective-permute-done | bytes 524320 | tf_op jit(solution)/shard_map/ppermute | solution.py:83
  273.7 16.0 %collective-permute-done.55.refs_1_ = bf16[144,2048]{1,0:T(8,128)(2,1)S(1)} collective-permute-done((bf16[144,2048]{1,0:T(8,128)(2,1)S(1)}, bf16[144,2048]{1,0:T(8,128)(2,1)S(1)}, u32[]{:S(2)}, u32[]{:S(2)}) %collective-permute-start.55) | collective-permute-done | bytes 589856 | tf_op jit(solution)/shard_map/ppermute | solution.py:83
  293.0 12.7 %collective-permute-done.56.refs_1_ = bf16[80,2048]{1,0:T(8,128)(2,1)S(1)} collective-permute-done((bf16[80,2048]{1,0:T(8,128)(2,1)S(1)}, bf16[80,2048]{1,0:T(8,128)(2,1)S(1)}, u32[]{:S(2)}, u32[]{:S(2)}) %collective-permute-start.56) | collective-permute-done | bytes 327712 | tf_op jit(solution)/shard_map/ppermute | solution.py:83
  (187 shorter events, 100.4 us)
Async XLA Ops:
  3.8 26.2 %collective-permute-start.3 = (bf16[256,2048]{1,0:T(8,128)(2,1)S(1)}, bf16[256,2048]{1,0:T(8,128)(2,1)S(1)}, u32[]{:S(2)}, u32[]{:S(2)}) collective-permute-start(bf16[256,2048]{1,0:T(8,128)(2,1)S(1)} %pack.2.refs_5_.refs_8_.refs_22_.refs_20_), channel_id=1, source_target_pairs={{0,8},{8,0},{16,24},{24,16},{1,9},{9,1},{17,25},{25,17},{2,10},{10... | collective-permute-start | bytes 3145736 | tf_op jit(solution)/shard_map/ppermute | solution.py:83
  6.8 24.6 %collective-permute-start.4 = (bf16[256,2048]{1,0:T(8,128)(2,1)S(1)}, bf16[256,2048]{1,0:T(8,128)(2,1)S(1)}, u32[]{:S(2)}, u32[]{:S(2)}) collective-permute-start(bf16[256,2048]{1,0:T(8,128)(2,1)S(1)} %pack.2.refs_5_.refs_8_.refs_22_.refs_20_), channel_id=1, source_target_pairs={{0,16},{8,24},{16,0},{24,8},{1,17},{9,25},{17,1},{25,9},{2,18},{10... | collective-permute-start | bytes 3145736 | tf_op jit(solution)/shard_map/ppermute | solution.py:83
  45.4 31.7 %collective-permute-start.10 = (bf16[256,2560]{1,0:T(8,128)(2,1)S(1)}, bf16[256,2560]{1,0:T(8,128)(2,1)S(1)}, u32[]{:S(2)}, u32[]{:S(2)}) collective-permute-start(bf16[256,2560]{1,0:T(8,128)(2,1)S(1)} %pack.3.refs_5_.refs_10_), channel_id=1, source_target_pairs={{0,8},{8,0},{16,24},{24,16},{1,9},{9,1},{17,25},{25,17},{2,10},{10... | collective-permute-start | bytes 3932168 | tf_op jit(solution)/shard_map/ppermute | solution.py:83
  46.0 31.7 %collective-permute-start.11 = (bf16[256,2560]{1,0:T(8,128)(2,1)S(1)}, bf16[256,2560]{1,0:T(8,128)(2,1)S(1)}, u32[]{:S(2)}, u32[]{:S(2)}) collective-permute-start(bf16[256,2560]{1,0:T(8,128)(2,1)S(1)} %pack.3.refs_5_.refs_10_), channel_id=1, source_target_pairs={{0,16},{8,24},{16,0},{24,8},{1,17},{9,25},{17,1},{25,9},{2,18},{10... | collective-permute-start | bytes 3932168 | tf_op jit(solution)/shard_map/ppermute | solution.py:83
  46.6 50.0 %collective-permute-start.16 = (bf16[2048,256]{1,0:T(8,128)(2,1)S(1)}, bf16[2048,256]{1,0:T(8,128)(2,1)S(1)}, u32[]{:S(2)}, u32[]{:S(2)}) collective-permute-start(bf16[2048,256]{1,0:T(8,128)(2,1)S(1)} %copy-done), channel_id=1, source_target_pairs={{0,8},{8,0},{16,24},{24,16},{1,9},{9,1},{17,25},{25,17},{2,10},{10... | collective-permute-start | bytes 3145736 | tf_op jit(solution)/shard_map/ppermute | solution.py:83
  48.0 49.6 %collective-permute-start.17 = (bf16[2048,256]{1,0:T(8,128)(2,1)S(1)}, bf16[2048,256]{1,0:T(8,128)(2,1)S(1)}, u32[]{:S(2)}, u32[]{:S(2)}) collective-permute-start(bf16[2048,256]{1,0:T(8,128)(2,1)S(1)} %copy-done), channel_id=1, source_target_pairs={{0,16},{8,24},{16,0},{24,8},{1,17},{9,25},{17,1},{25,9},{2,18},{10... | collective-permute-start | bytes 3145736 | tf_op jit(solution)/shard_map/ppermute | solution.py:83
  82.6 17.0 %collective-permute-start.12 = (f32[512,256]{1,0:T(8,128)S(1)}, f32[512,256]{1,0:T(8,128)S(1)}, u32[]{:S(2)}, u32[]{:S(2)}) collective-permute-start(f32[512,256]{1,0:T(8,128)S(1)} %get-tuple-element.188.refs_4_), channel_id=1, source_target_pairs={{0,1},{1,0},{2,3},{3,2},{4,5},{5,4},{6,7},{7,6},{8,9},{9,8},{10,11... | collective-permute-start | bytes 1572872 | tf_op jit(solution)/shard_map/ppermute | solution.py:83
  82.6 17.1 %collective-permute-start.13 = (f32[512,256]{1,0:T(8,128)S(1)}, f32[512,256]{1,0:T(8,128)S(1)}, u32[]{:S(2)}, u32[]{:S(2)}) collective-permute-start(f32[512,256]{1,0:T(8,128)S(1)} %get-tuple-element.189.refs_5_), channel_id=1, source_target_pairs={{0,1},{1,0},{2,3},{3,2},{4,5},{5,4},{6,7},{7,6},{8,9},{9,8},{10,11... | collective-permute-start | bytes 1572872 | tf_op jit(solution)/shard_map/ppermute | solution.py:83
  83.1 16.7 %collective-permute-start.14 = (f32[512,256]{1,0:T(8,128)S(1)}, f32[512,256]{1,0:T(8,128)S(1)}, u32[]{:S(2)}, u32[]{:S(2)}) collective-permute-start(f32[512,256]{1,0:T(8,128)S(1)} %get-tuple-element.186.refs_2_), channel_id=1, source_target_pairs={{0,1},{1,0},{2,3},{3,2},{4,5},{5,4},{6,7},{7,6},{8,9},{9,8},{10,11... | collective-permute-start | bytes 1572872 | tf_op jit(solution)/shard_map/ppermute | solution.py:83
  96.6 17.7 %collective-permute-start.19 = (bf16[256,1280]{1,0:T(8,128)(2,1)S(1)}, bf16[256,1280]{1,0:T(8,128)(2,1)S(1)}, u32[]{:S(2)}, u32[]{:S(2)}) collective-permute-start(bf16[256,1280]{1,0:T(8,128)(2,1)S(1)} %slice.85.refs_13_), channel_id=1, source_target_pairs={{0,16},{8,24},{16,0},{24,8},{1,17},{9,25},{17,1},{25,9},{2,18},{10... | collective-permute-start | bytes 1966088 | tf_op jit(solution)/shard_map/ppermute | solution.py:83
  97.6 17.7 %collective-permute-start.20 = (bf16[256,1280]{1,0:T(8,128)(2,1)S(1)}, bf16[256,1280]{1,0:T(8,128)(2,1)S(1)}, u32[]{:S(2)}, u32[]{:S(2)}) collective-permute-start(bf16[256,1280]{1,0:T(8,128)(2,1)S(1)} %slice.86.refs_14_), channel_id=1, source_target_pairs={{0,8},{8,0},{16,24},{24,16},{1,9},{9,1},{17,25},{25,17},{2,10},{10... | collective-permute-start | bytes 1966088 | tf_op jit(solution)/shard_map/ppermute | solution.py:83
  99.7 22.0 %collective-permute-start.21 = (bf16[1024,256]{1,0:T(8,128)(2,1)S(1)}, bf16[1024,256]{1,0:T(8,128)(2,1)S(1)}, u32[]{:S(2)}, u32[]{:S(2)}) collective-permute-start(bf16[1024,256]{1,0:T(8,128)(2,1)S(1)} %slice.109.refs_10_), channel_id=1, source_target_pairs={{0,16},{8,24},{16,0},{24,8},{1,17},{9,25},{17,1},{25,9},{2,18},{10... | collective-permute-start | bytes 1572872 | tf_op jit(solution)/shard_map/ppermute | solution.py:83
  99.8 21.9 %collective-permute-start.22 = (bf16[1024,256]{1,0:T(8,128)(2,1)S(1)}, bf16[1024,256]{1,0:T(8,128)(2,1)S(1)}, u32[]{:S(2)}, u32[]{:S(2)}) collective-permute-start(bf16[1024,256]{1,0:T(8,128)(2,1)S(1)} %slice.110.refs_11_), channel_id=1, source_target_pairs={{0,8},{8,0},{16,24},{24,16},{1,9},{9,1},{17,25},{25,17},{2,10},{10... | collective-permute-start | bytes 1572872 | tf_op jit(solution)/shard_map/ppermute | solution.py:83
  135.8 27.8 %collective-permute-start.26 = (bf16[512,1024]{1,0:T(8,128)(2,1)S(1)}, bf16[512,1024]{1,0:T(8,128)(2,1)S(1)}, u32[]{:S(2)}, u32[]{:S(2)}) collective-permute-start(bf16[512,1024]{1,0:T(8,128)(2,1)S(1)} %get-tuple-element.206.refs_20_), channel_id=1, source_target_pairs={{0,8},{8,0},{16,24},{24,16},{1,9},{9,1},{17,25},{25,17},{2,10},{10... | collective-permute-start | bytes 3145736 | tf_op jit(solution)/shard_map/ppermute | solution.py:83
  137.1 26.5 %collective-permute-start.27 = (bf16[512,1024]{1,0:T(8,128)(2,1)}, bf16[512,1024]{1,0:T(8,128)(2,1)}, u32[]{:S(2)}, u32[]{:S(2)}) collective-permute-start(bf16[512,1024]{1,0:T(8,128)(2,1)} %get-tuple-element.214), channel_id=1, source_target_pairs={{0,16},{8,24},{16,0},{24,8},{1,17},{9,25},{17,1},{25,9},{2,18},{10... | collective-permute-start | bytes 3145736 | tf_op jit(solution)/shard_map/ppermute | solution.py:83
  161.3 31.8 %collective-permute-start.36 = (bf16[512,1280]{1,0:T(8,128)(2,1)S(1)}, bf16[512,1280]{1,0:T(8,128)(2,1)S(1)}, u32[]{:S(2)}, u32[]{:S(2)}) collective-permute-start(bf16[512,1280]{1,0:T(8,128)(2,1)S(1)} %get-tuple-element.246), channel_id=1, source_target_pairs={{0,8},{8,0},{16,24},{24,16},{1,9},{9,1},{17,25},{25,17},{2,10},{10... | collective-permute-start | bytes 3932168 | tf_op jit(solution)/shard_map/ppermute | solution.py:83
  162.4 31.7 %collective-permute-start.37 = (bf16[512,1280]{1,0:T(8,128)(2,1)S(1)}, bf16[512,1280]{1,0:T(8,128)(2,1)S(1)}, u32[]{:S(2)}, u32[]{:S(2)}) collective-permute-start(bf16[512,1280]{1,0:T(8,128)(2,1)S(1)} %get-tuple-element.248), channel_id=1, source_target_pairs={{0,16},{8,24},{16,0},{24,8},{1,17},{9,25},{17,1},{25,9},{2,18},{10... | collective-permute-start | bytes 3932168 | tf_op jit(solution)/shard_map/ppermute | solution.py:83
  172.9 33.8 %collective-permute-start.44 = (bf16[256,1024]{1,0:T(8,128)(2,1)S(1)}, bf16[256,1024]{1,0:T(8,128)(2,1)S(1)}, u32[]{:S(2)}, u32[]{:S(2)}) collective-permute-start(bf16[256,1024]{1,0:T(8,128)(2,1)S(1)} %get-tuple-element.270), channel_id=1, source_target_pairs={{0,16},{8,24},{16,0},{24,8},{1,17},{9,25},{17,1},{25,9},{2,18},{10... | collective-permute-start | bytes 1572872 | tf_op jit(solution)/shard_map/ppermute | solution.py:83
  173.8 33.4 %collective-permute-start.45 = (bf16[256,1024]{1,0:T(8,128)(2,1)S(1)}, bf16[256,1024]{1,0:T(8,128)(2,1)S(1)}, u32[]{:S(2)}, u32[]{:S(2)}) collective-permute-start(bf16[256,1024]{1,0:T(8,128)(2,1)S(1)} %get-tuple-element.271), channel_id=1, source_target_pairs={{0,8},{8,0},{16,24},{24,16},{1,9},{9,1},{17,25},{25,17},{2,10},{10... | collective-permute-start | bytes 1572872 | tf_op jit(solution)/shard_map/ppermute | solution.py:83
  206.0 14.2 %collective-permute-start.38 = (f32[512,256]{1,0:T(8,128)S(1)}, f32[512,256]{1,0:T(8,128)S(1)}, u32[]{:S(2)}, u32[]{:S(2)}) collective-permute-start(f32[512,256]{1,0:T(8,128)S(1)} %get-tuple-element.253), channel_id=1, source_target_pairs={{0,1},{1,0},{2,3},{3,2},{4,5},{5,4},{6,7},{7,6},{8,9},{9,8},{10,11... | collective-permute-start | bytes 1572872 | tf_op jit(solution)/shard_map/ppermute | solution.py:83
  206.1 14.2 %collective-permute-start.39 = (f32[512,256]{1,0:T(8,128)S(1)}, f32[512,256]{1,0:T(8,128)S(1)}, u32[]{:S(2)}, u32[]{:S(2)}) collective-permute-start(f32[512,256]{1,0:T(8,128)S(1)} %get-tuple-element.254), channel_id=1, source_target_pairs={{0,1},{1,0},{2,3},{3,2},{4,5},{5,4},{6,7},{7,6},{8,9},{9,8},{10,11... | collective-permute-start | bytes 1572872 | tf_op jit(solution)/shard_map/ppermute | solution.py:83
  206.6 13.7 %collective-permute-start.40 = (f32[512,128]{1,0:T(8,128)S(1)}, f32[512,128]{1,0:T(8,128)S(1)}, u32[]{:S(2)}, u32[]{:S(2)}) collective-permute-start(f32[512,128]{1,0:T(8,128)S(1)} %get-tuple-element.252.refs_1_), channel_id=1, source_target_pairs={{0,1},{1,0},{2,3},{3,2},{4,5},{5,4},{6,7},{7,6},{8,9},{9,8},{10,11... | collective-permute-start | bytes 786440 | tf_op jit(solution)/shard_map/ppermute | solution.py:83
  217.7 17.7 %collective-permute-start.49 = (bf16[256,1280]{1,0:T(8,128)(2,1)S(1)}, bf16[256,1280]{1,0:T(8,128)(2,1)S(1)}, u32[]{:S(2)}, u32[]{:S(2)}) collective-permute-start(bf16[256,1280]{1,0:T(8,128)(2,1)S(1)} %get-tuple-element.249.refs_25_), channel_id=1, source_target_pairs={{0,16},{8,24},{16,0},{24,8},{1,17},{9,25},{17,1},{25,9},{2,18},{10... | collective-permute-start | bytes 1966088 | tf_op jit(solution)/shard_map/ppermute | solution.py:83
  218.9 17.7 %collective-permute-start.50 = (bf16[256,1280]{1,0:T(8,128)(2,1)S(1)}, bf16[256,1280]{1,0:T(8,128)(2,1)S(1)}, u32[]{:S(2)}, u32[]{:S(2)}) collective-permute-start(bf16[256,1280]{1,0:T(8,128)(2,1)S(1)} %get-tuple-element.250.refs_26_), channel_id=1, source_target_pairs={{0,8},{8,0},{16,24},{24,16},{1,9},{9,1},{17,25},{25,17},{2,10},{10... | collective-permute-start | bytes 1966088 | tf_op jit(solution)/shard_map/ppermute | solution.py:83
  224.1 33.3 %collective-permute-start.47 = (bf16[528,1024]{1,0:T(8,128)(2,1)S(1)}, bf16[528,1024]{1,0:T(8,128)(2,1)S(1)}, u32[]{:S(2)}, u32[]{:S(2)}) collective-permute-start(bf16[528,1024]{1,0:T(8,128)(2,1)S(1)} %get-tuple-element.280), channel_id=1, source_target_pairs={{0,8},{8,0},{16,24},{24,16},{1,9},{9,1},{17,25},{25,17},{2,10},{10... | collective-permute-start | bytes 3244040 | tf_op jit(solution)/shard_map/ppermute | solution.py:83
  224.8 32.5 %collective-permute-start.48 = (bf16[512,1024]{1,0:T(8,128)(2,1)S(1)}, bf16[512,1024]{1,0:T(8,128)(2,1)S(1)}, u32[]{:S(2)}, u32[]{:S(2)}) collective-permute-start(bf16[512,1024]{1,0:T(8,128)(2,1)S(1)} %get-tuple-element.282), channel_id=1, source_target_pairs={{0,16},{8,24},{16,0},{24,8},{1,17},{9,25},{17,1},{25,9},{2,18},{10... | collective-permute-start | bytes 3145736 | tf_op jit(solution)/shard_map/ppermute | solution.py:83
  225.9 17.2 %collective-permute-start.46 = (bf16[128,2048]{1,0:T(8,128)(2,1)S(1)}, bf16[128,2048]{1,0:T(8,128)(2,1)S(1)}, u32[]{:S(2)}, u32[]{:S(2)}) collective-permute-start(bf16[128,2048]{1,0:T(8,128)(2,1)S(1)} %get-tuple-element.279), channel_id=1, source_target_pairs={{0,2},{2,0},{4,6},{6,4},{1,3},{3,1},{5,7},{7,5},{8,10},{10,8},{12,... | collective-permute-start | bytes 1572872 | tf_op jit(solution)/shard_map/ppermute | solution.py:83
  236.8 20.4 %collective-permute-start.51 = (bf16[128,2560]{1,0:T(8,128)(2,1)S(1)}, bf16[128,2560]{1,0:T(8,128)(2,1)S(1)}, u32[]{:S(2)}, u32[]{:S(2)}) collective-permute-start(bf16[128,2560]{1,0:T(8,128)(2,1)S(1)} %get-tuple-element.290), channel_id=1, source_target_pairs={{0,2},{2,0},{4,6},{6,4},{1,3},{3,1},{5,7},{7,5},{8,10},{10,8},{12,... | collective-permute-start | bytes 1966088 | tf_op jit(solution)/shard_map/ppermute | solution.py:83
  243.2 12.9 %collective-permute-start.52 = (bf16[64,2048]{1,0:T(8,128)(2,1)S(1)}, bf16[64,2048]{1,0:T(8,128)(2,1)S(1)}, u32[]{:S(2)}, u32[]{:S(2)}) collective-permute-start(bf16[64,2048]{1,0:T(8,128)(2,1)S(1)} %get-tuple-element.292), channel_id=1, source_target_pairs={{0,4},{2,6},{4,0},{6,2},{1,5},{3,7},{5,1},{7,3},{8,12},{10,14},{12... | collective-permute-start | bytes 786440 | tf_op jit(solution)/shard_map/ppermute | solution.py:83
  270.5 19.2 %collective-permute-start.55 = (bf16[144,2048]{1,0:T(8,128)(2,1)S(1)}, bf16[144,2048]{1,0:T(8,128)(2,1)S(1)}, u32[]{:S(2)}, u32[]{:S(2)}) collective-permute-start(bf16[144,2048]{1,0:T(8,128)(2,1)S(1)} %get-tuple-element.309), channel_id=1, source_target_pairs={{0,2},{2,0},{4,6},{6,4},{1,3},{3,1},{5,7},{7,5},{8,10},{10,8},{12,... | collective-permute-start | bytes 1769480 | tf_op jit(solution)/shard_map/ppermute | solution.py:83
  272.3 19.1 %collective-permute-start.57 = (bf16[64,2560]{1,0:T(8,128)(2,1)S(1)}, bf16[64,2560]{1,0:T(8,128)(2,1)S(1)}, u32[]{:S(2)}, u32[]{:S(2)}) collective-permute-start(bf16[64,2560]{1,0:T(8,128)(2,1)S(1)} %get-tuple-element.318), channel_id=1, source_target_pairs={{0,4},{2,6},{4,0},{6,2},{1,5},{3,7},{5,1},{7,3},{8,12},{10,14},{12... | collective-permute-start | bytes 983048 | tf_op jit(solution)/shard_map/ppermute | solution.py:83
  289.8 15.9 %collective-permute-start.56 = (bf16[80,2048]{1,0:T(8,128)(2,1)S(1)}, bf16[80,2048]{1,0:T(8,128)(2,1)S(1)}, u32[]{:S(2)}, u32[]{:S(2)}) collective-permute-start(bf16[80,2048]{1,0:T(8,128)(2,1)S(1)} %get-tuple-element.312), channel_id=1, source_target_pairs={{0,4},{2,6},{4,0},{6,2},{1,5},{3,7},{5,1},{7,3},{8,12},{10,14},{12... | collective-permute-start | bytes 983048 | tf_op jit(solution)/shard_map/ppermute | solution.py:83
  (50 other events, 398.5 us)

commit v3 on v2

--- a/solution.py
+++ b/solution.py
@@ -709,7 +709,7 @@
                             keep_b[:, to] = acc[:half]
                             send_b[:, to] = acc[half:]
 
-        extra = VR if riders else 0
+        extra = 2 * VR if riders else 0
         return launch(
             weight_products,
             "s" + "v" * (len(flat) + len(rights) + len(riders)),
@@ -724,14 +724,14 @@
     def write_pair(ref, row, values):
         high = values.astype(BF16)
         low = (values - high.astype(F32)).astype(BF16)
-        ref[row:, :H] = high
-        ref[row:, H : 2 * H] = low
-        if ref.shape[1] > 2 * H:
-            ref[row:, 2 * H :] = jnp.zeros((VR, ref.shape[1] - 2 * H), BF16)
+        ref[row : row + VR, :H] = high
+        ref[row + VR :, :H] = low
+        if ref.shape[1] > H:
+            ref[row:, H:] = jnp.zeros((2 * VR, ref.shape[1] - H), BF16)
         return high.astype(F32) + low.astype(F32)
 
     def read_pair(ref, row):
-        return ref[row:, :H].astype(F32) + ref[row:, H : 2 * H].astype(F32)
+        return ref[row : row + VR, :H].astype(F32) + ref[row + VR :, :H].astype(F32)
 
     def add(mine, theirs):
         return mine.astype(F32) + theirs.astype(F32)
@@ -742,7 +742,7 @@
     def square_turn(state):
         rows, width = state[0].shape
         half = rows // 2
-        extra = VR if len(state) > 4 else 0
+        extra = 2 * VR if len(state) > 4 else 0
 
         def turn_square(keep_a, got_a, keep_b, got_b, *refs):
             if extra:
@@ -771,7 +771,7 @@
     def square_end(state):
         rows, width = state[0].shape
         half = rows // 2
-        extra = VR if len(state) > 4 else 0
+        extra = 2 * VR if len(state) > 4 else 0
 
         def end_square(keep_a, got_a, keep_b, got_b, *refs):
             if extra:
@@ -792,8 +792,8 @@
             + ([((VR, H), F32)] if extra else []),
         )
 
-    def scatter_line(send, keep, *mine, seen=None):
-        extra = VR if mine else 0
+    def scatter_line(send, keep, *mine, widths, seen=None):
+        extra = 2 * VR if mine else 0
         for bit in range(bits_of(C)):
             got = swap(send, "ctx", 1 << bit)
             if seen is not None:
@@ -805,28 +805,30 @@
             def turn_line(keep, got, *refs):
                 if extra:
                     own, refs = refs[0], refs[1:]
-                new, *refs = refs
                 if last:
-                    new[...] = add(keep[...], got[:rows, :])
+                    news, refs = refs[: len(widths)], refs[len(widths) :]
+                    at = 0
+                    for new, size in zip(news, widths):
+                        new[...] = add(keep[:, at : at + size], got[:rows, at : at + size])
+                        at += size
                 else:
-                    send = refs.pop(0)
+                    new, send, *refs = refs
                     new[...] = add(keep[:half, :], got[:half, :]).astype(BF16)
                     send[:half, :] = add(keep[half:, :], got[half:rows, :]).astype(BF16)
                 if extra:
                     total = own[...] + read_pair(got, rows)
                     refs[0][...] = total if last else write_pair(send, half, total)
 
-            outs = [((half, width), F32 if last else BF16)]
-            if not last:
-                outs.append(((half + extra, width), BF16))
+            if last:
+                outs = [((rows, size), F32) for size in widths]
+            else:
+                outs = [((half, width), BF16), ((half + extra, width), BF16)]
             if extra:
                 outs.append(((VR, H), F32))
             result = launch(turn_line, "v" * (2 + len(mine)), (keep, got, *mine), outs)
-            keep, result = result[0], result[1:]
             if not last:
-                send, result = result[0], result[1:]
-            mine = tuple(result)
-        return (keep, *mine)
+                keep, send, *mine = result
+        return result
 
     return_parts = weight_grads(
         [[grad_returned, grad_returned_other]],
@@ -1087,6 +1089,13 @@
 
     late = scan_rounds(entry, no_adjoint, join_adjoints)
 
+    early_parts = weight_grads(
+        [[grad_mid], [mixed_gate]],
+        [gated, grad_gate],
+        [(0, 0, 0, H, 0, 0), (1, 1, 0, H, 1, 0)],
+    )
+    early_state = square_start(*early_parts)
+
     def time_backward(
         idx, res, out, value, part_old, part_new, keep, fresh, nums, dens, fade, adjoint, late,
         ld, gate, diff, hat, edge, po, pp, p0, p1, p2, p3, p4,
@@ -1178,7 +1187,7 @@
         for i in range(5):
             sums[i : i + 1, :] = totals[i]
 
-    hidden_turn_out = square_turn(hidden_state)
+    hidden_turn_out = square_turn(hold(hidden_state, late))
     hidden_cross = square_cross(*hidden_turn_out)
     grad_key, grad_value, one_own, *one_send, first_one, sums_one, sums_own = launch(
         time_backward,
@@ -1221,7 +1230,7 @@
         + [pltpu.VMEM((G, T, 128), F32)] * 2
         + [pltpu.VMEM((T, WIDTH), F32)] * 3
         + [pltpu.VMEM((G, 2 * R * CHUNKS, 128), F32), pltpu.SemaphoreType.DMA((5,))],
-        after=(hidden_turn_out[0], hidden_turn_out[2]),
+        after=(hidden_turn_out[0], hidden_turn_out[2], early_parts[1]),
     )
     one_other = [swap(part, "tp", 1) for part in one_send]
     first_one_own = along_ctx(first_one, -1, False)
@@ -1229,22 +1238,18 @@
 
     sums_other = swap(jnp.concatenate([sums_one[:, H:], sums_two[:, H:]], axis=0), "tp", 1)
     late_parts = weight_grads(
-        [[grad_mid], [mixed_gate], [mixed_key], [mixed_value]],
-        [gated, grad_gate, grad_key, grad_value],
-        [(0, 0, 0, H, 0, 0), (1, 1, 0, H, 0, H), (2, 2, 0, H, 1, 0), (3, 3, 0, H, 1, H)],
-        after=(
-            return_cross[1],
-            return_cross[3],
-            first_one_own,
-            first_one_other,
-            *one_other,
-        ),
+        [[mixed_key], [mixed_value]],
+        [grad_key, grad_value],
+        [(0, 0, 0, H, 0, 0), (1, 1, 0, H, 1, 0)],
+        after=(return_cross[1], return_cross[3], hidden_cross[1], hidden_cross[3]),
         riders=(sums_one, sums_two, sums_other, sums_own),
     )
     late_state = square_start(*late_parts)
 
     return_seen = []
-    (return_w,) = scatter_line(*square_end(hold(return_cross, first_one_other)), seen=return_seen)
+    (return_w,) = scatter_line(
+        *square_end(hold(return_cross, first_one_own, first_one_other)), widths=[FH], seen=return_seen
+    )
 
     def input_backward(
         mine, sent, t0, t1, theirs, e_own, e_other, hat, root, po, pp, gm, out
@@ -1295,9 +1300,13 @@
         after=(late_parts[1], return_seen[0]),
     )
     hidden_seen = []
-    (hidden_w,) = scatter_line(*square_end(hold(hidden_cross, late_parts[1])), seen=hidden_seen)
-    late_cross = square_cross(*square_turn(hold(late_state, hidden_seen[0], return_seen[-1])))
-    late_w, vectors = scatter_line(*square_end(hold(late_cross, input_grad)))
+    hidden_w, filter_w = scatter_line(
+        *square_end(hold(hidden_cross, late_parts[1])), widths=[FH, H], seen=hidden_seen
+    )
+    early_cross = square_cross(*square_turn(hold(early_state, hidden_seen[0], return_seen[-1])))
+    late_cross = square_cross(*square_turn(late_state))
+    output_w, gate_w = scatter_line(*square_end(hold(early_cross, input_grad)), widths=[H, H])
+    key_w, value_w, vectors = scatter_line(*square_end(late_cross), widths=[H, H])
     shape = block_entries.shape
     return (
         block_out.reshape(shape),
@@ -1309,16 +1318,16 @@
         vectors[4],
         vectors[9],
         vectors[10],
-        late_w[:, H : 2 * H],
-        late_w[:, 2 * H : 3 * H],
-        late_w[:, 3 * H :],
-        late_w[:, :H].T,
+        gate_w,
+        key_w,
+        value_w,
+        output_w.T,
         vectors[5],
         vectors[6],
         vectors[7],
         vectors[8],
-        hidden_w[:, :FH],
-        hidden_w[:, FH:],
+        hidden_w,
+        filter_w,
         return_w.T,
     )
 

time: 308 us -> 300 us (0.974)
  waiting for transfers between devices: 150 us -> 136 us
  starting transfers between devices: 58.9 us -> 65.3 us
    ppermute x52 -> x58, waiting for transfers between devices: 135 us -> 125 us  [swap(): return lax.ppermute(value, axis, [(i, i ^ step) for i in range(size)])]
    ppermute x52 -> x58, starting transfers between devices: 46.3 us -> 52.7 us  [swap(): return lax.ppermute(value, axis, [(i, i ^ step) for i in range(size)])]
    pallas_call x34 -> x39, Pallas kernels: 87.4 us -> 89.4 us  [launch(): pl.pallas_call(run, out_shape=[jax.ShapeDtypeStruct(shape, dtype) for sha...]
  transfers between devices with their start and end apart: 58 -> 64, of which waited for: 38 -> 42; matrix products, arithmetic and copies ran while one was open for 1% -> 1% of each run, Pallas kernels for 25% -> 26%
where the time goes in v3:
time: 300 us; the launch traced here: 299 us
  waiting for transfers between devices  136 us (45%)
  Pallas kernels  89.4 us (30%)
  starting transfers between devices  65.3 us (22%)
  local copies, waits for them, and re-layouts  7.5 us (2%)
    ppermute x58, waiting for transfers between devices, swap(): return lax.ppermute(value, axis, [(i, i ^ step) for i in range(size)])  125 us
    pallas_call x39, Pallas kernels, launch(): pl.pallas_call(run, out_shape=[jax.ShapeDtypeStruct(shape, dtype) for sha...  89.4 us
    ppermute x58, starting transfers between devices, swap(): return lax.ppermute(value, axis, [(i, i ^ step) for i in range(size)])  52.7 us
    ppermute x4, starting transfers between devices, along_ctx(): return lax.ppermute(value, 'ctx', pairs)  9.73 us
    ppermute x4, waiting for transfers between devices, along_ctx(): return lax.ppermute(value, 'ctx', pairs)  7.99 us
  transfers between devices with their start and end apart: 64, of which 42 were waited for; matrix products, arithmetic and copies ran while one was open for 1% of the time, Pallas kernels for 26%

profile of v3, /device:TPU:0, one launch (start us, length us, event | category | flops | bytes accessed | tf_op | source)
XLA Modules:
  0.0 299.3 jit_solution(2754247955714628914)
XLA Ops:
  3.8 3.0 %collective-permute-start.3 = (bf16[256,2048]{1,0:T(8,128)(2,1)S(1)}, bf16[256,2048]{1,0:T(8,128)(2,1)S(1)}, u32[]{:S(2)}, u32[]{:S(2)}) collective-permute-start(bf16[256,2048]{1,0:T(8,128)(2,1)S(1)} %pack.2.refs_5_.refs_8_.refs_22_.refs_20_), channel_id=1, source_target_pairs={{0,8},{8,0},{16,24},{24,16},{1,9},{9,1},{17,25},{25,17},{2,10},{10... | collective-permute-start | bytes 3145736 | tf_op jit(solution)/shard_map/ppermute | solution.py:83
  11.4 3.5 %collective-permute-start.1 = (bf16[2,1024]{1,0:T(2,128)(2,1)S(1)}, bf16[2,1024]{1,0:T(2,128)(2,1)S(1)}, u32[]{:S(2)}, u32[]{:S(2)}) collective-permute-start(bf16[2,1024]{1,0:T(2,128)(2,1)S(1)} %pad_maximum_fusion.1), channel_id=1, source_target_pairs={{0,2},{2,4},{4,6},{1,3},{3,5},{5,7},{8,10},{10,12},{12,14},{9,11},... | collective-permute-start | bytes 12296 | tf_op jit(solution)/shard_map/ppermute | solution.py:90
  16.2 5.8 %mix_time.2 = (bf16[512,1024]{1,0:T(8,128)(2,1)S(1)}, bf16[512,1024]{1,0:T(8,128)(2,1)S(1)}, bf16[512,1024]{1,0:T(8,128)(2,1)S(1)}, bf16[512,1024]{1,0:T(8,128)(...) custom-call(s32[5]{0:T(128)S(1)} %pad_add_fusion.refs_0_, ...), custom_call_target="tpu_custom_call" | custom-call | tf_op jit(solution)/shard_map/mix_time/pallas_call | solution.py:37
  22.0 8.0 %collective-permute-done.3.refs_6_.refs_9_.refs_23_.refs_21_ = bf16[256,2048]{1,0:T(8,128)(2,1)S(1)} collective-permute-done((bf16[256,2048]{1,0:T(8,128)(2,1)S(1)}, bf16[256,2048]{1,0:T(8,128)(2,1)S(1)}, u32[]{:S(2)}, u32[]{:S(2)}) %collective-permute-start.3) | collective-permute-done | bytes 1048608 | tf_op jit(solution)/shard_map/ppermute | solution.py:83
  35.1 9.0 %collective-permute-done.5.refs_8_.refs_11_.refs_25_.refs_23_ = bf16[256,1024]{1,0:T(8,128)(2,1)S(1)} collective-permute-done((bf16[256,1024]{1,0:T(8,128)(2,1)S(1)}, bf16[256,1024]{1,0:T(8,128)(2,1)S(1)}, u32[]{:S(2)}, u32[]{:S(2)}) %collective-permute-start.5) | collective-permute-done | bytes 524320 | tf_op jit(solution)/shard_map/ppermute | solution.py:83
  51.4 5.1 %project_time.1 = (f32[4,512,128]{2,1,0:T(8,128)S(1)}, f32[4,512,128]{2,1,0:T(8,128)S(1)}, f32[512,512]{1,0:T(8,128)S(1)}, f32[4,48,128]{2,1,0:T(8,128)S(1)}, f32[6,512]{1,0:T(8,128)S(1)}) custom-call(s32[5]{0:T(128)S(1)} %pad_add_fusion.refs_0_, bf16[512,1024]{1,0:T(8,128)(2,1)S(1)} %get-tuple-element.189.refs_1_, ...), custom_call_target="tpu_custom_call" | custom-call | tf_op jit(solution)/shard_map/project_time/pallas_call | solution.py:37
  66.2 10.9 %collective-permute-done.10.refs_6_.refs_11_ = bf16[256,2560]{1,0:T(8,128)(2,1)S(1)} collective-permute-done((bf16[256,2560]{1,0:T(8,128)(2,1)S(1)}, bf16[256,2560]{1,0:T(8,128)(2,1)S(1)}, u32[]{:S(2)}, u32[]{:S(2)}) %collective-permute-start.10) | collective-permute-done | bytes 1310752 | tf_op jit(solution)/shard_map/ppermute | solution.py:83
  77.9 4.7 %sweep_time.1 = (f32[512,256]{1,0:T(8,128)S(1)}, f32[512,256]{1,0:T(8,128)S(1)}, f32[512,256]{1,0:T(8,128)S(1)}, f32[512,256]{1,0:T(8,128)S(1)}) custom-call(s32[5]{0:T(128)S(1)} %pad_add_fusion.refs_0_, f32[4,512,128]{2,1,0:T(8,128)S(1)} %get-tuple-element.195.refs_1_.refs_0_, f32[4,512,128]{2,1,0:T(8,128)S(1)} %get-tuple-element.196.refs_2_.refs_1_.refs_3_, ...), custom_call_target="tpu_custom_call" | custom-call | tf_op jit(solution)/shard_map/sweep_time/pallas_call | solution.py:37
  83.2 13.4 %collective-permute-done.16.refs_3_.refs_16_ = bf16[2048,256]{1,0:T(8,128)(2,1)S(1)} collective-permute-done((bf16[2048,256]{1,0:T(8,128)(2,1)S(1)}, bf16[2048,256]{1,0:T(8,128)(2,1)S(1)}, u32[]{:S(2)}, u32[]{:S(2)}) %collective-permute-start.16) | collective-permute-done | bytes 1048608 | tf_op jit(solution)/shard_map/ppermute | solution.py:83
  101.5 3.2 %middle_norm.1 = (f32[512,512]{1,0:T(8,128)S(1)}, f32[512,1024]{1,0:T(8,128)S(1)}, f32[512,1]{1,0:T(8,128)S(1)}, f32[2,1024]{1,0:T(2,128)S(1)}) custom-call(bf16[512,512]{1,0:T(8,128)(2,1)} %bitcast.4.refs_1_.refs_0_, bf16[512,512]{1,0:T(8,128)(2,1)} %collective-permute-done.refs_2_.refs_1_, f32[512,256]{1,0:T(8,128)S(1)} %get-tuple-element.205.refs_2_, ...), custom_call_target="tpu_custom_call" | custom-call | tf_op jit(solution)/shard_map/middle_norm/pallas_call | solution.py:37
  104.7 3.7 %collective-permute-start.18 = (f32[2,1024]{1,0:T(2,128)S(1)}, f32[2,1024]{1,0:T(2,128)S(1)}, u32[]{:S(2)}, u32[]{:S(2)}) collective-permute-start(f32[2,1024]{1,0:T(2,128)S(1)} %get-tuple-element.211), channel_id=1, source_target_pairs={{0,2},{2,4},{4,6},{1,3},{3,5},{5,7},{8,10},{10,12},{12,14},{9,11},... | collective-permute-start | bytes 24584 | tf_op jit(solution)/shard_map/ppermute | solution.py:90
  109.6 4.7 %collective-permute-done.19.refs_8_.refs_13_ = bf16[256,1280]{1,0:T(8,128)(2,1)S(1)} collective-permute-done((bf16[256,1280]{1,0:T(8,128)(2,1)S(1)}, bf16[256,1280]{1,0:T(8,128)(2,1)S(1)}, u32[]{:S(2)}, u32[]{:S(2)}) %collective-permute-start.19) | collective-permute-done | bytes 655392 | tf_op jit(solution)/shard_map/ppermute | solution.py:83
  115.3 5.0 %channel_forward.1 = (bf16[512,1024]{1,0:T(8,128)(2,1)S(1)}, bf16[512,1024]{1,0:T(8,128)(2,1)S(1)}, bf16[512,1024]{1,0:T(8,128)(2,1)S(1)}, bf16[512,1024]{1,0:T(...) custom-call(s32[5]{0:T(128)S(1)} %pad_add_fusion.refs_0_, ...), custom_call_target="tpu_custom_call" | custom-call | tf_op jit(solution)/shard_map/channel_forward/pallas_call | solution.py:37
  121.7 3.2 %channel_return.1 = (f32[512,256]{1,0:T(8,128)S(1)}, f32[512,256]{1,0:T(8,128)S(1)}, f32[512,256]{1,0:T(8,128)S(1)}, f32[512,256]{1,0:T(8,128)S(1)}) custom-call(s32[5]{0:T(128)S(1)} %pad_add_fusion.refs_0_, bf16[512,2048]{1,0:T(8,128)(2,1)S(1)} %get-tuple-element.212.refs_1_.refs_3_, bf16[2048,256]{1,0:T(8,128)(2,1)S(1)} %copy-done, ...), custom_call_target="tpu_custom_call" | custom-call | tf_op jit(solution)/shard_map/channel_return/pallas_call | solution.py:37
  131.6 3.2 %weight_products.4 = (bf16[512,1024]{1,0:T(8,128)(2,1)}, bf16[512,1024]{1,0:T(8,128)(2,1)S(1)}, bf16[512,1024]{1,0:T(8,128)(2,1)S(1)}, bf16[512,1024]{1,0:T(8,128)(2,1)S(1)}) custom-call(s32[5]{0:T(128)S(1)} %pad_add_fusion.refs_0_, bf16[512,512]{1,0:T(8,128)(2,1)S(1)} %get-tuple-element.220.refs_1_, bf16[512,512]{1,0:T(8,128)(2,1)S(1)} %collective-permute-done.25.refs_2_, ...), custom_call_target="tpu_custom_call" | custom-call | tf_op jit(solution)/shard_map/weight_products/pallas_call | solution.py:37
  137.6 3.1 %sweep_again.1 = (bf16[512,512]{1,0:T(8,128)(2,1)S(1)}, f32[4,512,128]{2,1,0:T(8,128)S(1)}, f32[512,512]{1,0:T(8,128)S(1)}, f32[512,512]{1,0:T(8,128)S(1)}, f32[...) custom-call(f32[4,512,128]{2,1,0:T(8,128)S(1)} %get-tuple-element.19, ...), custom_call_target="tpu_custom_call" | custom-call | tf_op jit(solution)/shard_map/sweep_again/pallas_call | solution.py:37
  140.7 4.9 %mix_time.3 = (bf16[512,1024]{1,0:T(8,128)(2,1)S(1)}, bf16[512,1024]{1,0:T(8,128)(2,1)S(1)}, bf16[512,1024]{1,0:T(8,128)(2,1)S(1)}, bf16[512,1024]{1,0:T(8,128)(...) custom-call(s32[5]{0:T(128)S(1)} %pad_add_fusion.refs_0_, ...), custom_call_target="tpu_custom_call" | custom-call | tf_op jit(solution)/shard_map/mix_time/pallas_call | solution.py:37
  146.6 9.0 %channel_backward.1 = (bf16[512,2048]{1,0:T(8,128)(2,1)S(1)}, f32[512,256]{1,0:T(8,128)S(1)}, f32[512,256]{1,0:T(8,128)S(1)}, f32[512,256]{1,0:T(8,128)S(1)}, f3...) custom-call(s32[5]{0:T(128)S(1)} %pad_add_fusion.refs_0_, ...), custom_call_target="tpu_custom_call" | custom-call | tf_op jit(solution)/shard_map/channel_backward/pallas_call | solution.py:37
  156.8 3.8 %weight_products.5 = (bf16[512,1280]{1,0:T(8,128)(2,1)S(1)}, bf16[512,1280]{1,0:T(8,128)(2,1)S(1)}, bf16[512,1280]{1,0:T(8,128)(2,1)S(1)}, bf16[512,1280]{1,0:T(8,128)(2,1)S(1)}) custom-call(s32[5]{0:T(128)S(1)} %pad_add_fusion.refs_0_, bf16[512,1024]{1,0:T(8,128)(2,1)S(1)} %copy-done.9, bf16[512,1024]{1,0:T(8,128)(2,1)S(1)} %copy-done.11, ...), custom_call_target="tpu_custom_call" | custom-call | tf_op jit(solution)/shard_map/weight_products/pallas_call | solution.py:37
  165.5 2.9 collective-permute-done.32.refs_9_
  174.1 6.6 %middle_backward.1 = (bf16[512,1024]{1,0:T(8,128)(2,1)S(1)}, f32[512,512]{1,0:T(8,128)S(1)}, f32[4,512,128]{2,1,0:T(8,128)S(1)}, bf16[512,512]{1,0:T(8,128)(2,1)...) custom-call(s32[5]{0:T(128)S(1)} %pad_add_fusion.refs_0_, f32[512,256]{1,0:T(8,128)S(1)} %get-tuple-element.234.refs_1_, ...), custom_call_target="tpu_custom_call" | custom-call | tf_op jit(solution)/shard_map/middle_backward/pallas_call | solution.py:37
  185.1 2.9 collective-permute-start.35
  198.9 10.7 %time_backward.1 = (bf16[512,512]{1,0:T(8,128)(2,1)S(1)}, bf16[512,512]{1,0:T(8,128)(2,1)S(1)}, f32[512,512]{1,0:T(8,128)S(1)}, f32[512,256]{1,0:T(8,128)S(1)}, ...) custom-call(s32[5]{0:T(128)S(1)} %pad_add_fusion.refs_0_, ...), custom_call_target="tpu_custom_call" | custom-call | tf_op jit(solution)/shard_map/time_backward/pallas_call | solution.py:37
  216.1 2.7 collective-permute-start.48
  226.8 4.3 %collective-permute-done.48.refs_13_.refs_1_ = bf16[128,2048]{1,0:T(8,128)(2,1)S(1)} collective-permute-done((bf16[128,2048]{1,0:T(8,128)(2,1)S(1)}, bf16[128,2048]{1,0:T(8,128)(2,1)S(1)}, u32[]{:S(2)}, u32[]{:S(2)}) %collective-permute-start.48) | collective-permute-done | bytes 524320 | tf_op jit(solution)/shard_map/ppermute | solution.py:83
  232.9 4.4 %collective-permute-done.50.refs_3_ = bf16[512,512]{1,0:T(8,128)(2,1)S(1)} collective-permute-done((bf16[512,512]{1,0:T(8,128)(2,1)S(1)}, bf16[512,512]{1,0:T(8,128)(2,1)S(1)}, u32[]{:S(2)}, u32[]{:S(2)}) %collective-permute-start.50) | collective-permute-done | bytes 524320 | tf_op jit(solution)/shard_map/ppermute | solution.py:83
  240.3 8.3 %collective-permute-done.55.refs_1_ = bf16[512,512]{1,0:T(8,128)(2,1)S(1)} collective-permute-done((bf16[512,512]{1,0:T(8,128)(2,1)S(1)}, bf16[512,512]{1,0:T(8,128)(2,1)S(1)}, u32[]{:S(2)}, u32[]{:S(2)}) %collective-permute-start.55) | collective-permute-done | bytes 524320 | tf_op jit(solution)/shard_map/ppermute | solution.py:83
  253.5 3.9 %collective-permute-done.52.refs_3_ = bf16[256,512]{1,0:T(8,128)(2,1)S(1)} collective-permute-done((bf16[256,512]{1,0:T(8,128)(2,1)S(1)}, bf16[256,512]{1,0:T(8,128)(2,1)S(1)}, u32[]{:S(2)}, u32[]{:S(2)}) %collective-permute-start.52) | collective-permute-done | bytes 262176 | tf_op jit(solution)/shard_map/ppermute | solution.py:83
  267.0 3.0 collective-permute-start.63
  270.6 9.4 %collective-permute-done.61.refs_1_ = bf16[128,1024]{1,0:T(8,128)(2,1)S(1)} collective-permute-done((bf16[128,1024]{1,0:T(8,128)(2,1)S(1)}, bf16[128,1024]{1,0:T(8,128)(2,1)S(1)}, u32[]{:S(2)}, u32[]{:S(2)}) %collective-permute-start.61) | collective-permute-done | bytes 262176 | tf_op jit(solution)/shard_map/ppermute | solution.py:83
  281.0 11.7 %collective-permute-done.63.refs_1_ = bf16[64,2560]{1,0:T(8,128)(2,1)S(1)} collective-permute-done((bf16[64,2560]{1,0:T(8,128)(2,1)S(1)}, bf16[64,2560]{1,0:T(8,128)(2,1)S(1)}, u32[]{:S(2)}, u32[]{:S(2)}) %collective-permute-start.63) | collective-permute-done | bytes 327712 | tf_op jit(solution)/shard_map/ppermute | solution.py:83
  293.5 3.7 %collective-permute-done.62.refs_1_ = bf16[64,1024]{1,0:T(8,128)(2,1)S(1)} collective-permute-done((bf16[64,1024]{1,0:T(8,128)(2,1)S(1)}, bf16[64,1024]{1,0:T(8,128)(2,1)S(1)}, u32[]{:S(2)}, u32[]{:S(2)}) %collective-permute-start.62) | collective-permute-done | bytes 131104 | tf_op jit(solution)/shard_map/ppermute | solution.py:83
  (201 shorter events, 116.3 us)
Async XLA Ops:
  3.8 26.2 %collective-permute-start.3 = (bf16[256,2048]{1,0:T(8,128)(2,1)S(1)}, bf16[256,2048]{1,0:T(8,128)(2,1)S(1)}, u32[]{:S(2)}, u32[]{:S(2)}) collective-permute-start(bf16[256,2048]{1,0:T(8,128)(2,1)S(1)} %pack.2.refs_5_.refs_8_.refs_22_.refs_20_), channel_id=1, source_target_pairs={{0,8},{8,0},{16,24},{24,16},{1,9},{9,1},{17,25},{25,17},{2,10},{10... | collective-permute-start | bytes 3145736 | tf_op jit(solution)/shard_map/ppermute | solution.py:83
  6.8 24.6 %collective-permute-start.4 = (bf16[256,2048]{1,0:T(8,128)(2,1)S(1)}, bf16[256,2048]{1,0:T(8,128)(2,1)S(1)}, u32[]{:S(2)}, u32[]{:S(2)}) collective-permute-start(bf16[256,2048]{1,0:T(8,128)(2,1)S(1)} %pack.2.refs_5_.refs_8_.refs_22_.refs_20_), channel_id=1, source_target_pairs={{0,16},{8,24},{16,0},{24,8},{1,17},{9,25},{17,1},{25,9},{2,18},{10... | collective-permute-start | bytes 3145736 | tf_op jit(solution)/shard_map/ppermute | solution.py:83
  45.4 31.7 %collective-permute-start.10 = (bf16[256,2560]{1,0:T(8,128)(2,1)S(1)}, bf16[256,2560]{1,0:T(8,128)(2,1)S(1)}, u32[]{:S(2)}, u32[]{:S(2)}) collective-permute-start(bf16[256,2560]{1,0:T(8,128)(2,1)S(1)} %pack.3.refs_5_.refs_10_), channel_id=1, source_target_pairs={{0,8},{8,0},{16,24},{24,16},{1,9},{9,1},{17,25},{25,17},{2,10},{10... | collective-permute-start | bytes 3932168 | tf_op jit(solution)/shard_map/ppermute | solution.py:83
  46.0 31.7 %collective-permute-start.11 = (bf16[256,2560]{1,0:T(8,128)(2,1)S(1)}, bf16[256,2560]{1,0:T(8,128)(2,1)S(1)}, u32[]{:S(2)}, u32[]{:S(2)}) collective-permute-start(bf16[256,2560]{1,0:T(8,128)(2,1)S(1)} %pack.3.refs_5_.refs_10_), channel_id=1, source_target_pairs={{0,16},{8,24},{16,0},{24,8},{1,17},{9,25},{17,1},{25,9},{2,18},{10... | collective-permute-start | bytes 3932168 | tf_op jit(solution)/shard_map/ppermute | solution.py:83
  46.6 50.0 %collective-permute-start.16 = (bf16[2048,256]{1,0:T(8,128)(2,1)S(1)}, bf16[2048,256]{1,0:T(8,128)(2,1)S(1)}, u32[]{:S(2)}, u32[]{:S(2)}) collective-permute-start(bf16[2048,256]{1,0:T(8,128)(2,1)S(1)} %copy-done), channel_id=1, source_target_pairs={{0,8},{8,0},{16,24},{24,16},{1,9},{9,1},{17,25},{25,17},{2,10},{10... | collective-permute-start | bytes 3145736 | tf_op jit(solution)/shard_map/ppermute | solution.py:83
  48.0 49.6 %collective-permute-start.17 = (bf16[2048,256]{1,0:T(8,128)(2,1)S(1)}, bf16[2048,256]{1,0:T(8,128)(2,1)S(1)}, u32[]{:S(2)}, u32[]{:S(2)}) collective-permute-start(bf16[2048,256]{1,0:T(8,128)(2,1)S(1)} %copy-done), channel_id=1, source_target_pairs={{0,16},{8,24},{16,0},{24,8},{1,17},{9,25},{17,1},{25,9},{2,18},{10... | collective-permute-start | bytes 3145736 | tf_op jit(solution)/shard_map/ppermute | solution.py:83
  82.6 17.0 %collective-permute-start.12 = (f32[512,256]{1,0:T(8,128)S(1)}, f32[512,256]{1,0:T(8,128)S(1)}, u32[]{:S(2)}, u32[]{:S(2)}) collective-permute-start(f32[512,256]{1,0:T(8,128)S(1)} %get-tuple-element.207.refs_4_), channel_id=1, source_target_pairs={{0,1},{1,0},{2,3},{3,2},{4,5},{5,4},{6,7},{7,6},{8,9},{9,8},{10,11... | collective-permute-start | bytes 1572872 | tf_op jit(solution)/shard_map/ppermute | solution.py:83
  82.6 17.1 %collective-permute-start.13 = (f32[512,256]{1,0:T(8,128)S(1)}, f32[512,256]{1,0:T(8,128)S(1)}, u32[]{:S(2)}, u32[]{:S(2)}) collective-permute-start(f32[512,256]{1,0:T(8,128)S(1)} %get-tuple-element.208.refs_5_), channel_id=1, source_target_pairs={{0,1},{1,0},{2,3},{3,2},{4,5},{5,4},{6,7},{7,6},{8,9},{9,8},{10,11... | collective-permute-start | bytes 1572872 | tf_op jit(solution)/shard_map/ppermute | solution.py:83
  83.1 16.7 %collective-permute-start.14 = (f32[512,256]{1,0:T(8,128)S(1)}, f32[512,256]{1,0:T(8,128)S(1)}, u32[]{:S(2)}, u32[]{:S(2)}) collective-permute-start(f32[512,256]{1,0:T(8,128)S(1)} %get-tuple-element.205.refs_2_), channel_id=1, source_target_pairs={{0,1},{1,0},{2,3},{3,2},{4,5},{5,4},{6,7},{7,6},{8,9},{9,8},{10,11... | collective-permute-start | bytes 1572872 | tf_op jit(solution)/shard_map/ppermute | solution.py:83
  96.6 17.7 %collective-permute-start.19 = (bf16[256,1280]{1,0:T(8,128)(2,1)S(1)}, bf16[256,1280]{1,0:T(8,128)(2,1)S(1)}, u32[]{:S(2)}, u32[]{:S(2)}) collective-permute-start(bf16[256,1280]{1,0:T(8,128)(2,1)S(1)} %slice.67.refs_13_), channel_id=1, source_target_pairs={{0,16},{8,24},{16,0},{24,8},{1,17},{9,25},{17,1},{25,9},{2,18},{10... | collective-permute-start | bytes 1966088 | tf_op jit(solution)/shard_map/ppermute | solution.py:83
  97.6 17.7 %collective-permute-start.20 = (bf16[256,1280]{1,0:T(8,128)(2,1)S(1)}, bf16[256,1280]{1,0:T(8,128)(2,1)S(1)}, u32[]{:S(2)}, u32[]{:S(2)}) collective-permute-start(bf16[256,1280]{1,0:T(8,128)(2,1)S(1)} %slice.68.refs_14_), channel_id=1, source_target_pairs={{0,8},{8,0},{16,24},{24,16},{1,9},{9,1},{17,25},{25,17},{2,10},{10... | collective-permute-start | bytes 1966088 | tf_op jit(solution)/shard_map/ppermute | solution.py:83
  99.7 22.0 %collective-permute-start.21 = (bf16[1024,256]{1,0:T(8,128)(2,1)S(1)}, bf16[1024,256]{1,0:T(8,128)(2,1)S(1)}, u32[]{:S(2)}, u32[]{:S(2)}) collective-permute-start(bf16[1024,256]{1,0:T(8,128)(2,1)S(1)} %slice.85.refs_10_), channel_id=1, source_target_pairs={{0,16},{8,24},{16,0},{24,8},{1,17},{9,25},{17,1},{25,9},{2,18},{10... | collective-permute-start | bytes 1572872 | tf_op jit(solution)/shard_map/ppermute | solution.py:83
  99.8 21.9 %collective-permute-start.22 = (bf16[1024,256]{1,0:T(8,128)(2,1)S(1)}, bf16[1024,256]{1,0:T(8,128)(2,1)S(1)}, u32[]{:S(2)}, u32[]{:S(2)}) collective-permute-start(bf16[1024,256]{1,0:T(8,128)(2,1)S(1)} %slice.86.refs_11_), channel_id=1, source_target_pairs={{0,8},{8,0},{16,24},{24,16},{1,9},{9,1},{17,25},{25,17},{2,10},{10... | collective-permute-start | bytes 1572872 | tf_op jit(solution)/shard_map/ppermute | solution.py:83
  135.8 27.1 %collective-permute-start.26 = (bf16[512,1024]{1,0:T(8,128)(2,1)}, bf16[512,1024]{1,0:T(8,128)(2,1)S(1)}, u32[]{:S(2)}, u32[]{:S(2)}) collective-permute-start(bf16[512,1024]{1,0:T(8,128)(2,1)} %get-tuple-element.225.refs_20_), channel_id=1, source_target_pairs={{0,8},{8,0},{16,24},{24,16},{1,9},{9,1},{17,25},{25,17},{2,10},{10... | collective-permute-start | bytes 3145736 | tf_op jit(solution)/shard_map/ppermute | solution.py:83
  137.1 25.7 %collective-permute-start.27 = (bf16[512,1024]{1,0:T(8,128)(2,1)S(1)}, bf16[512,1024]{1,0:T(8,128)(2,1)}, u32[]{:S(2)}, u32[]{:S(2)}) collective-permute-start(bf16[512,1024]{1,0:T(8,128)(2,1)S(1)} %get-tuple-element.233), channel_id=1, source_target_pairs={{0,16},{8,24},{16,0},{24,8},{1,17},{9,25},{17,1},{25,9},{2,18},{10... | collective-permute-start | bytes 3145736 | tf_op jit(solution)/shard_map/ppermute | solution.py:83
  160.6 31.8 %collective-permute-start.36 = (bf16[512,1280]{1,0:T(8,128)(2,1)S(1)}, bf16[512,1280]{1,0:T(8,128)(2,1)S(1)}, u32[]{:S(2)}, u32[]{:S(2)}) collective-permute-start(bf16[512,1280]{1,0:T(8,128)(2,1)S(1)} %get-tuple-element.265), channel_id=1, source_target_pairs={{0,8},{8,0},{16,24},{24,16},{1,9},{9,1},{17,25},{25,17},{2,10},{10... | collective-permute-start | bytes 3932168 | tf_op jit(solution)/shard_map/ppermute | solution.py:83
  161.7 31.7 %collective-permute-start.37 = (bf16[512,1280]{1,0:T(8,128)(2,1)S(1)}, bf16[512,1280]{1,0:T(8,128)(2,1)S(1)}, u32[]{:S(2)}, u32[]{:S(2)}) collective-permute-start(bf16[512,1280]{1,0:T(8,128)(2,1)S(1)} %get-tuple-element.267), channel_id=1, source_target_pairs={{0,16},{8,24},{16,0},{24,8},{1,17},{9,25},{17,1},{25,9},{2,18},{10... | collective-permute-start | bytes 3932168 | tf_op jit(solution)/shard_map/ppermute | solution.py:83
  172.2 38.7 %collective-permute-start.44 = (bf16[256,1024]{1,0:T(8,128)(2,1)S(1)}, bf16[256,1024]{1,0:T(8,128)(2,1)S(1)}, u32[]{:S(2)}, u32[]{:S(2)}) collective-permute-start(bf16[256,1024]{1,0:T(8,128)(2,1)S(1)} %get-tuple-element.294), channel_id=1, source_target_pairs={{0,16},{8,24},{16,0},{24,8},{1,17},{9,25},{17,1},{25,9},{2,18},{10... | collective-permute-start | bytes 1572872 | tf_op jit(solution)/shard_map/ppermute | solution.py:83
  173.1 39.3 %collective-permute-start.45 = (bf16[256,1024]{1,0:T(8,128)(2,1)S(1)}, bf16[256,1024]{1,0:T(8,128)(2,1)S(1)}, u32[]{:S(2)}, u32[]{:S(2)}) collective-permute-start(bf16[256,1024]{1,0:T(8,128)(2,1)S(1)} %get-tuple-element.295), channel_id=1, source_target_pairs={{0,8},{8,0},{16,24},{24,16},{1,9},{9,1},{17,25},{25,17},{2,10},{10... | collective-permute-start | bytes 1572872 | tf_op jit(solution)/shard_map/ppermute | solution.py:83
  194.0 26.1 %collective-permute-start.46 = (bf16[256,1280]{1,0:T(8,128)(2,1)S(1)}, bf16[256,1280]{1,0:T(8,128)(2,1)S(1)}, u32[]{:S(2)}, u32[]{:S(2)}) collective-permute-start(bf16[256,1280]{1,0:T(8,128)(2,1)S(1)} %get-tuple-element.272.refs_25_), channel_id=1, source_target_pairs={{0,16},{8,24},{16,0},{24,8},{1,17},{9,25},{17,1},{25,9},{2,18},{10... | collective-permute-start | bytes 1966088 | tf_op jit(solution)/shard_map/ppermute | solution.py:83
  195.2 24.9 %collective-permute-start.47 = (bf16[256,1280]{1,0:T(8,128)(2,1)S(1)}, bf16[256,1280]{1,0:T(8,128)(2,1)S(1)}, u32[]{:S(2)}, u32[]{:S(2)}) collective-permute-start(bf16[256,1280]{1,0:T(8,128)(2,1)S(1)} %get-tuple-element.273.refs_26_), channel_id=1, source_target_pairs={{0,8},{8,0},{16,24},{24,16},{1,9},{9,1},{17,25},{25,17},{2,10},{10... | collective-permute-start | bytes 1966088 | tf_op jit(solution)/shard_map/ppermute | solution.py:83
  216.1 15.1 %collective-permute-start.48 = (bf16[128,2048]{1,0:T(8,128)(2,1)S(1)}, bf16[128,2048]{1,0:T(8,128)(2,1)S(1)}, u32[]{:S(2)}, u32[]{:S(2)}) collective-permute-start(bf16[128,2048]{1,0:T(8,128)(2,1)S(1)} %get-tuple-element.303), channel_id=1, source_target_pairs={{0,2},{2,0},{4,6},{6,4},{1,3},{3,1},{5,7},{7,5},{8,10},{10,8},{12,... | collective-permute-start | bytes 1572872 | tf_op jit(solution)/shard_map/ppermute | solution.py:83
  222.4 14.8 %collective-permute-start.50 = (bf16[512,512]{1,0:T(8,128)(2,1)S(1)}, bf16[512,512]{1,0:T(8,128)(2,1)S(1)}, u32[]{:S(2)}, u32[]{:S(2)}) collective-permute-start(bf16[512,512]{1,0:T(8,128)(2,1)S(1)} %get-tuple-element.306), channel_id=1, source_target_pairs={{0,16},{8,24},{16,0},{24,8},{1,17},{9,25},{17,1},{25,9},{2,18},{10... | collective-permute-start | bytes 1572872 | tf_op jit(solution)/shard_map/ppermute | solution.py:83
  223.0 15.5 %collective-permute-start.49 = (bf16[544,512]{1,0:T(8,128)(2,1)S(1)}, bf16[544,512]{1,0:T(8,128)(2,1)S(1)}, u32[]{:S(2)}, u32[]{:S(2)}) collective-permute-start(bf16[544,512]{1,0:T(8,128)(2,1)S(1)} %get-tuple-element.304), channel_id=1, source_target_pairs={{0,8},{8,0},{16,24},{24,16},{1,9},{9,1},{17,25},{25,17},{2,10},{10... | collective-permute-start | bytes 1671176 | tf_op jit(solution)/shard_map/ppermute | solution.py:83
  224.0 24.6 %collective-permute-start.55 = (bf16[512,512]{1,0:T(8,128)(2,1)S(1)}, bf16[512,512]{1,0:T(8,128)(2,1)S(1)}, u32[]{:S(2)}, u32[]{:S(2)}) collective-permute-start(bf16[512,512]{1,0:T(8,128)(2,1)S(1)} %get-tuple-element.320), channel_id=1, source_target_pairs={{0,8},{8,0},{16,24},{24,16},{1,9},{9,1},{17,25},{25,17},{2,10},{10... | collective-permute-start | bytes 1572872 | tf_op jit(solution)/shard_map/ppermute | solution.py:83
  225.0 23.6 %collective-permute-start.56 = (bf16[512,512]{1,0:T(8,128)(2,1)S(1)}, bf16[512,512]{1,0:T(8,128)(2,1)S(1)}, u32[]{:S(2)}, u32[]{:S(2)}) collective-permute-start(bf16[512,512]{1,0:T(8,128)(2,1)S(1)} %get-tuple-element.322), channel_id=1, source_target_pairs={{0,16},{8,24},{16,0},{24,8},{1,17},{9,25},{17,1},{25,9},{2,18},{10... | collective-permute-start | bytes 1572872 | tf_op jit(solution)/shard_map/ppermute | solution.py:83
  231.2 22.1 %collective-permute-start.57 = (bf16[128,2560]{1,0:T(8,128)(2,1)S(1)}, bf16[128,2560]{1,0:T(8,128)(2,1)S(1)}, u32[]{:S(2)}, u32[]{:S(2)}) collective-permute-start(bf16[128,2560]{1,0:T(8,128)(2,1)S(1)} %get-tuple-element.329), channel_id=1, source_target_pairs={{0,2},{2,0},{4,6},{6,4},{1,3},{3,1},{5,7},{7,5},{8,10},{10,8},{12,... | collective-permute-start | bytes 1966088 | tf_op jit(solution)/shard_map/ppermute | solution.py:83
  237.2 14.6 %collective-permute-start.58 = (bf16[64,2048]{1,0:T(8,128)(2,1)S(1)}, bf16[64,2048]{1,0:T(8,128)(2,1)S(1)}, u32[]{:S(2)}, u32[]{:S(2)}) collective-permute-start(bf16[64,2048]{1,0:T(8,128)(2,1)S(1)} %get-tuple-element.331), channel_id=1, source_target_pairs={{0,4},{2,6},{4,0},{6,2},{1,5},{3,7},{5,1},{7,3},{8,12},{10,14},{12... | collective-permute-start | bytes 786440 | tf_op jit(solution)/shard_map/ppermute | solution.py:83
  238.7 20.1 %collective-permute-start.51 = (bf16[288,512]{1,0:T(8,128)(2,1)S(1)}, bf16[288,512]{1,0:T(8,128)(2,1)S(1)}, u32[]{:S(2)}, u32[]{:S(2)}) collective-permute-start(bf16[288,512]{1,0:T(8,128)(2,1)S(1)} %get-tuple-element.309), channel_id=1, source_target_pairs={{0,16},{8,24},{16,0},{24,8},{1,17},{9,25},{17,1},{25,9},{2,18},{10... | collective-permute-start | bytes 884744 | tf_op jit(solution)/shard_map/ppermute | solution.py:83
  267.0 25.7 %collective-permute-start.63 = (bf16[64,2560]{1,0:T(8,128)(2,1)S(1)}, bf16[64,2560]{1,0:T(8,128)(2,1)S(1)}, u32[]{:S(2)}, u32[]{:S(2)}) collective-permute-start(bf16[64,2560]{1,0:T(8,128)(2,1)S(1)} %get-tuple-element.354), channel_id=1, source_target_pairs={{0,4},{2,6},{4,0},{6,2},{1,5},{3,7},{5,1},{7,3},{8,12},{10,14},{12... | collective-permute-start | bytes 983048 | tf_op jit(solution)/shard_map/ppermute | solution.py:83
  270.1 27.9 %collective-permute-start.54 = (bf16[96,1024]{1,0:T(8,128)(2,1)S(1)}, bf16[96,1024]{1,0:T(8,128)(2,1)S(1)}, u32[]{:S(2)}, u32[]{:S(2)}) collective-permute-start(bf16[96,1024]{1,0:T(8,128)(2,1)S(1)} %get-tuple-element.317), channel_id=1, source_target_pairs={{0,4},{2,6},{4,0},{6,2},{1,5},{3,7},{5,1},{7,3},{8,12},{10,14},{12... | collective-permute-start | bytes 589832 | tf_op jit(solution)/shard_map/ppermute | solution.py:83
  280.1 17.1 %collective-permute-start.62 = (bf16[64,1024]{1,0:T(8,128)(2,1)S(1)}, bf16[64,1024]{1,0:T(8,128)(2,1)S(1)}, u32[]{:S(2)}, u32[]{:S(2)}) collective-permute-start(bf16[64,1024]{1,0:T(8,128)(2,1)S(1)} %get-tuple-element.347), channel_id=1, source_target_pairs={{0,4},{2,6},{4,0},{6,2},{1,5},{3,7},{5,1},{7,3},{8,12},{10,14},{12... | collective-permute-start | bytes 393224 | tf_op jit(solution)/shard_map/ppermute | solution.py:83
  (56 other events, 385.9 us)

commit v4 on v3

--- a/solution.py
+++ b/solution.py
@@ -299,11 +299,26 @@
     )
     fading = logarithmic_fading_per_feature.reshape(1, H)
     bonus = present_entry_reward.reshape(1, H)
-    time_matrix = side_by_side(
-        lookup_projection,
-        payload_projection,
-        filter_projection,
-        temporal_mix_emit_projection.T,
+    def pack_time(key_part, value_part, gate_part, emit_part, whole, tall, sems):
+        copies = [
+            pltpu.make_async_copy(part, whole.at[:, pl.ds(i * H, H)], sems.at[i])
+            for i, part in enumerate((key_part, value_part, gate_part))
+        ]
+        copies.append(pltpu.make_async_copy(emit_part, tall, sems.at[3]))
+        begin(copies)
+        copies[3].wait()
+        whole[:, 3 * H :] = tall[...].astype(F32).T.astype(BF16)
+        finish(copies[:3])
+
+    time_parts = (
+        lookup_projection, payload_projection, filter_projection, temporal_mix_emit_projection,
+    )
+    (time_matrix,) = launch(
+        pack_time,
+        "hhhh",
+        [pltpu.with_memory_space_constraint(part, pltpu.HBM) for part in time_parts],
+        [((SR, 4 * H), BF16)],
+        [pltpu.VMEM((H, SR), BF16), pltpu.SemaphoreType.DMA((4,))],
     )
     time_first = gather_first(time_matrix)
     x_other = swap(x_own, "tp", 1)
@@ -611,13 +626,13 @@
         begin(copies_r)
         finish(copies_r)
         for p in range(S):
-            parts[p][...] = dot(squared[...], wr[p])
+            parts[p][...] = dot(squared[...], wr[p]).astype(parts[p].dtype)
 
     returned = launch(
         channel_return,
         "sv" + "h" * 5,
         (idx, squared, *return_pieces),
-        [((T, SR), F32)] * S,
+        [((T, SR), F32)] * (S // 2) + [((T, SR), BF16)] * (S // 2),
         [pltpu.VMEM((S, FH, SR), BF16), pltpu.SemaphoreType.DMA((5,))],
     )
     ret_keep = returned[: S // 2]
@@ -633,7 +648,7 @@
             def tile(i, carry):
                 at = rows_at(r, i)
                 live = live_rows(idx, r, i)
-                returned = columns((m0, m1), at) + columns((t0, t1), at)
+                returned = columns((m0, m1), at) + columns((t0, t1), at).astype(F32)
                 s = opened[at, :]
                 out[at, :] = (live * (middle[at, :] + s * returned)).astype(BF16)
                 grad = live * up[at, :].astype(F32)
@@ -957,7 +972,7 @@
             (0, 0, part, FH - part, 1, 0),
             (1, 1, 0, H, 1, FH - part),
         ],
-        after=(gated, root_one),
+        after=(gated, root_one,),
     )
     hidden_state = square_start(*hidden_parts)
     return_turn = square_turn(return_state)
@@ -1068,7 +1083,7 @@
             pltpu.VMEM((T, H), F32),
             pltpu.SemaphoreType.DMA((5,)),
         ],
-        after=(hidden_parts[1],),
+        after=(hidden_parts[1], return_turn[0], return_turn[2],),
     )
 
     def no_adjoint():
@@ -1230,7 +1245,7 @@
         + [pltpu.VMEM((G, T, 128), F32)] * 2
         + [pltpu.VMEM((T, WIDTH), F32)] * 3
         + [pltpu.VMEM((G, 2 * R * CHUNKS, 128), F32), pltpu.SemaphoreType.DMA((5,))],
-        after=(hidden_turn_out[0], hidden_turn_out[2], early_parts[1]),
+        after=(early_parts[1],),
     )
     one_other = [swap(part, "tp", 1) for part in one_send]
     first_one_own = along_ctx(first_one, -1, False)
@@ -1241,7 +1256,7 @@
         [[mixed_key], [mixed_value]],
         [grad_key, grad_value],
         [(0, 0, 0, H, 0, 0), (1, 1, 0, H, 1, 0)],
-        after=(return_cross[1], return_cross[3], hidden_cross[1], hidden_cross[3]),
+        after=(return_cross[1], return_cross[3], hidden_cross[1], hidden_cross[3],),
         riders=(sums_one, sums_two, sums_other, sums_own),
     )
     late_state = square_start(*late_parts)
@@ -1250,7 +1265,6 @@
     (return_w,) = scatter_line(
         *square_end(hold(return_cross, first_one_own, first_one_other)), widths=[FH], seen=return_seen
     )
-
     def input_backward(
         mine, sent, t0, t1, theirs, e_own, e_other, hat, root, po, pp, gm, out
     ):
@@ -1297,15 +1311,16 @@
             grad_mid_own,
         ),
         [((T, H), F32)],
-        after=(late_parts[1], return_seen[0]),
+        after=(late_parts[1],),
     )
     hidden_seen = []
     hidden_w, filter_w = scatter_line(
-        *square_end(hold(hidden_cross, late_parts[1])), widths=[FH, H], seen=hidden_seen
+        *square_end(hidden_cross), widths=[FH, H], seen=hidden_seen
     )
     early_cross = square_cross(*square_turn(hold(early_state, hidden_seen[0], return_seen[-1])))
     late_cross = square_cross(*square_turn(late_state))
-    output_w, gate_w = scatter_line(*square_end(hold(early_cross, input_grad)), widths=[H, H])
+    early_seen = []
+    output_w, gate_w = scatter_line(*square_end(hold(early_cross, late_cross[1], late_cross[3])), widths=[H, H], seen=early_seen)
     key_w, value_w, vectors = scatter_line(*square_end(late_cross), widths=[H, H])
     shape = block_entries.shape
     return (

time: 300 us -> 297 us (0.990)
  transfers between devices with their start and end apart: 64 -> 64, of which waited for: 42 -> 43; matrix products, arithmetic and copies ran while one was open for 1% -> 1% of each run, Pallas kernels for 26% -> 27%
where the time goes in v4:
time: 297 us; the launch traced here: 296 us
  waiting for transfers between devices  135 us (45%)
  Pallas kernels  90.6 us (31%)
  starting transfers between devices  63.5 us (21%)
  local copies, waits for them, and re-layouts  5.09 us (2%)
    ppermute x58, waiting for transfers between devices, swap(): return lax.ppermute(value, axis, [(i, i ^ step) for i in range(size)])  125 us
    pallas_call x39, Pallas kernels, launch(): pl.pallas_call(run, out_shape=[jax.ShapeDtypeStruct(shape, dtype) for sha...  90.6 us
    ppermute x58, starting transfers between devices, swap(): return lax.ppermute(value, axis, [(i, i ^ step) for i in range(size)])  51 us
    ppermute x4, starting transfers between devices, along_ctx(): return lax.ppermute(value, 'ctx', pairs)  9.73 us
    ppermute x4, waiting for transfers between devices, along_ctx(): return lax.ppermute(value, 'ctx', pairs)  7.99 us
  transfers between devices with their start and end apart: 64, of which 43 were waited for; matrix products, arithmetic and copies ran while one was open for 1% of the time, Pallas kernels for 27%

profile of v4, /device:TPU:0, one launch (start us, length us, event | category | flops | bytes accessed | tf_op | source)
XLA Modules:
  0.0 296.1 jit_solution(6742874845362407348)
XLA Ops:
  2.2 3.0 %collective-permute-start.3 = (bf16[256,2048]{1,0:T(8,128)(2,1)S(1)}, bf16[256,2048]{1,0:T(8,128)(2,1)S(1)}, u32[]{:S(2)}, u32[]{:S(2)}) collective-permute-start(bf16[256,2048]{1,0:T(8,128)(2,1)S(1)} %pack_time.1.refs_5_.refs_8_.refs_22_.refs_20_), channel_id=1, source_target_pairs={{0,8},{8,0},{16,24},{24,16},{1,9},{9,1},{17,25},{25,17},{2,10},{10... | collective-permute-start | bytes 3145736 | tf_op jit(solution)/shard_map/ppermute | solution.py:83
  9.7 3.5 %collective-permute-start.1 = (bf16[2,1024]{1,0:T(2,128)(2,1)S(1)}, bf16[2,1024]{1,0:T(2,128)(2,1)S(1)}, u32[]{:S(2)}, u32[]{:S(2)}) collective-permute-start(bf16[2,1024]{1,0:T(2,128)(2,1)S(1)} %pad_maximum_fusion.1), channel_id=1, source_target_pairs={{0,2},{2,4},{4,6},{1,3},{3,5},{5,7},{8,10},{10,12},{12,14},{9,11},... | collective-permute-start | bytes 12296 | tf_op jit(solution)/shard_map/ppermute | solution.py:90
  14.5 5.8 %mix_time.2 = (bf16[512,1024]{1,0:T(8,128)(2,1)S(1)}, bf16[512,1024]{1,0:T(8,128)(2,1)S(1)}, bf16[512,1024]{1,0:T(8,128)(2,1)S(1)}, bf16[512,1024]{1,0:T(8,128)(...) custom-call(s32[5]{0:T(128)S(1)} %pad_add_fusion.refs_0_, ...), custom_call_target="tpu_custom_call" | custom-call | tf_op jit(solution)/shard_map/mix_time/pallas_call | solution.py:37
  20.3 8.0 %collective-permute-done.3.refs_6_.refs_9_.refs_23_.refs_21_ = bf16[256,2048]{1,0:T(8,128)(2,1)S(1)} collective-permute-done((bf16[256,2048]{1,0:T(8,128)(2,1)S(1)}, bf16[256,2048]{1,0:T(8,128)(2,1)S(1)}, u32[]{:S(2)}, u32[]{:S(2)}) %collective-permute-start.3) | collective-permute-done | bytes 1048608 | tf_op jit(solution)/shard_map/ppermute | solution.py:83
  33.4 9.0 %collective-permute-done.5.refs_8_.refs_11_.refs_25_.refs_23_ = bf16[256,1024]{1,0:T(8,128)(2,1)S(1)} collective-permute-done((bf16[256,1024]{1,0:T(8,128)(2,1)S(1)}, bf16[256,1024]{1,0:T(8,128)(2,1)S(1)}, u32[]{:S(2)}, u32[]{:S(2)}) %collective-permute-start.5) | collective-permute-done | bytes 524320 | tf_op jit(solution)/shard_map/ppermute | solution.py:83
  49.8 5.1 %project_time.1 = (f32[4,512,128]{2,1,0:T(8,128)S(1)}, f32[4,512,128]{2,1,0:T(8,128)S(1)}, f32[512,512]{1,0:T(8,128)S(1)}, f32[4,48,128]{2,1,0:T(8,128)S(1)}, f32[6,512]{1,0:T(8,128)S(1)}) custom-call(s32[5]{0:T(128)S(1)} %pad_add_fusion.refs_0_, bf16[512,1024]{1,0:T(8,128)(2,1)S(1)} %get-tuple-element.185.refs_1_, ...), custom_call_target="tpu_custom_call" | custom-call | tf_op jit(solution)/shard_map/project_time/pallas_call | solution.py:37
  59.3 2.7 collective-permute-start.9
  64.6 10.9 %collective-permute-done.10.refs_6_.refs_11_ = bf16[256,2560]{1,0:T(8,128)(2,1)S(1)} collective-permute-done((bf16[256,2560]{1,0:T(8,128)(2,1)S(1)}, bf16[256,2560]{1,0:T(8,128)(2,1)S(1)}, u32[]{:S(2)}, u32[]{:S(2)}) %collective-permute-start.10) | collective-permute-done | bytes 1310752 | tf_op jit(solution)/shard_map/ppermute | solution.py:83
  76.2 4.7 %sweep_time.1 = (f32[512,256]{1,0:T(8,128)S(1)}, f32[512,256]{1,0:T(8,128)S(1)}, f32[512,256]{1,0:T(8,128)S(1)}, f32[512,256]{1,0:T(8,128)S(1)}) custom-call(s32[5]{0:T(128)S(1)} %pad_add_fusion.refs_0_, f32[4,512,128]{2,1,0:T(8,128)S(1)} %get-tuple-element.191.refs_1_.refs_0_, f32[4,512,128]{2,1,0:T(8,128)S(1)} %get-tuple-element.192.refs_2_.refs_1_.refs_3_, ...), custom_call_target="tpu_custom_call" | custom-call | tf_op jit(solution)/shard_map/sweep_time/pallas_call | solution.py:37
  81.6 13.4 %collective-permute-done.16.refs_3_.refs_16_ = bf16[2048,256]{1,0:T(8,128)(2,1)S(1)} collective-permute-done((bf16[2048,256]{1,0:T(8,128)(2,1)S(1)}, bf16[2048,256]{1,0:T(8,128)(2,1)S(1)}, u32[]{:S(2)}, u32[]{:S(2)}) %collective-permute-start.16) | collective-permute-done | bytes 1048608 | tf_op jit(solution)/shard_map/ppermute | solution.py:83
  99.9 3.3 %middle_norm.1 = (f32[512,512]{1,0:T(8,128)S(1)}, f32[512,1024]{1,0:T(8,128)S(1)}, f32[512,1]{1,0:T(8,128)S(1)}, f32[2,1024]{1,0:T(2,128)S(1)}) custom-call(bf16[512,512]{1,0:T(8,128)(2,1)} %bitcast.4.refs_1_.refs_0_, bf16[512,512]{1,0:T(8,128)(2,1)} %collective-permute-done.refs_2_.refs_1_, f32[512,256]{1,0:T(8,128)S(1)} %get-tuple-element.201.refs_2_, ...), custom_call_target="tpu_custom_call" | custom-call | tf_op jit(solution)/shard_map/middle_norm/pallas_call | solution.py:37
  103.1 3.7 %collective-permute-start.18 = (f32[2,1024]{1,0:T(2,128)S(1)}, f32[2,1024]{1,0:T(2,128)S(1)}, u32[]{:S(2)}, u32[]{:S(2)}) collective-permute-start(f32[2,1024]{1,0:T(2,128)S(1)} %get-tuple-element.207), channel_id=1, source_target_pairs={{0,2},{2,4},{4,6},{1,3},{3,5},{5,7},{8,10},{10,12},{12,14},{9,11},... | collective-permute-start | bytes 24584 | tf_op jit(solution)/shard_map/ppermute | solution.py:90
  108.0 4.7 %collective-permute-done.19.refs_8_.refs_13_ = bf16[256,1280]{1,0:T(8,128)(2,1)S(1)} collective-permute-done((bf16[256,1280]{1,0:T(8,128)(2,1)S(1)}, bf16[256,1280]{1,0:T(8,128)(2,1)S(1)}, u32[]{:S(2)}, u32[]{:S(2)}) %collective-permute-start.19) | collective-permute-done | bytes 655392 | tf_op jit(solution)/shard_map/ppermute | solution.py:83
  113.6 5.0 %channel_forward.1 = (bf16[512,1024]{1,0:T(8,128)(2,1)S(1)}, bf16[512,1024]{1,0:T(8,128)(2,1)S(1)}, bf16[512,1024]{1,0:T(8,128)(2,1)S(1)}, bf16[512,1024]{1,0:T(...) custom-call(s32[5]{0:T(128)S(1)} %pad_add_fusion.refs_0_, ...), custom_call_target="tpu_custom_call" | custom-call | tf_op jit(solution)/shard_map/channel_forward/pallas_call | solution.py:37
  120.1 3.2 %channel_return.1 = (f32[512,256]{1,0:T(8,128)S(1)}, f32[512,256]{1,0:T(8,128)S(1)}, bf16[512,256]{1,0:T(8,128)(2,1)S(1)}, bf16[512,256]{1,0:T(8,128)(2,1)S(1)}) custom-call(s32[5]{0:T(128)S(1)} %pad_add_fusion.refs_0_, bf16[512,2048]{1,0:T(8,128)(2,1)S(1)} %get-tuple-element.208.refs_1_.refs_3_, bf16[2048,256]{1,0:T(8,128)(2,1)S(1)} %copy-done, ...), custom_call_target="tpu_custom_call" | custom-call | tf_op jit(solution)/shard_map/channel_return/pallas_call | solution.py:37
  129.2 4.2 %weight_products.4 = (bf16[512,1024]{1,0:T(8,128)(2,1)S(1)}, bf16[512,1024]{1,0:T(8,128)(2,1)S(1)}, bf16[512,1024]{1,0:T(8,128)(2,1)}, bf16[512,1024]{1,0:T(8,128)(2,1)S(1)}) custom-call(s32[5]{0:T(128)S(1)} %pad_add_fusion.refs_0_, bf16[512,512]{1,0:T(8,128)(2,1)S(1)} %get-tuple-element.216.refs_1_, bf16[512,512]{1,0:T(8,128)(2,1)S(1)} %collective-permute-done.25.refs_2_, ...), custom_call_target="tpu_custom_call" | custom-call | tf_op jit(solution)/shard_map/weight_products/pallas_call | solution.py:37
  135.2 3.1 %sweep_again.1 = (bf16[512,512]{1,0:T(8,128)(2,1)S(1)}, f32[4,512,128]{2,1,0:T(8,128)S(1)}, f32[512,512]{1,0:T(8,128)S(1)}, f32[512,512]{1,0:T(8,128)S(1)}, f32[...) custom-call(f32[4,512,128]{2,1,0:T(8,128)S(1)} %get-tuple-element.19, ...), custom_call_target="tpu_custom_call" | custom-call | tf_op jit(solution)/shard_map/sweep_again/pallas_call | solution.py:37
  138.3 4.9 %mix_time.3 = (bf16[512,1024]{1,0:T(8,128)(2,1)S(1)}, bf16[512,1024]{1,0:T(8,128)(2,1)S(1)}, bf16[512,1024]{1,0:T(8,128)(2,1)S(1)}, bf16[512,1024]{1,0:T(8,128)(...) custom-call(s32[5]{0:T(128)S(1)} %pad_add_fusion.refs_0_, ...), custom_call_target="tpu_custom_call" | custom-call | tf_op jit(solution)/shard_map/mix_time/pallas_call | solution.py:37
  143.2 9.0 %channel_backward.1 = (bf16[512,2048]{1,0:T(8,128)(2,1)S(1)}, f32[512,256]{1,0:T(8,128)S(1)}, f32[512,256]{1,0:T(8,128)S(1)}, f32[512,256]{1,0:T(8,128)S(1)}, f3...) custom-call(s32[5]{0:T(128)S(1)} %pad_add_fusion.refs_0_, ...), custom_call_target="tpu_custom_call" | custom-call | tf_op jit(solution)/shard_map/channel_backward/pallas_call | solution.py:37
  154.8 3.8 %weight_products.5 = (bf16[512,1280]{1,0:T(8,128)(2,1)S(1)}, bf16[512,1280]{1,0:T(8,128)(2,1)S(1)}, bf16[512,1280]{1,0:T(8,128)(2,1)S(1)}, bf16[512,1280]{1,0:T(8,128)(2,1)S(1)}) custom-call(s32[5]{0:T(128)S(1)} %pad_add_fusion.refs_0_, bf16[512,1024]{1,0:T(8,128)(2,1)S(1)} %copy-done.3, bf16[512,1024]{1,0:T(8,128)(2,1)S(1)} %copy-done.5, ...), custom_call_target="tpu_custom_call" | custom-call | tf_op jit(solution)/shard_map/weight_products/pallas_call | solution.py:37
  163.4 2.9 collective-permute-done.32.refs_9_
  172.3 6.6 %middle_backward.1 = (bf16[512,1024]{1,0:T(8,128)(2,1)S(1)}, f32[512,512]{1,0:T(8,128)S(1)}, f32[4,512,128]{2,1,0:T(8,128)S(1)}, bf16[512,512]{1,0:T(8,128)(2,1)...) custom-call(s32[5]{0:T(128)S(1)} %pad_add_fusion.refs_0_, f32[512,256]{1,0:T(8,128)S(1)} %get-tuple-element.230.refs_1_, ...), custom_call_target="tpu_custom_call" | custom-call | tf_op jit(solution)/shard_map/middle_backward/pallas_call | solution.py:37
  183.2 2.9 collective-permute-start.35
  196.9 10.7 %time_backward.1 = (bf16[512,512]{1,0:T(8,128)(2,1)S(1)}, bf16[512,512]{1,0:T(8,128)(2,1)S(1)}, f32[512,512]{1,0:T(8,128)S(1)}, f32[512,256]{1,0:T(8,128)S(1)}, ...) custom-call(s32[5]{0:T(128)S(1)} %pad_add_fusion.refs_0_, ...), custom_call_target="tpu_custom_call" | custom-call | tf_op jit(solution)/shard_map/time_backward/pallas_call | solution.py:37
  210.4 2.7 collective-permute-done.39.refs_5_
  214.1 2.7 collective-permute-start.57
  223.4 6.0 %collective-permute-done.57.refs_1_ = bf16[128,2048]{1,0:T(8,128)(2,1)S(1)} collective-permute-done((bf16[128,2048]{1,0:T(8,128)(2,1)S(1)}, bf16[128,2048]{1,0:T(8,128)(2,1)S(1)}, u32[]{:S(2)}, u32[]{:S(2)}) %collective-permute-start.57) | collective-permute-done | bytes 524320 | tf_op jit(solution)/shard_map/ppermute | solution.py:83
  230.2 5.1 %collective-permute-done.49.refs_3_ = bf16[512,512]{1,0:T(8,128)(2,1)S(1)} collective-permute-done((bf16[512,512]{1,0:T(8,128)(2,1)S(1)}, bf16[512,512]{1,0:T(8,128)(2,1)S(1)}, u32[]{:S(2)}, u32[]{:S(2)}) %collective-permute-start.49) | collective-permute-done | bytes 524320 | tf_op jit(solution)/shard_map/ppermute | solution.py:83
  238.3 8.3 %collective-permute-done.54.refs_1_ = bf16[512,512]{1,0:T(8,128)(2,1)S(1)} collective-permute-done((bf16[512,512]{1,0:T(8,128)(2,1)S(1)}, bf16[512,512]{1,0:T(8,128)(2,1)S(1)}, u32[]{:S(2)}, u32[]{:S(2)}) %collective-permute-start.54) | collective-permute-done | bytes 524320 | tf_op jit(solution)/shard_map/ppermute | solution.py:83
  250.8 4.9 %collective-permute-done.51.refs_3_ = bf16[256,512]{1,0:T(8,128)(2,1)S(1)} collective-permute-done((bf16[256,512]{1,0:T(8,128)(2,1)S(1)}, bf16[256,512]{1,0:T(8,128)(2,1)S(1)}, u32[]{:S(2)}, u32[]{:S(2)}) %collective-permute-start.51) | collective-permute-done | bytes 262176 | tf_op jit(solution)/shard_map/ppermute | solution.py:83
  260.3 8.7 %collective-permute-done.52.refs_1_ = bf16[160,1024]{1,0:T(8,128)(2,1)S(1)} collective-permute-done((bf16[160,1024]{1,0:T(8,128)(2,1)S(1)}, bf16[160,1024]{1,0:T(8,128)(2,1)S(1)}, u32[]{:S(2)}, u32[]{:S(2)}) %collective-permute-start.52) | collective-permute-done | bytes 327712 | tf_op jit(solution)/shard_map/ppermute | solution.py:83
  278.6 11.9 %collective-permute-done.63.refs_1_ = bf16[64,2560]{1,0:T(8,128)(2,1)S(1)} collective-permute-done((bf16[64,2560]{1,0:T(8,128)(2,1)S(1)}, bf16[64,2560]{1,0:T(8,128)(2,1)S(1)}, u32[]{:S(2)}, u32[]{:S(2)}) %collective-permute-start.63) | collective-permute-done | bytes 327712 | tf_op jit(solution)/shard_map/ppermute | solution.py:83
  (192 shorter events, 110.6 us)
Async XLA Ops:
  2.2 26.2 %collective-permute-start.3 = (bf16[256,2048]{1,0:T(8,128)(2,1)S(1)}, bf16[256,2048]{1,0:T(8,128)(2,1)S(1)}, u32[]{:S(2)}, u32[]{:S(2)}) collective-permute-start(bf16[256,2048]{1,0:T(8,128)(2,1)S(1)} %pack_time.1.refs_5_.refs_8_.refs_22_.refs_20_), channel_id=1, source_target_pairs={{0,8},{8,0},{16,24},{24,16},{1,9},{9,1},{17,25},{25,17},{2,10},{10... | collective-permute-start | bytes 3145736 | tf_op jit(solution)/shard_map/ppermute | solution.py:83
  5.2 24.6 %collective-permute-start.4 = (bf16[256,2048]{1,0:T(8,128)(2,1)S(1)}, bf16[256,2048]{1,0:T(8,128)(2,1)S(1)}, u32[]{:S(2)}, u32[]{:S(2)}) collective-permute-start(bf16[256,2048]{1,0:T(8,128)(2,1)S(1)} %pack_time.1.refs_5_.refs_8_.refs_22_.refs_20_), channel_id=1, source_target_pairs={{0,16},{8,24},{16,0},{24,8},{1,17},{9,25},{17,1},{25,9},{2,18},{10... | collective-permute-start | bytes 3145736 | tf_op jit(solution)/shard_map/ppermute | solution.py:83
  43.8 31.7 %collective-permute-start.10 = (bf16[256,2560]{1,0:T(8,128)(2,1)S(1)}, bf16[256,2560]{1,0:T(8,128)(2,1)S(1)}, u32[]{:S(2)}, u32[]{:S(2)}) collective-permute-start(bf16[256,2560]{1,0:T(8,128)(2,1)S(1)} %pack.1.refs_5_.refs_10_), channel_id=1, source_target_pairs={{0,8},{8,0},{16,24},{24,16},{1,9},{9,1},{17,25},{25,17},{2,10},{10... | collective-permute-start | bytes 3932168 | tf_op jit(solution)/shard_map/ppermute | solution.py:83
  44.4 31.7 %collective-permute-start.11 = (bf16[256,2560]{1,0:T(8,128)(2,1)S(1)}, bf16[256,2560]{1,0:T(8,128)(2,1)S(1)}, u32[]{:S(2)}, u32[]{:S(2)}) collective-permute-start(bf16[256,2560]{1,0:T(8,128)(2,1)S(1)} %pack.1.refs_5_.refs_10_), channel_id=1, source_target_pairs={{0,16},{8,24},{16,0},{24,8},{1,17},{9,25},{17,1},{25,9},{2,18},{10... | collective-permute-start | bytes 3932168 | tf_op jit(solution)/shard_map/ppermute | solution.py:83
  45.0 50.0 %collective-permute-start.16 = (bf16[2048,256]{1,0:T(8,128)(2,1)S(1)}, bf16[2048,256]{1,0:T(8,128)(2,1)S(1)}, u32[]{:S(2)}, u32[]{:S(2)}) collective-permute-start(bf16[2048,256]{1,0:T(8,128)(2,1)S(1)} %copy-done), channel_id=1, source_target_pairs={{0,8},{8,0},{16,24},{24,16},{1,9},{9,1},{17,25},{25,17},{2,10},{10... | collective-permute-start | bytes 3145736 | tf_op jit(solution)/shard_map/ppermute | solution.py:83
  46.3 49.6 %collective-permute-start.17 = (bf16[2048,256]{1,0:T(8,128)(2,1)S(1)}, bf16[2048,256]{1,0:T(8,128)(2,1)S(1)}, u32[]{:S(2)}, u32[]{:S(2)}) collective-permute-start(bf16[2048,256]{1,0:T(8,128)(2,1)S(1)} %copy-done), channel_id=1, source_target_pairs={{0,16},{8,24},{16,0},{24,8},{1,17},{9,25},{17,1},{25,9},{2,18},{10... | collective-permute-start | bytes 3145736 | tf_op jit(solution)/shard_map/ppermute | solution.py:83
  80.9 17.0 %collective-permute-start.12 = (f32[512,256]{1,0:T(8,128)S(1)}, f32[512,256]{1,0:T(8,128)S(1)}, u32[]{:S(2)}, u32[]{:S(2)}) collective-permute-start(f32[512,256]{1,0:T(8,128)S(1)} %get-tuple-element.203.refs_4_), channel_id=1, source_target_pairs={{0,1},{1,0},{2,3},{3,2},{4,5},{5,4},{6,7},{7,6},{8,9},{9,8},{10,11... | collective-permute-start | bytes 1572872 | tf_op jit(solution)/shard_map/ppermute | solution.py:83
  81.0 17.1 %collective-permute-start.13 = (f32[512,256]{1,0:T(8,128)S(1)}, f32[512,256]{1,0:T(8,128)S(1)}, u32[]{:S(2)}, u32[]{:S(2)}) collective-permute-start(f32[512,256]{1,0:T(8,128)S(1)} %get-tuple-element.204.refs_5_), channel_id=1, source_target_pairs={{0,1},{1,0},{2,3},{3,2},{4,5},{5,4},{6,7},{7,6},{8,9},{9,8},{10,11... | collective-permute-start | bytes 1572872 | tf_op jit(solution)/shard_map/ppermute | solution.py:83
  81.5 16.7 %collective-permute-start.14 = (f32[512,256]{1,0:T(8,128)S(1)}, f32[512,256]{1,0:T(8,128)S(1)}, u32[]{:S(2)}, u32[]{:S(2)}) collective-permute-start(f32[512,256]{1,0:T(8,128)S(1)} %get-tuple-element.201.refs_2_), channel_id=1, source_target_pairs={{0,1},{1,0},{2,3},{3,2},{4,5},{5,4},{6,7},{7,6},{8,9},{9,8},{10,11... | collective-permute-start | bytes 1572872 | tf_op jit(solution)/shard_map/ppermute | solution.py:83
  95.0 17.7 %collective-permute-start.19 = (bf16[256,1280]{1,0:T(8,128)(2,1)S(1)}, bf16[256,1280]{1,0:T(8,128)(2,1)S(1)}, u32[]{:S(2)}, u32[]{:S(2)}) collective-permute-start(bf16[256,1280]{1,0:T(8,128)(2,1)S(1)} %slice.67.refs_13_), channel_id=1, source_target_pairs={{0,16},{8,24},{16,0},{24,8},{1,17},{9,25},{17,1},{25,9},{2,18},{10... | collective-permute-start | bytes 1966088 | tf_op jit(solution)/shard_map/ppermute | solution.py:83
  96.0 17.7 %collective-permute-start.20 = (bf16[256,1280]{1,0:T(8,128)(2,1)S(1)}, bf16[256,1280]{1,0:T(8,128)(2,1)S(1)}, u32[]{:S(2)}, u32[]{:S(2)}) collective-permute-start(bf16[256,1280]{1,0:T(8,128)(2,1)S(1)} %slice.68.refs_14_), channel_id=1, source_target_pairs={{0,8},{8,0},{16,24},{24,16},{1,9},{9,1},{17,25},{25,17},{2,10},{10... | collective-permute-start | bytes 1966088 | tf_op jit(solution)/shard_map/ppermute | solution.py:83
  98.1 22.0 %collective-permute-start.21 = (bf16[1024,256]{1,0:T(8,128)(2,1)S(1)}, bf16[1024,256]{1,0:T(8,128)(2,1)S(1)}, u32[]{:S(2)}, u32[]{:S(2)}) collective-permute-start(bf16[1024,256]{1,0:T(8,128)(2,1)S(1)} %slice.85.refs_10_), channel_id=1, source_target_pairs={{0,16},{8,24},{16,0},{24,8},{1,17},{9,25},{17,1},{25,9},{2,18},{10... | collective-permute-start | bytes 1572872 | tf_op jit(solution)/shard_map/ppermute | solution.py:83
  98.1 21.9 %collective-permute-start.22 = (bf16[1024,256]{1,0:T(8,128)(2,1)S(1)}, bf16[1024,256]{1,0:T(8,128)(2,1)S(1)}, u32[]{:S(2)}, u32[]{:S(2)}) collective-permute-start(bf16[1024,256]{1,0:T(8,128)(2,1)S(1)} %slice.86.refs_11_), channel_id=1, source_target_pairs={{0,8},{8,0},{16,24},{24,16},{1,9},{9,1},{17,25},{25,17},{2,10},{10... | collective-permute-start | bytes 1572872 | tf_op jit(solution)/shard_map/ppermute | solution.py:83
  133.4 27.5 %collective-permute-start.26 = (bf16[512,1024]{1,0:T(8,128)(2,1)S(1)}, bf16[512,1024]{1,0:T(8,128)(2,1)S(1)}, u32[]{:S(2)}, u32[]{:S(2)}) collective-permute-start(bf16[512,1024]{1,0:T(8,128)(2,1)S(1)} %get-tuple-element.221.refs_20_), channel_id=1, source_target_pairs={{0,8},{8,0},{16,24},{24,16},{1,9},{9,1},{17,25},{25,17},{2,10},{10... | collective-permute-start | bytes 3145736 | tf_op jit(solution)/shard_map/ppermute | solution.py:83
  134.7 26.1 %collective-permute-start.27 = (bf16[512,1024]{1,0:T(8,128)(2,1)}, bf16[512,1024]{1,0:T(8,128)(2,1)}, u32[]{:S(2)}, u32[]{:S(2)}) collective-permute-start(bf16[512,1024]{1,0:T(8,128)(2,1)} %get-tuple-element.229), channel_id=1, source_target_pairs={{0,16},{8,24},{16,0},{24,8},{1,17},{9,25},{17,1},{25,9},{2,18},{10... | collective-permute-start | bytes 3145736 | tf_op jit(solution)/shard_map/ppermute | solution.py:83
  158.6 31.8 %collective-permute-start.44 = (bf16[512,1280]{1,0:T(8,128)(2,1)S(1)}, bf16[512,1280]{1,0:T(8,128)(2,1)S(1)}, u32[]{:S(2)}, u32[]{:S(2)}) collective-permute-start(bf16[512,1280]{1,0:T(8,128)(2,1)S(1)} %get-tuple-element.283), channel_id=1, source_target_pairs={{0,8},{8,0},{16,24},{24,16},{1,9},{9,1},{17,25},{25,17},{2,10},{10... | collective-permute-start | bytes 3932168 | tf_op jit(solution)/shard_map/ppermute | solution.py:83
  159.6 31.7 %collective-permute-start.45 = (bf16[512,1280]{1,0:T(8,128)(2,1)S(1)}, bf16[512,1280]{1,0:T(8,128)(2,1)S(1)}, u32[]{:S(2)}, u32[]{:S(2)}) collective-permute-start(bf16[512,1280]{1,0:T(8,128)(2,1)S(1)} %get-tuple-element.285), channel_id=1, source_target_pairs={{0,16},{8,24},{16,0},{24,8},{1,17},{9,25},{17,1},{25,9},{2,18},{10... | collective-permute-start | bytes 3932168 | tf_op jit(solution)/shard_map/ppermute | solution.py:83
  170.3 38.5 %collective-permute-start.42 = (bf16[256,1024]{1,0:T(8,128)(2,1)S(1)}, bf16[256,1024]{1,0:T(8,128)(2,1)S(1)}, u32[]{:S(2)}, u32[]{:S(2)}) collective-permute-start(bf16[256,1024]{1,0:T(8,128)(2,1)S(1)} %get-tuple-element.253.refs_28_), channel_id=1, source_target_pairs={{0,16},{8,24},{16,0},{24,8},{1,17},{9,25},{17,1},{25,9},{2,18},{10... | collective-permute-start | bytes 1572872 | tf_op jit(solution)/shard_map/ppermute | solution.py:83
  171.2 39.2 %collective-permute-start.43 = (bf16[256,1024]{1,0:T(8,128)(2,1)S(1)}, bf16[256,1024]{1,0:T(8,128)(2,1)S(1)}, u32[]{:S(2)}, u32[]{:S(2)}) collective-permute-start(bf16[256,1024]{1,0:T(8,128)(2,1)S(1)} %get-tuple-element.254.refs_29_), channel_id=1, source_target_pairs={{0,8},{8,0},{16,24},{24,16},{1,9},{9,1},{17,25},{25,17},{2,10},{10... | collective-permute-start | bytes 1572872 | tf_op jit(solution)/shard_map/ppermute | solution.py:83
  192.0 26.1 %collective-permute-start.46 = (bf16[256,1280]{1,0:T(8,128)(2,1)S(1)}, bf16[256,1280]{1,0:T(8,128)(2,1)S(1)}, u32[]{:S(2)}, u32[]{:S(2)}) collective-permute-start(bf16[256,1280]{1,0:T(8,128)(2,1)S(1)} %get-tuple-element.290), channel_id=1, source_target_pairs={{0,16},{8,24},{16,0},{24,8},{1,17},{9,25},{17,1},{25,9},{2,18},{10... | collective-permute-start | bytes 1966088 | tf_op jit(solution)/shard_map/ppermute | solution.py:83
  193.2 24.9 %collective-permute-start.47 = (bf16[256,1280]{1,0:T(8,128)(2,1)S(1)}, bf16[256,1280]{1,0:T(8,128)(2,1)S(1)}, u32[]{:S(2)}, u32[]{:S(2)}) collective-permute-start(bf16[256,1280]{1,0:T(8,128)(2,1)S(1)} %get-tuple-element.291), channel_id=1, source_target_pairs={{0,8},{8,0},{16,24},{24,16},{1,9},{9,1},{17,25},{25,17},{2,10},{10... | collective-permute-start | bytes 1966088 | tf_op jit(solution)/shard_map/ppermute | solution.py:83
  214.1 15.4 %collective-permute-start.57 = (bf16[128,2048]{1,0:T(8,128)(2,1)S(1)}, bf16[128,2048]{1,0:T(8,128)(2,1)S(1)}, u32[]{:S(2)}, u32[]{:S(2)}) collective-permute-start(bf16[128,2048]{1,0:T(8,128)(2,1)S(1)} %get-tuple-element.322), channel_id=1, source_target_pairs={{0,2},{2,0},{4,6},{6,4},{1,3},{3,1},{5,7},{7,5},{8,10},{10,8},{12,... | collective-permute-start | bytes 1572872 | tf_op jit(solution)/shard_map/ppermute | solution.py:83
  221.0 15.5 %collective-permute-start.48 = (bf16[544,512]{1,0:T(8,128)(2,1)S(1)}, bf16[544,512]{1,0:T(8,128)(2,1)S(1)}, u32[]{:S(2)}, u32[]{:S(2)}) collective-permute-start(bf16[544,512]{1,0:T(8,128)(2,1)S(1)} %get-tuple-element.293), channel_id=1, source_target_pairs={{0,8},{8,0},{16,24},{24,16},{1,9},{9,1},{17,25},{25,17},{2,10},{10... | collective-permute-start | bytes 1671176 | tf_op jit(solution)/shard_map/ppermute | solution.py:83
  222.0 24.6 %collective-permute-start.54 = (bf16[512,512]{1,0:T(8,128)(2,1)S(1)}, bf16[512,512]{1,0:T(8,128)(2,1)S(1)}, u32[]{:S(2)}, u32[]{:S(2)}) collective-permute-start(bf16[512,512]{1,0:T(8,128)(2,1)S(1)} %get-tuple-element.309), channel_id=1, source_target_pairs={{0,8},{8,0},{16,24},{24,16},{1,9},{9,1},{17,25},{25,17},{2,10},{10... | collective-permute-start | bytes 1572872 | tf_op jit(solution)/shard_map/ppermute | solution.py:83
  223.3 25.5 %collective-permute-start.56 = (bf16[128,2560]{1,0:T(8,128)(2,1)S(1)}, bf16[128,2560]{1,0:T(8,128)(2,1)S(1)}, u32[]{:S(2)}, u32[]{:S(2)}) collective-permute-start(bf16[128,2560]{1,0:T(8,128)(2,1)S(1)} %get-tuple-element.314), channel_id=1, source_target_pairs={{0,2},{2,0},{4,6},{6,4},{1,3},{3,1},{5,7},{7,5},{8,10},{10,8},{12,... | collective-permute-start | bytes 1966088 | tf_op jit(solution)/shard_map/ppermute | solution.py:83
  229.5 18.1 %collective-permute-start.55 = (bf16[512,512]{1,0:T(8,128)(2,1)S(1)}, bf16[512,512]{1,0:T(8,128)(2,1)S(1)}, u32[]{:S(2)}, u32[]{:S(2)}) collective-permute-start(bf16[512,512]{1,0:T(8,128)(2,1)S(1)} %get-tuple-element.311), channel_id=1, source_target_pairs={{0,16},{8,24},{16,0},{24,8},{1,17},{9,25},{17,1},{25,9},{2,18},{10... | collective-permute-start | bytes 1572872 | tf_op jit(solution)/shard_map/ppermute | solution.py:83
  236.7 19.0 %collective-permute-start.50 = (bf16[288,512]{1,0:T(8,128)(2,1)S(1)}, bf16[288,512]{1,0:T(8,128)(2,1)S(1)}, u32[]{:S(2)}, u32[]{:S(2)}) collective-permute-start(bf16[288,512]{1,0:T(8,128)(2,1)S(1)} %get-tuple-element.298), channel_id=1, source_target_pairs={{0,16},{8,24},{16,0},{24,8},{1,17},{9,25},{17,1},{25,9},{2,18},{10... | collective-permute-start | bytes 884744 | tf_op jit(solution)/shard_map/ppermute | solution.py:83
  256.0 19.1 %collective-permute-start.36 = (f32[512,256]{1,0:T(8,128)S(1)}, f32[512,256]{1,0:T(8,128)S(1)}, u32[]{:S(2)}, u32[]{:S(2)}) collective-permute-start(f32[512,256]{1,0:T(8,128)S(1)} %get-tuple-element.272), channel_id=1, source_target_pairs={{0,1},{1,0},{2,3},{3,2},{4,5},{5,4},{6,7},{7,6},{8,9},{9,8},{10,11... | collective-permute-start | bytes 1572872 | tf_op jit(solution)/shard_map/ppermute | solution.py:83
  256.0 19.1 %collective-permute-start.37 = (f32[512,256]{1,0:T(8,128)S(1)}, f32[512,256]{1,0:T(8,128)S(1)}, u32[]{:S(2)}, u32[]{:S(2)}) collective-permute-start(f32[512,256]{1,0:T(8,128)S(1)} %get-tuple-element.273), channel_id=1, source_target_pairs={{0,1},{1,0},{2,3},{3,2},{4,5},{5,4},{6,7},{7,6},{8,9},{9,8},{10,11... | collective-permute-start | bytes 1572872 | tf_op jit(solution)/shard_map/ppermute | solution.py:83
  269.0 21.5 %collective-permute-start.63 = (bf16[64,2560]{1,0:T(8,128)(2,1)S(1)}, bf16[64,2560]{1,0:T(8,128)(2,1)S(1)}, u32[]{:S(2)}, u32[]{:S(2)}) collective-permute-start(bf16[64,2560]{1,0:T(8,128)(2,1)S(1)} %get-tuple-element.346), channel_id=1, source_target_pairs={{0,4},{2,6},{4,0},{6,2},{1,5},{3,7},{5,1},{7,3},{8,12},{10,14},{12... | collective-permute-start | bytes 983048 | tf_op jit(solution)/shard_map/ppermute | solution.py:83
  272.1 22.6 %collective-permute-start.53 = (bf16[96,1024]{1,0:T(8,128)(2,1)S(1)}, bf16[96,1024]{1,0:T(8,128)(2,1)S(1)}, u32[]{:S(2)}, u32[]{:S(2)}) collective-permute-start(bf16[96,1024]{1,0:T(8,128)(2,1)S(1)} %get-tuple-element.306), channel_id=1, source_target_pairs={{0,4},{2,6},{4,0},{6,2},{1,5},{3,7},{5,1},{7,3},{8,12},{10,14},{12... | collective-permute-start | bytes 589832 | tf_op jit(solution)/shard_map/ppermute | solution.py:83
  272.9 21.0 %collective-permute-start.62 = (bf16[64,1024]{1,0:T(8,128)(2,1)S(1)}, bf16[64,1024]{1,0:T(8,128)(2,1)S(1)}, u32[]{:S(2)}, u32[]{:S(2)}) collective-permute-start(bf16[64,1024]{1,0:T(8,128)(2,1)S(1)} %get-tuple-element.339), channel_id=1, source_target_pairs={{0,4},{2,6},{4,0},{6,2},{1,5},{3,7},{5,1},{7,3},{8,12},{10,14},{12... | collective-permute-start | bytes 393224 | tf_op jit(solution)/shard_map/ppermute | solution.py:83
  (52 other events, 362.9 us)

commit v5 on v4

--- a/solution.py
+++ b/solution.py
@@ -807,9 +807,11 @@
             + ([((VR, H), F32)] if extra else []),
         )
 
-    def scatter_line(send, keep, *mine, widths, seen=None):
+    def scatter_line(send, keep, *mine, widths, seen=None, behind=None):
         extra = 2 * VR if mine else 0
         for bit in range(bits_of(C)):
+            if behind is not None and bit + 1 == bits_of(C):
+                send = hold(send, behind)
             got = swap(send, "ctx", 1 << bit)
             if seen is not None:
                 seen.append(got)
@@ -1320,7 +1322,7 @@
     early_cross = square_cross(*square_turn(hold(early_state, hidden_seen[0], return_seen[-1])))
     late_cross = square_cross(*square_turn(late_state))
     early_seen = []
-    output_w, gate_w = scatter_line(*square_end(hold(early_cross, late_cross[1], late_cross[3])), widths=[H, H], seen=early_seen)
+    output_w, gate_w = scatter_line(*square_end(hold(early_cross, late_cross[1], late_cross[3])), widths=[H, H], behind=hidden_seen[-1], seen=early_seen)
     key_w, value_w, vectors = scatter_line(*square_end(late_cross), widths=[H, H])
     shape = block_entries.shape
     return (

time: 297 us -> 293 us (0.987)
  waiting for transfers between devices: 135 us -> 130 us
    ppermute x58, waiting for transfers between devices: 125 us -> 120 us  [swap(): return lax.ppermute(value, axis, [(i, i ^ step) for i in range(size)])]
  transfers between devices with their start and end apart: 64 -> 64, of which waited for: 43 -> 41; matrix products, arithmetic and copies ran while one was open for 1% -> 1% of each run, Pallas kernels for 27% -> 27%
where the time goes in v5:
time: 293 us; the launch traced here: 292 us
  waiting for transfers between devices  130 us (44%)
  Pallas kernels  90.6 us (31%)
  starting transfers between devices  65.2 us (22%)
  local copies, waits for them, and re-layouts  5.09 us (2%)
    ppermute x58, waiting for transfers between devices, swap(): return lax.ppermute(value, axis, [(i, i ^ step) for i in range(size)])  120 us
    pallas_call x39, Pallas kernels, launch(): pl.pallas_call(run, out_shape=[jax.ShapeDtypeStruct(shape, dtype) for sha...  90.6 us
    ppermute x58, starting transfers between devices, swap(): return lax.ppermute(value, axis, [(i, i ^ step) for i in range(size)])  52.6 us
    ppermute x4, starting transfers between devices, along_ctx(): return lax.ppermute(value, 'ctx', pairs)  9.73 us
    ppermute x4, waiting for transfers between devices, along_ctx(): return lax.ppermute(value, 'ctx', pairs)  7.99 us
  transfers between devices with their start and end apart: 64, of which 41 were waited for; matrix products, arithmetic and copies ran while one was open for 1% of the time, Pallas kernels for 27%

profile of v5, /device:TPU:0, one launch (start us, length us, event | category | flops | bytes accessed | tf_op | source)
XLA Modules:
  0.0 292.5 jit_solution(2282147932654073793)
XLA Ops:
  2.2 3.0 %collective-permute-start.3 = (bf16[256,2048]{1,0:T(8,128)(2,1)S(1)}, bf16[256,2048]{1,0:T(8,128)(2,1)S(1)}, u32[]{:S(2)}, u32[]{:S(2)}) collective-permute-start(bf16[256,2048]{1,0:T(8,128)(2,1)S(1)} %pack_time.1.refs_5_.refs_8_.refs_22_.refs_20_), channel_id=1, source_target_pairs={{0,8},{8,0},{16,24},{24,16},{1,9},{9,1},{17,25},{25,17},{2,10},{10... | collective-permute-start | bytes 3145736 | tf_op jit(solution)/shard_map/ppermute | solution.py:83
  9.7 3.5 %collective-permute-start.1 = (bf16[2,1024]{1,0:T(2,128)(2,1)S(1)}, bf16[2,1024]{1,0:T(2,128)(2,1)S(1)}, u32[]{:S(2)}, u32[]{:S(2)}) collective-permute-start(bf16[2,1024]{1,0:T(2,128)(2,1)S(1)} %pad_maximum_fusion.1), channel_id=1, source_target_pairs={{0,2},{2,4},{4,6},{1,3},{3,5},{5,7},{8,10},{10,12},{12,14},{9,11},... | collective-permute-start | bytes 12296 | tf_op jit(solution)/shard_map/ppermute | solution.py:90
  14.5 5.8 %mix_time.2 = (bf16[512,1024]{1,0:T(8,128)(2,1)S(1)}, bf16[512,1024]{1,0:T(8,128)(2,1)S(1)}, bf16[512,1024]{1,0:T(8,128)(2,1)S(1)}, bf16[512,1024]{1,0:T(8,128)(...) custom-call(s32[5]{0:T(128)S(1)} %pad_add_fusion.refs_0_, ...), custom_call_target="tpu_custom_call" | custom-call | tf_op jit(solution)/shard_map/mix_time/pallas_call | solution.py:37
  20.3 8.0 %collective-permute-done.3.refs_6_.refs_9_.refs_23_.refs_21_ = bf16[256,2048]{1,0:T(8,128)(2,1)S(1)} collective-permute-done((bf16[256,2048]{1,0:T(8,128)(2,1)S(1)}, bf16[256,2048]{1,0:T(8,128)(2,1)S(1)}, u32[]{:S(2)}, u32[]{:S(2)}) %collective-permute-start.3) | collective-permute-done | bytes 1048608 | tf_op jit(solution)/shard_map/ppermute | solution.py:83
  33.4 9.0 %collective-permute-done.5.refs_8_.refs_11_.refs_25_.refs_23_ = bf16[256,1024]{1,0:T(8,128)(2,1)S(1)} collective-permute-done((bf16[256,1024]{1,0:T(8,128)(2,1)S(1)}, bf16[256,1024]{1,0:T(8,128)(2,1)S(1)}, u32[]{:S(2)}, u32[]{:S(2)}) %collective-permute-start.5) | collective-permute-done | bytes 524320 | tf_op jit(solution)/shard_map/ppermute | solution.py:83
  49.8 5.1 %project_time.1 = (f32[4,512,128]{2,1,0:T(8,128)S(1)}, f32[4,512,128]{2,1,0:T(8,128)S(1)}, f32[512,512]{1,0:T(8,128)S(1)}, f32[4,48,128]{2,1,0:T(8,128)S(1)}, f32[6,512]{1,0:T(8,128)S(1)}) custom-call(s32[5]{0:T(128)S(1)} %pad_add_fusion.refs_0_, bf16[512,1024]{1,0:T(8,128)(2,1)S(1)} %get-tuple-element.186.refs_1_, ...), custom_call_target="tpu_custom_call" | custom-call | tf_op jit(solution)/shard_map/project_time/pallas_call | solution.py:37
  64.6 10.9 %collective-permute-done.10.refs_6_.refs_11_ = bf16[256,2560]{1,0:T(8,128)(2,1)S(1)} collective-permute-done((bf16[256,2560]{1,0:T(8,128)(2,1)S(1)}, bf16[256,2560]{1,0:T(8,128)(2,1)S(1)}, u32[]{:S(2)}, u32[]{:S(2)}) %collective-permute-start.10) | collective-permute-done | bytes 1310752 | tf_op jit(solution)/shard_map/ppermute | solution.py:83
  76.2 4.7 %sweep_time.1 = (f32[512,256]{1,0:T(8,128)S(1)}, f32[512,256]{1,0:T(8,128)S(1)}, f32[512,256]{1,0:T(8,128)S(1)}, f32[512,256]{1,0:T(8,128)S(1)}) custom-call(s32[5]{0:T(128)S(1)} %pad_add_fusion.refs_0_, f32[4,512,128]{2,1,0:T(8,128)S(1)} %get-tuple-element.192.refs_1_.refs_0_, f32[4,512,128]{2,1,0:T(8,128)S(1)} %get-tuple-element.193.refs_2_.refs_1_.refs_3_, ...), custom_call_target="tpu_custom_call" | custom-call | tf_op jit(solution)/shard_map/sweep_time/pallas_call | solution.py:37
  81.6 13.4 %collective-permute-done.16.refs_3_.refs_16_ = bf16[2048,256]{1,0:T(8,128)(2,1)S(1)} collective-permute-done((bf16[2048,256]{1,0:T(8,128)(2,1)S(1)}, bf16[2048,256]{1,0:T(8,128)(2,1)S(1)}, u32[]{:S(2)}, u32[]{:S(2)}) %collective-permute-start.16) | collective-permute-done | bytes 1048608 | tf_op jit(solution)/shard_map/ppermute | solution.py:83
  99.9 3.3 %middle_norm.1 = (f32[512,512]{1,0:T(8,128)S(1)}, f32[512,1024]{1,0:T(8,128)S(1)}, f32[512,1]{1,0:T(8,128)S(1)}, f32[2,1024]{1,0:T(2,128)S(1)}) custom-call(bf16[512,512]{1,0:T(8,128)(2,1)} %bitcast.4.refs_1_.refs_0_, bf16[512,512]{1,0:T(8,128)(2,1)} %collective-permute-done.refs_2_.refs_1_, f32[512,256]{1,0:T(8,128)S(1)} %get-tuple-element.202.refs_2_, ...), custom_call_target="tpu_custom_call" | custom-call | tf_op jit(solution)/shard_map/middle_norm/pallas_call | solution.py:37
  103.1 3.7 %collective-permute-start.18 = (f32[2,1024]{1,0:T(2,128)S(1)}, f32[2,1024]{1,0:T(2,128)S(1)}, u32[]{:S(2)}, u32[]{:S(2)}) collective-permute-start(f32[2,1024]{1,0:T(2,128)S(1)} %get-tuple-element.208), channel_id=1, source_target_pairs={{0,2},{2,4},{4,6},{1,3},{3,5},{5,7},{8,10},{10,12},{12,14},{9,11},... | collective-permute-start | bytes 24584 | tf_op jit(solution)/shard_map/ppermute | solution.py:90
  108.0 4.7 %collective-permute-done.19.refs_8_.refs_13_ = bf16[256,1280]{1,0:T(8,128)(2,1)S(1)} collective-permute-done((bf16[256,1280]{1,0:T(8,128)(2,1)S(1)}, bf16[256,1280]{1,0:T(8,128)(2,1)S(1)}, u32[]{:S(2)}, u32[]{:S(2)}) %collective-permute-start.19) | collective-permute-done | bytes 655392 | tf_op jit(solution)/shard_map/ppermute | solution.py:83
  113.6 5.0 %channel_forward.1 = (bf16[512,1024]{1,0:T(8,128)(2,1)S(1)}, bf16[512,1024]{1,0:T(8,128)(2,1)S(1)}, bf16[512,1024]{1,0:T(8,128)(2,1)S(1)}, bf16[512,1024]{1,0:T(...) custom-call(s32[5]{0:T(128)S(1)} %pad_add_fusion.refs_0_, ...), custom_call_target="tpu_custom_call" | custom-call | tf_op jit(solution)/shard_map/channel_forward/pallas_call | solution.py:37
  120.1 3.2 %channel_return.1 = (f32[512,256]{1,0:T(8,128)S(1)}, f32[512,256]{1,0:T(8,128)S(1)}, bf16[512,256]{1,0:T(8,128)(2,1)S(1)}, bf16[512,256]{1,0:T(8,128)(2,1)S(1)}) custom-call(s32[5]{0:T(128)S(1)} %pad_add_fusion.refs_0_, bf16[512,2048]{1,0:T(8,128)(2,1)S(1)} %get-tuple-element.209.refs_1_.refs_3_, bf16[2048,256]{1,0:T(8,128)(2,1)S(1)} %copy-done, ...), custom_call_target="tpu_custom_call" | custom-call | tf_op jit(solution)/shard_map/channel_return/pallas_call | solution.py:37
  129.2 4.2 %weight_products.4 = (bf16[512,1024]{1,0:T(8,128)(2,1)S(1)}, bf16[512,1024]{1,0:T(8,128)(2,1)S(1)}, bf16[512,1024]{1,0:T(8,128)(2,1)}, bf16[512,1024]{1,0:T(8,128)(2,1)S(1)}) custom-call(s32[5]{0:T(128)S(1)} %pad_add_fusion.refs_0_, bf16[512,512]{1,0:T(8,128)(2,1)S(1)} %get-tuple-element.217.refs_1_, bf16[512,512]{1,0:T(8,128)(2,1)S(1)} %collective-permute-done.25.refs_2_, ...), custom_call_target="tpu_custom_call" | custom-call | tf_op jit(solution)/shard_map/weight_products/pallas_call | solution.py:37
  135.2 3.1 %sweep_again.1 = (bf16[512,512]{1,0:T(8,128)(2,1)S(1)}, f32[4,512,128]{2,1,0:T(8,128)S(1)}, f32[512,512]{1,0:T(8,128)S(1)}, f32[512,512]{1,0:T(8,128)S(1)}, f32[...) custom-call(f32[4,512,128]{2,1,0:T(8,128)S(1)} %get-tuple-element.19, ...), custom_call_target="tpu_custom_call" | custom-call | tf_op jit(solution)/shard_map/sweep_again/pallas_call | solution.py:37
  138.3 4.9 %mix_time.3 = (bf16[512,1024]{1,0:T(8,128)(2,1)S(1)}, bf16[512,1024]{1,0:T(8,128)(2,1)S(1)}, bf16[512,1024]{1,0:T(8,128)(2,1)S(1)}, bf16[512,1024]{1,0:T(8,128)(...) custom-call(s32[5]{0:T(128)S(1)} %pad_add_fusion.refs_0_, ...), custom_call_target="tpu_custom_call" | custom-call | tf_op jit(solution)/shard_map/mix_time/pallas_call | solution.py:37
  143.2 9.0 %channel_backward.1 = (bf16[512,2048]{1,0:T(8,128)(2,1)S(1)}, f32[512,256]{1,0:T(8,128)S(1)}, f32[512,256]{1,0:T(8,128)S(1)}, f32[512,256]{1,0:T(8,128)S(1)}, f3...) custom-call(s32[5]{0:T(128)S(1)} %pad_add_fusion.refs_0_, ...), custom_call_target="tpu_custom_call" | custom-call | tf_op jit(solution)/shard_map/channel_backward/pallas_call | solution.py:37
  154.8 3.8 %weight_products.5 = (bf16[512,1280]{1,0:T(8,128)(2,1)S(1)}, bf16[512,1280]{1,0:T(8,128)(2,1)S(1)}, bf16[512,1280]{1,0:T(8,128)(2,1)S(1)}, bf16[512,1280]{1,0:T(8,128)(2,1)S(1)}) custom-call(s32[5]{0:T(128)S(1)} %pad_add_fusion.refs_0_, bf16[512,1024]{1,0:T(8,128)(2,1)S(1)} %copy-done.3, bf16[512,1024]{1,0:T(8,128)(2,1)S(1)} %copy-done.5, ...), custom_call_target="tpu_custom_call" | custom-call | tf_op jit(solution)/shard_map/weight_products/pallas_call | solution.py:37
  163.4 2.9 %collective-permute-done.32.refs_9_ = f32[2,1024]{1,0:T(2,128)S(1)} collective-permute-done((f32[2,1024]{1,0:T(2,128)S(1)}, f32[2,1024]{1,0:T(2,128)S(1)}, u32[]{:S(2)}, u32[]{:S(2)}) %collective-permute-start.32) | collective-permute-done | bytes 8224 | tf_op jit(solution)/shard_map/ppermute | solution.py:90
  172.3 6.6 %middle_backward.1 = (bf16[512,1024]{1,0:T(8,128)(2,1)S(1)}, f32[512,512]{1,0:T(8,128)S(1)}, f32[4,512,128]{2,1,0:T(8,128)S(1)}, bf16[512,512]{1,0:T(8,128)(2,1)...) custom-call(s32[5]{0:T(128)S(1)} %pad_add_fusion.refs_0_, f32[512,256]{1,0:T(8,128)S(1)} %get-tuple-element.231.refs_1_, ...), custom_call_target="tpu_custom_call" | custom-call | tf_op jit(solution)/shard_map/middle_backward/pallas_call | solution.py:37
  183.2 2.9 collective-permute-start.35
  196.9 10.7 %time_backward.1 = (bf16[512,512]{1,0:T(8,128)(2,1)S(1)}, bf16[512,512]{1,0:T(8,128)(2,1)S(1)}, f32[512,512]{1,0:T(8,128)S(1)}, f32[512,256]{1,0:T(8,128)S(1)}, ...) custom-call(s32[5]{0:T(128)S(1)} %pad_add_fusion.refs_0_, ...), custom_call_target="tpu_custom_call" | custom-call | tf_op jit(solution)/shard_map/time_backward/pallas_call | solution.py:37
  210.4 2.7 collective-permute-done.39.refs_5_
  214.1 2.7 collective-permute-start.57
  223.4 6.0 %collective-permute-done.57.refs_1_ = bf16[128,2048]{1,0:T(8,128)(2,1)S(1)} collective-permute-done((bf16[128,2048]{1,0:T(8,128)(2,1)S(1)}, bf16[128,2048]{1,0:T(8,128)(2,1)S(1)}, u32[]{:S(2)}, u32[]{:S(2)}) %collective-permute-start.57) | collective-permute-done | bytes 524320 | tf_op jit(solution)/shard_map/ppermute | solution.py:83
  230.2 5.1 %collective-permute-done.49.refs_3_ = bf16[512,512]{1,0:T(8,128)(2,1)S(1)} collective-permute-done((bf16[512,512]{1,0:T(8,128)(2,1)S(1)}, bf16[512,512]{1,0:T(8,128)(2,1)S(1)}, u32[]{:S(2)}, u32[]{:S(2)}) %collective-permute-start.49) | collective-permute-done | bytes 524320 | tf_op jit(solution)/shard_map/ppermute | solution.py:83
  238.3 8.3 %collective-permute-done.54.refs_1_ = bf16[512,512]{1,0:T(8,128)(2,1)S(1)} collective-permute-done((bf16[512,512]{1,0:T(8,128)(2,1)S(1)}, bf16[512,512]{1,0:T(8,128)(2,1)S(1)}, u32[]{:S(2)}, u32[]{:S(2)}) %collective-permute-start.54) | collective-permute-done | bytes 524320 | tf_op jit(solution)/shard_map/ppermute | solution.py:83
  250.8 4.9 %collective-permute-done.51.refs_3_ = bf16[256,512]{1,0:T(8,128)(2,1)S(1)} collective-permute-done((bf16[256,512]{1,0:T(8,128)(2,1)S(1)}, bf16[256,512]{1,0:T(8,128)(2,1)S(1)}, u32[]{:S(2)}, u32[]{:S(2)}) %collective-permute-start.51) | collective-permute-done | bytes 262176 | tf_op jit(solution)/shard_map/ppermute | solution.py:83
  260.9 6.8 %collective-permute-done.52.refs_1_ = bf16[160,1024]{1,0:T(8,128)(2,1)S(1)} collective-permute-done((bf16[160,1024]{1,0:T(8,128)(2,1)S(1)}, bf16[160,1024]{1,0:T(8,128)(2,1)S(1)}, u32[]{:S(2)}, u32[]{:S(2)}) %collective-permute-start.52) | collective-permute-done | bytes 327712 | tf_op jit(solution)/shard_map/ppermute | solution.py:83
  267.8 7.9 %collective-permute-done.61.refs_1_ = bf16[128,1024]{1,0:T(8,128)(2,1)S(1)} collective-permute-done((bf16[128,1024]{1,0:T(8,128)(2,1)S(1)}, bf16[128,1024]{1,0:T(8,128)(2,1)S(1)}, u32[]{:S(2)}, u32[]{:S(2)}) %collective-permute-start.61) | collective-permute-done | bytes 262176 | tf_op jit(solution)/shard_map/ppermute | solution.py:83
  283.0 7.4 %collective-permute-done.63.refs_1_ = bf16[64,1024]{1,0:T(8,128)(2,1)S(1)} collective-permute-done((bf16[64,1024]{1,0:T(8,128)(2,1)S(1)}, bf16[64,1024]{1,0:T(8,128)(2,1)S(1)}, u32[]{:S(2)}, u32[]{:S(2)}) %collective-permute-start.63) | collective-permute-done | bytes 131104 | tf_op jit(solution)/shard_map/ppermute | solution.py:83
  (192 shorter events, 108.2 us)
Async XLA Ops:
  2.2 26.2 %collective-permute-start.3 = (bf16[256,2048]{1,0:T(8,128)(2,1)S(1)}, bf16[256,2048]{1,0:T(8,128)(2,1)S(1)}, u32[]{:S(2)}, u32[]{:S(2)}) collective-permute-start(bf16[256,2048]{1,0:T(8,128)(2,1)S(1)} %pack_time.1.refs_5_.refs_8_.refs_22_.refs_20_), channel_id=1, source_target_pairs={{0,8},{8,0},{16,24},{24,16},{1,9},{9,1},{17,25},{25,17},{2,10},{10... | collective-permute-start | bytes 3145736 | tf_op jit(solution)/shard_map/ppermute | solution.py:83
  5.2 24.6 %collective-permute-start.4 = (bf16[256,2048]{1,0:T(8,128)(2,1)S(1)}, bf16[256,2048]{1,0:T(8,128)(2,1)S(1)}, u32[]{:S(2)}, u32[]{:S(2)}) collective-permute-start(bf16[256,2048]{1,0:T(8,128)(2,1)S(1)} %pack_time.1.refs_5_.refs_8_.refs_22_.refs_20_), channel_id=1, source_target_pairs={{0,16},{8,24},{16,0},{24,8},{1,17},{9,25},{17,1},{25,9},{2,18},{10... | collective-permute-start | bytes 3145736 | tf_op jit(solution)/shard_map/ppermute | solution.py:83
  43.8 31.7 %collective-permute-start.10 = (bf16[256,2560]{1,0:T(8,128)(2,1)S(1)}, bf16[256,2560]{1,0:T(8,128)(2,1)S(1)}, u32[]{:S(2)}, u32[]{:S(2)}) collective-permute-start(bf16[256,2560]{1,0:T(8,128)(2,1)S(1)} %pack.1.refs_5_.refs_10_), channel_id=1, source_target_pairs={{0,8},{8,0},{16,24},{24,16},{1,9},{9,1},{17,25},{25,17},{2,10},{10... | collective-permute-start | bytes 3932168 | tf_op jit(solution)/shard_map/ppermute | solution.py:83
  44.4 31.7 %collective-permute-start.11 = (bf16[256,2560]{1,0:T(8,128)(2,1)S(1)}, bf16[256,2560]{1,0:T(8,128)(2,1)S(1)}, u32[]{:S(2)}, u32[]{:S(2)}) collective-permute-start(bf16[256,2560]{1,0:T(8,128)(2,1)S(1)} %pack.1.refs_5_.refs_10_), channel_id=1, source_target_pairs={{0,16},{8,24},{16,0},{24,8},{1,17},{9,25},{17,1},{25,9},{2,18},{10... | collective-permute-start | bytes 3932168 | tf_op jit(solution)/shard_map/ppermute | solution.py:83
  45.0 50.0 %collective-permute-start.16 = (bf16[2048,256]{1,0:T(8,128)(2,1)S(1)}, bf16[2048,256]{1,0:T(8,128)(2,1)S(1)}, u32[]{:S(2)}, u32[]{:S(2)}) collective-permute-start(bf16[2048,256]{1,0:T(8,128)(2,1)S(1)} %copy-done), channel_id=1, source_target_pairs={{0,8},{8,0},{16,24},{24,16},{1,9},{9,1},{17,25},{25,17},{2,10},{10... | collective-permute-start | bytes 3145736 | tf_op jit(solution)/shard_map/ppermute | solution.py:83
  46.3 49.6 %collective-permute-start.17 = (bf16[2048,256]{1,0:T(8,128)(2,1)S(1)}, bf16[2048,256]{1,0:T(8,128)(2,1)S(1)}, u32[]{:S(2)}, u32[]{:S(2)}) collective-permute-start(bf16[2048,256]{1,0:T(8,128)(2,1)S(1)} %copy-done), channel_id=1, source_target_pairs={{0,16},{8,24},{16,0},{24,8},{1,17},{9,25},{17,1},{25,9},{2,18},{10... | collective-permute-start | bytes 3145736 | tf_op jit(solution)/shard_map/ppermute | solution.py:83
  80.9 17.0 %collective-permute-start.12 = (f32[512,256]{1,0:T(8,128)S(1)}, f32[512,256]{1,0:T(8,128)S(1)}, u32[]{:S(2)}, u32[]{:S(2)}) collective-permute-start(f32[512,256]{1,0:T(8,128)S(1)} %get-tuple-element.204.refs_4_), channel_id=1, source_target_pairs={{0,1},{1,0},{2,3},{3,2},{4,5},{5,4},{6,7},{7,6},{8,9},{9,8},{10,11... | collective-permute-start | bytes 1572872 | tf_op jit(solution)/shard_map/ppermute | solution.py:83
  81.0 17.1 %collective-permute-start.13 = (f32[512,256]{1,0:T(8,128)S(1)}, f32[512,256]{1,0:T(8,128)S(1)}, u32[]{:S(2)}, u32[]{:S(2)}) collective-permute-start(f32[512,256]{1,0:T(8,128)S(1)} %get-tuple-element.205.refs_5_), channel_id=1, source_target_pairs={{0,1},{1,0},{2,3},{3,2},{4,5},{5,4},{6,7},{7,6},{8,9},{9,8},{10,11... | collective-permute-start | bytes 1572872 | tf_op jit(solution)/shard_map/ppermute | solution.py:83
  81.5 16.7 %collective-permute-start.14 = (f32[512,256]{1,0:T(8,128)S(1)}, f32[512,256]{1,0:T(8,128)S(1)}, u32[]{:S(2)}, u32[]{:S(2)}) collective-permute-start(f32[512,256]{1,0:T(8,128)S(1)} %get-tuple-element.202.refs_2_), channel_id=1, source_target_pairs={{0,1},{1,0},{2,3},{3,2},{4,5},{5,4},{6,7},{7,6},{8,9},{9,8},{10,11... | collective-permute-start | bytes 1572872 | tf_op jit(solution)/shard_map/ppermute | solution.py:83
  95.0 17.7 %collective-permute-start.19 = (bf16[256,1280]{1,0:T(8,128)(2,1)S(1)}, bf16[256,1280]{1,0:T(8,128)(2,1)S(1)}, u32[]{:S(2)}, u32[]{:S(2)}) collective-permute-start(bf16[256,1280]{1,0:T(8,128)(2,1)S(1)} %slice.67.refs_13_), channel_id=1, source_target_pairs={{0,16},{8,24},{16,0},{24,8},{1,17},{9,25},{17,1},{25,9},{2,18},{10... | collective-permute-start | bytes 1966088 | tf_op jit(solution)/shard_map/ppermute | solution.py:83
  96.0 17.7 %collective-permute-start.20 = (bf16[256,1280]{1,0:T(8,128)(2,1)S(1)}, bf16[256,1280]{1,0:T(8,128)(2,1)S(1)}, u32[]{:S(2)}, u32[]{:S(2)}) collective-permute-start(bf16[256,1280]{1,0:T(8,128)(2,1)S(1)} %slice.68.refs_14_), channel_id=1, source_target_pairs={{0,8},{8,0},{16,24},{24,16},{1,9},{9,1},{17,25},{25,17},{2,10},{10... | collective-permute-start | bytes 1966088 | tf_op jit(solution)/shard_map/ppermute | solution.py:83
  98.1 22.0 %collective-permute-start.21 = (bf16[1024,256]{1,0:T(8,128)(2,1)S(1)}, bf16[1024,256]{1,0:T(8,128)(2,1)S(1)}, u32[]{:S(2)}, u32[]{:S(2)}) collective-permute-start(bf16[1024,256]{1,0:T(8,128)(2,1)S(1)} %slice.85.refs_10_), channel_id=1, source_target_pairs={{0,16},{8,24},{16,0},{24,8},{1,17},{9,25},{17,1},{25,9},{2,18},{10... | collective-permute-start | bytes 1572872 | tf_op jit(solution)/shard_map/ppermute | solution.py:83
  98.1 21.9 %collective-permute-start.22 = (bf16[1024,256]{1,0:T(8,128)(2,1)S(1)}, bf16[1024,256]{1,0:T(8,128)(2,1)S(1)}, u32[]{:S(2)}, u32[]{:S(2)}) collective-permute-start(bf16[1024,256]{1,0:T(8,128)(2,1)S(1)} %slice.86.refs_11_), channel_id=1, source_target_pairs={{0,8},{8,0},{16,24},{24,16},{1,9},{9,1},{17,25},{25,17},{2,10},{10... | collective-permute-start | bytes 1572872 | tf_op jit(solution)/shard_map/ppermute | solution.py:83
  133.4 27.5 %collective-permute-start.26 = (bf16[512,1024]{1,0:T(8,128)(2,1)S(1)}, bf16[512,1024]{1,0:T(8,128)(2,1)S(1)}, u32[]{:S(2)}, u32[]{:S(2)}) collective-permute-start(bf16[512,1024]{1,0:T(8,128)(2,1)S(1)} %get-tuple-element.222.refs_20_), channel_id=1, source_target_pairs={{0,8},{8,0},{16,24},{24,16},{1,9},{9,1},{17,25},{25,17},{2,10},{10... | collective-permute-start | bytes 3145736 | tf_op jit(solution)/shard_map/ppermute | solution.py:83
  134.7 26.1 %collective-permute-start.27 = (bf16[512,1024]{1,0:T(8,128)(2,1)}, bf16[512,1024]{1,0:T(8,128)(2,1)}, u32[]{:S(2)}, u32[]{:S(2)}) collective-permute-start(bf16[512,1024]{1,0:T(8,128)(2,1)} %get-tuple-element.230), channel_id=1, source_target_pairs={{0,16},{8,24},{16,0},{24,8},{1,17},{9,25},{17,1},{25,9},{2,18},{10... | collective-permute-start | bytes 3145736 | tf_op jit(solution)/shard_map/ppermute | solution.py:83
  158.6 31.8 %collective-permute-start.44 = (bf16[512,1280]{1,0:T(8,128)(2,1)S(1)}, bf16[512,1280]{1,0:T(8,128)(2,1)S(1)}, u32[]{:S(2)}, u32[]{:S(2)}) collective-permute-start(bf16[512,1280]{1,0:T(8,128)(2,1)S(1)} %get-tuple-element.284), channel_id=1, source_target_pairs={{0,8},{8,0},{16,24},{24,16},{1,9},{9,1},{17,25},{25,17},{2,10},{10... | collective-permute-start | bytes 3932168 | tf_op jit(solution)/shard_map/ppermute | solution.py:83
  159.6 31.7 %collective-permute-start.45 = (bf16[512,1280]{1,0:T(8,128)(2,1)S(1)}, bf16[512,1280]{1,0:T(8,128)(2,1)S(1)}, u32[]{:S(2)}, u32[]{:S(2)}) collective-permute-start(bf16[512,1280]{1,0:T(8,128)(2,1)S(1)} %get-tuple-element.286), channel_id=1, source_target_pairs={{0,16},{8,24},{16,0},{24,8},{1,17},{9,25},{17,1},{25,9},{2,18},{10... | collective-permute-start | bytes 3932168 | tf_op jit(solution)/shard_map/ppermute | solution.py:83
  170.3 38.5 %collective-permute-start.42 = (bf16[256,1024]{1,0:T(8,128)(2,1)S(1)}, bf16[256,1024]{1,0:T(8,128)(2,1)S(1)}, u32[]{:S(2)}, u32[]{:S(2)}) collective-permute-start(bf16[256,1024]{1,0:T(8,128)(2,1)S(1)} %get-tuple-element.254.refs_28_), channel_id=1, source_target_pairs={{0,16},{8,24},{16,0},{24,8},{1,17},{9,25},{17,1},{25,9},{2,18},{10... | collective-permute-start | bytes 1572872 | tf_op jit(solution)/shard_map/ppermute | solution.py:83
  171.2 39.2 %collective-permute-start.43 = (bf16[256,1024]{1,0:T(8,128)(2,1)S(1)}, bf16[256,1024]{1,0:T(8,128)(2,1)S(1)}, u32[]{:S(2)}, u32[]{:S(2)}) collective-permute-start(bf16[256,1024]{1,0:T(8,128)(2,1)S(1)} %get-tuple-element.255.refs_29_), channel_id=1, source_target_pairs={{0,8},{8,0},{16,24},{24,16},{1,9},{9,1},{17,25},{25,17},{2,10},{10... | collective-permute-start | bytes 1572872 | tf_op jit(solution)/shard_map/ppermute | solution.py:83
  192.0 26.1 %collective-permute-start.46 = (bf16[256,1280]{1,0:T(8,128)(2,1)S(1)}, bf16[256,1280]{1,0:T(8,128)(2,1)S(1)}, u32[]{:S(2)}, u32[]{:S(2)}) collective-permute-start(bf16[256,1280]{1,0:T(8,128)(2,1)S(1)} %get-tuple-element.291), channel_id=1, source_target_pairs={{0,16},{8,24},{16,0},{24,8},{1,17},{9,25},{17,1},{25,9},{2,18},{10... | collective-permute-start | bytes 1966088 | tf_op jit(solution)/shard_map/ppermute | solution.py:83
  193.2 24.9 %collective-permute-start.47 = (bf16[256,1280]{1,0:T(8,128)(2,1)S(1)}, bf16[256,1280]{1,0:T(8,128)(2,1)S(1)}, u32[]{:S(2)}, u32[]{:S(2)}) collective-permute-start(bf16[256,1280]{1,0:T(8,128)(2,1)S(1)} %get-tuple-element.292), channel_id=1, source_target_pairs={{0,8},{8,0},{16,24},{24,16},{1,9},{9,1},{17,25},{25,17},{2,10},{10... | collective-permute-start | bytes 1966088 | tf_op jit(solution)/shard_map/ppermute | solution.py:83
  214.1 15.4 %collective-permute-start.57 = (bf16[128,2048]{1,0:T(8,128)(2,1)S(1)}, bf16[128,2048]{1,0:T(8,128)(2,1)S(1)}, u32[]{:S(2)}, u32[]{:S(2)}) collective-permute-start(bf16[128,2048]{1,0:T(8,128)(2,1)S(1)} %get-tuple-element.323), channel_id=1, source_target_pairs={{0,2},{2,0},{4,6},{6,4},{1,3},{3,1},{5,7},{7,5},{8,10},{10,8},{12,... | collective-permute-start | bytes 1572872 | tf_op jit(solution)/shard_map/ppermute | solution.py:83
  221.0 15.5 %collective-permute-start.48 = (bf16[544,512]{1,0:T(8,128)(2,1)S(1)}, bf16[544,512]{1,0:T(8,128)(2,1)S(1)}, u32[]{:S(2)}, u32[]{:S(2)}) collective-permute-start(bf16[544,512]{1,0:T(8,128)(2,1)S(1)} %get-tuple-element.294), channel_id=1, source_target_pairs={{0,8},{8,0},{16,24},{24,16},{1,9},{9,1},{17,25},{25,17},{2,10},{10... | collective-permute-start | bytes 1671176 | tf_op jit(solution)/shard_map/ppermute | solution.py:83
  222.3 26.5 %collective-permute-start.56 = (bf16[128,2560]{1,0:T(8,128)(2,1)S(1)}, bf16[128,2560]{1,0:T(8,128)(2,1)S(1)}, u32[]{:S(2)}, u32[]{:S(2)}) collective-permute-start(bf16[128,2560]{1,0:T(8,128)(2,1)S(1)} %get-tuple-element.315), channel_id=1, source_target_pairs={{0,2},{2,0},{4,6},{6,4},{1,3},{3,1},{5,7},{7,5},{8,10},{10,8},{12,... | collective-permute-start | bytes 1966088 | tf_op jit(solution)/shard_map/ppermute | solution.py:83
  222.4 24.2 %collective-permute-start.54 = (bf16[512,512]{1,0:T(8,128)(2,1)S(1)}, bf16[512,512]{1,0:T(8,128)(2,1)S(1)}, u32[]{:S(2)}, u32[]{:S(2)}) collective-permute-start(bf16[512,512]{1,0:T(8,128)(2,1)S(1)} %get-tuple-element.310), channel_id=1, source_target_pairs={{0,8},{8,0},{16,24},{24,16},{1,9},{9,1},{17,25},{25,17},{2,10},{10... | collective-permute-start | bytes 1572872 | tf_op jit(solution)/shard_map/ppermute | solution.py:83
  229.5 18.1 %collective-permute-start.55 = (bf16[512,512]{1,0:T(8,128)(2,1)S(1)}, bf16[512,512]{1,0:T(8,128)(2,1)S(1)}, u32[]{:S(2)}, u32[]{:S(2)}) collective-permute-start(bf16[512,512]{1,0:T(8,128)(2,1)S(1)} %get-tuple-element.312), channel_id=1, source_target_pairs={{0,16},{8,24},{16,0},{24,8},{1,17},{9,25},{17,1},{25,9},{2,18},{10... | collective-permute-start | bytes 1572872 | tf_op jit(solution)/shard_map/ppermute | solution.py:83
  236.7 19.0 %collective-permute-start.50 = (bf16[288,512]{1,0:T(8,128)(2,1)S(1)}, bf16[288,512]{1,0:T(8,128)(2,1)S(1)}, u32[]{:S(2)}, u32[]{:S(2)}) collective-permute-start(bf16[288,512]{1,0:T(8,128)(2,1)S(1)} %get-tuple-element.299), channel_id=1, source_target_pairs={{0,16},{8,24},{16,0},{24,8},{1,17},{9,25},{17,1},{25,9},{2,18},{10... | collective-permute-start | bytes 884744 | tf_op jit(solution)/shard_map/ppermute | solution.py:83
  256.0 22.7 %collective-permute-start.36 = (f32[512,256]{1,0:T(8,128)S(1)}, f32[512,256]{1,0:T(8,128)S(1)}, u32[]{:S(2)}, u32[]{:S(2)}) collective-permute-start(f32[512,256]{1,0:T(8,128)S(1)} %get-tuple-element.273), channel_id=1, source_target_pairs={{0,1},{1,0},{2,3},{3,2},{4,5},{5,4},{6,7},{7,6},{8,9},{9,8},{10,11... | collective-permute-start | bytes 1572872 | tf_op jit(solution)/shard_map/ppermute | solution.py:83
  256.0 22.7 %collective-permute-start.37 = (f32[512,256]{1,0:T(8,128)S(1)}, f32[512,256]{1,0:T(8,128)S(1)}, u32[]{:S(2)}, u32[]{:S(2)}) collective-permute-start(f32[512,256]{1,0:T(8,128)S(1)} %get-tuple-element.274), channel_id=1, source_target_pairs={{0,1},{1,0},{2,3},{3,2},{4,5},{5,4},{6,7},{7,6},{8,9},{9,8},{10,11... | collective-permute-start | bytes 1572872 | tf_op jit(solution)/shard_map/ppermute | solution.py:83
  257.6 19.3 %collective-permute-start.62 = (bf16[64,2560]{1,0:T(8,128)(2,1)S(1)}, bf16[64,2560]{1,0:T(8,128)(2,1)S(1)}, u32[]{:S(2)}, u32[]{:S(2)}) collective-permute-start(bf16[64,2560]{1,0:T(8,128)(2,1)S(1)} %get-tuple-element.342), channel_id=1, source_target_pairs={{0,4},{2,6},{4,0},{6,2},{1,5},{3,7},{5,1},{7,3},{8,12},{10,14},{12... | collective-permute-start | bytes 983048 | tf_op jit(solution)/shard_map/ppermute | solution.py:83
  260.0 15.6 %collective-permute-start.61 = (bf16[128,1024]{1,0:T(8,128)(2,1)S(1)}, bf16[128,1024]{1,0:T(8,128)(2,1)S(1)}, u32[]{:S(2)}, u32[]{:S(2)}) collective-permute-start(bf16[128,1024]{1,0:T(8,128)(2,1)S(1)} %get-tuple-element.338), channel_id=1, source_target_pairs={{0,2},{2,0},{4,6},{6,4},{1,3},{3,1},{5,7},{7,5},{8,10},{10,8},{12,... | collective-permute-start | bytes 786440 | tf_op jit(solution)/shard_map/ppermute | solution.py:83
  275.6 15.5 %collective-permute-start.53 = (bf16[96,1024]{1,0:T(8,128)(2,1)S(1)}, bf16[96,1024]{1,0:T(8,128)(2,1)S(1)}, u32[]{:S(2)}, u32[]{:S(2)}) collective-permute-start(bf16[96,1024]{1,0:T(8,128)(2,1)S(1)} %get-tuple-element.307), channel_id=1, source_target_pairs={{0,4},{2,6},{4,0},{6,2},{1,5},{3,7},{5,1},{7,3},{8,12},{10,14},{12... | collective-permute-start | bytes 589832 | tf_op jit(solution)/shard_map/ppermute | solution.py:83
  (52 other events, 361.2 us)

commit v6 on v5

--- a/solution.py
+++ b/solution.py
@@ -834,14 +834,18 @@
                     send[:half, :] = add(keep[half:, :], got[half:rows, :]).astype(BF16)
                 if extra:
                     total = own[...] + read_pair(got, rows)
-                    refs[0][...] = total if last else write_pair(send, half, total)
+                    if last:
+                        for i, ref in enumerate(refs):
+                            ref[...] = total[i : i + 1, :]
+                    else:
+                        refs[0][...] = write_pair(send, half, total)
 
             if last:
                 outs = [((rows, size), F32) for size in widths]
             else:
                 outs = [((half, width), BF16), ((half + extra, width), BF16)]
             if extra:
-                outs.append(((VR, H), F32))
+                outs += [((1, H), F32)] * 11 if last else [((VR, H), F32)]
             result = launch(turn_line, "v" * (2 + len(mine)), (keep, got, *mine), outs)
             if not last:
                 keep, send, *mine = result
@@ -1323,7 +1327,8 @@
     late_cross = square_cross(*square_turn(late_state))
     early_seen = []
     output_w, gate_w = scatter_line(*square_end(hold(early_cross, late_cross[1], late_cross[3])), widths=[H, H], behind=hidden_seen[-1], seen=early_seen)
-    key_w, value_w, vectors = scatter_line(*square_end(late_cross), widths=[H, H])
+    key_w, value_w, *vectors = scatter_line(*square_end(late_cross), widths=[H, H])
+    vectors = [vector.reshape(H) for vector in vectors]
     shape = block_entries.shape
     return (
         block_out.reshape(shape),

time: 293 us -> 293 us (level)
  no operation moved by 1% of the time
where the time goes in v6:
time: 293 us; the launch traced here: 292 us
  waiting for transfers between devices  130 us (44%)
  Pallas kernels  90.7 us (31%)
  starting transfers between devices  65.2 us (22%)
  local copies, waits for them, and re-layouts  4.47 us (2%)
    ppermute x58, waiting for transfers between devices, swap(): return lax.ppermute(value, axis, [(i, i ^ step) for i in range(size)])  120 us
    pallas_call x39, Pallas kernels, launch(): pl.pallas_call(run, out_shape=[jax.ShapeDtypeStruct(shape, dtype) for sha...  90.7 us
    ppermute x58, starting transfers between devices, swap(): return lax.ppermute(value, axis, [(i, i ^ step) for i in range(size)])  52.6 us
    ppermute x4, starting transfers between devices, along_ctx(): return lax.ppermute(value, 'ctx', pairs)  9.73 us
    ppermute x4, waiting for transfers between devices, along_ctx(): return lax.ppermute(value, 'ctx', pairs)  7.99 us
  transfers between devices with their start and end apart: 64, of which 41 were waited for; matrix products, arithmetic and copies ran while one was open for 1% of the time, Pallas kernels for 27%

profile of v6, /device:TPU:0, one launch (start us, length us, event | category | flops | bytes accessed | tf_op | source)
XLA Modules:
  0.0 292.1 jit_solution(3198803075304254870)
XLA Ops:
  2.2 3.0 %collective-permute-start.3 = (bf16[256,2048]{1,0:T(8,128)(2,1)S(1)}, bf16[256,2048]{1,0:T(8,128)(2,1)S(1)}, u32[]{:S(2)}, u32[]{:S(2)}) collective-permute-start(bf16[256,2048]{1,0:T(8,128)(2,1)S(1)} %pack_time.1.refs_5_.refs_8_.refs_22_.refs_20_), channel_id=1, source_target_pairs={{0,8},{8,0},{16,24},{24,16},{1,9},{9,1},{17,25},{25,17},{2,10},{10... | collective-permute-start | bytes 3145736 | tf_op jit(solution)/shard_map/ppermute | solution.py:83
  9.7 3.5 %collective-permute-start.1 = (bf16[2,1024]{1,0:T(2,128)(2,1)S(1)}, bf16[2,1024]{1,0:T(2,128)(2,1)S(1)}, u32[]{:S(2)}, u32[]{:S(2)}) collective-permute-start(bf16[2,1024]{1,0:T(2,128)(2,1)S(1)} %pad_maximum_fusion.1), channel_id=1, source_target_pairs={{0,2},{2,4},{4,6},{1,3},{3,5},{5,7},{8,10},{10,12},{12,14},{9,11},... | collective-permute-start | bytes 12296 | tf_op jit(solution)/shard_map/ppermute | solution.py:90
  14.5 5.8 %mix_time.2 = (bf16[512,1024]{1,0:T(8,128)(2,1)S(1)}, bf16[512,1024]{1,0:T(8,128)(2,1)S(1)}, bf16[512,1024]{1,0:T(8,128)(2,1)S(1)}, bf16[512,1024]{1,0:T(8,128)(...) custom-call(s32[5]{0:T(128)S(1)} %pad_add_fusion.refs_0_, ...), custom_call_target="tpu_custom_call" | custom-call | tf_op jit(solution)/shard_map/mix_time/pallas_call | solution.py:37
  20.3 8.0 %collective-permute-done.3.refs_6_.refs_9_.refs_23_.refs_21_ = bf16[256,2048]{1,0:T(8,128)(2,1)S(1)} collective-permute-done((bf16[256,2048]{1,0:T(8,128)(2,1)S(1)}, bf16[256,2048]{1,0:T(8,128)(2,1)S(1)}, u32[]{:S(2)}, u32[]{:S(2)}) %collective-permute-start.3) | collective-permute-done | bytes 1048608 | tf_op jit(solution)/shard_map/ppermute | solution.py:83
  33.4 9.0 %collective-permute-done.5.refs_8_.refs_11_.refs_25_.refs_23_ = bf16[256,1024]{1,0:T(8,128)(2,1)S(1)} collective-permute-done((bf16[256,1024]{1,0:T(8,128)(2,1)S(1)}, bf16[256,1024]{1,0:T(8,128)(2,1)S(1)}, u32[]{:S(2)}, u32[]{:S(2)}) %collective-permute-start.5) | collective-permute-done | bytes 524320 | tf_op jit(solution)/shard_map/ppermute | solution.py:83
  49.8 5.1 %project_time.1 = (f32[4,512,128]{2,1,0:T(8,128)S(1)}, f32[4,512,128]{2,1,0:T(8,128)S(1)}, f32[512,512]{1,0:T(8,128)S(1)}, f32[4,48,128]{2,1,0:T(8,128)S(1)}, f32[6,512]{1,0:T(8,128)S(1)}) custom-call(s32[5]{0:T(128)S(1)} %pad_add_fusion.refs_0_, bf16[512,1024]{1,0:T(8,128)(2,1)S(1)} %get-tuple-element.196.refs_1_, ...), custom_call_target="tpu_custom_call" | custom-call | tf_op jit(solution)/shard_map/project_time/pallas_call | solution.py:37
  64.6 10.9 %collective-permute-done.10.refs_6_.refs_11_ = bf16[256,2560]{1,0:T(8,128)(2,1)S(1)} collective-permute-done((bf16[256,2560]{1,0:T(8,128)(2,1)S(1)}, bf16[256,2560]{1,0:T(8,128)(2,1)S(1)}, u32[]{:S(2)}, u32[]{:S(2)}) %collective-permute-start.10) | collective-permute-done | bytes 1310752 | tf_op jit(solution)/shard_map/ppermute | solution.py:83
  76.2 4.7 %sweep_time.1 = (f32[512,256]{1,0:T(8,128)S(1)}, f32[512,256]{1,0:T(8,128)S(1)}, f32[512,256]{1,0:T(8,128)S(1)}, f32[512,256]{1,0:T(8,128)S(1)}) custom-call(s32[5]{0:T(128)S(1)} %pad_add_fusion.refs_0_, f32[4,512,128]{2,1,0:T(8,128)S(1)} %get-tuple-element.202.refs_1_.refs_0_, f32[4,512,128]{2,1,0:T(8,128)S(1)} %get-tuple-element.203.refs_2_.refs_1_.refs_3_, ...), custom_call_target="tpu_custom_call" | custom-call | tf_op jit(solution)/shard_map/sweep_time/pallas_call | solution.py:37
  81.6 13.4 %collective-permute-done.16.refs_3_.refs_16_ = bf16[2048,256]{1,0:T(8,128)(2,1)S(1)} collective-permute-done((bf16[2048,256]{1,0:T(8,128)(2,1)S(1)}, bf16[2048,256]{1,0:T(8,128)(2,1)S(1)}, u32[]{:S(2)}, u32[]{:S(2)}) %collective-permute-start.16) | collective-permute-done | bytes 1048608 | tf_op jit(solution)/shard_map/ppermute | solution.py:83
  99.9 3.3 %middle_norm.1 = (f32[512,512]{1,0:T(8,128)S(1)}, f32[512,1024]{1,0:T(8,128)S(1)}, f32[512,1]{1,0:T(8,128)S(1)}, f32[2,1024]{1,0:T(2,128)S(1)}) custom-call(bf16[512,512]{1,0:T(8,128)(2,1)} %bitcast.4.refs_1_.refs_0_, bf16[512,512]{1,0:T(8,128)(2,1)} %collective-permute-done.refs_2_.refs_1_, f32[512,256]{1,0:T(8,128)S(1)} %get-tuple-element.212.refs_2_, ...), custom_call_target="tpu_custom_call" | custom-call | tf_op jit(solution)/shard_map/middle_norm/pallas_call | solution.py:37
  103.1 3.7 %collective-permute-start.18 = (f32[2,1024]{1,0:T(2,128)S(1)}, f32[2,1024]{1,0:T(2,128)S(1)}, u32[]{:S(2)}, u32[]{:S(2)}) collective-permute-start(f32[2,1024]{1,0:T(2,128)S(1)} %get-tuple-element.218), channel_id=1, source_target_pairs={{0,2},{2,4},{4,6},{1,3},{3,5},{5,7},{8,10},{10,12},{12,14},{9,11},... | collective-permute-start | bytes 24584 | tf_op jit(solution)/shard_map/ppermute | solution.py:90
  108.0 4.7 %collective-permute-done.19.refs_8_.refs_13_ = bf16[256,1280]{1,0:T(8,128)(2,1)S(1)} collective-permute-done((bf16[256,1280]{1,0:T(8,128)(2,1)S(1)}, bf16[256,1280]{1,0:T(8,128)(2,1)S(1)}, u32[]{:S(2)}, u32[]{:S(2)}) %collective-permute-start.19) | collective-permute-done | bytes 655392 | tf_op jit(solution)/shard_map/ppermute | solution.py:83
  113.6 5.0 %channel_forward.1 = (bf16[512,1024]{1,0:T(8,128)(2,1)S(1)}, bf16[512,1024]{1,0:T(8,128)(2,1)S(1)}, bf16[512,1024]{1,0:T(8,128)(2,1)S(1)}, bf16[512,1024]{1,0:T(...) custom-call(s32[5]{0:T(128)S(1)} %pad_add_fusion.refs_0_, ...), custom_call_target="tpu_custom_call" | custom-call | tf_op jit(solution)/shard_map/channel_forward/pallas_call | solution.py:37
  120.1 3.2 %channel_return.1 = (f32[512,256]{1,0:T(8,128)S(1)}, f32[512,256]{1,0:T(8,128)S(1)}, bf16[512,256]{1,0:T(8,128)(2,1)S(1)}, bf16[512,256]{1,0:T(8,128)(2,1)S(1)}) custom-call(s32[5]{0:T(128)S(1)} %pad_add_fusion.refs_0_, bf16[512,2048]{1,0:T(8,128)(2,1)S(1)} %get-tuple-element.219.refs_1_.refs_3_, bf16[2048,256]{1,0:T(8,128)(2,1)S(1)} %copy-done, ...), custom_call_target="tpu_custom_call" | custom-call | tf_op jit(solution)/shard_map/channel_return/pallas_call | solution.py:37
  129.2 4.2 %weight_products.4 = (bf16[512,1024]{1,0:T(8,128)(2,1)S(1)}, bf16[512,1024]{1,0:T(8,128)(2,1)S(1)}, bf16[512,1024]{1,0:T(8,128)(2,1)}, bf16[512,1024]{1,0:T(8,128)(2,1)S(1)}) custom-call(s32[5]{0:T(128)S(1)} %pad_add_fusion.refs_0_, bf16[512,512]{1,0:T(8,128)(2,1)S(1)} %get-tuple-element.227.refs_1_, bf16[512,512]{1,0:T(8,128)(2,1)S(1)} %collective-permute-done.25.refs_2_, ...), custom_call_target="tpu_custom_call" | custom-call | tf_op jit(solution)/shard_map/weight_products/pallas_call | solution.py:37
  135.2 3.1 %sweep_again.1 = (bf16[512,512]{1,0:T(8,128)(2,1)S(1)}, f32[4,512,128]{2,1,0:T(8,128)S(1)}, f32[512,512]{1,0:T(8,128)S(1)}, f32[512,512]{1,0:T(8,128)S(1)}, f32[...) custom-call(f32[4,512,128]{2,1,0:T(8,128)S(1)} %get-tuple-element.20, ...), custom_call_target="tpu_custom_call" | custom-call | tf_op jit(solution)/shard_map/sweep_again/pallas_call | solution.py:37
  138.3 4.9 %mix_time.3 = (bf16[512,1024]{1,0:T(8,128)(2,1)S(1)}, bf16[512,1024]{1,0:T(8,128)(2,1)S(1)}, bf16[512,1024]{1,0:T(8,128)(2,1)S(1)}, bf16[512,1024]{1,0:T(8,128)(...) custom-call(s32[5]{0:T(128)S(1)} %pad_add_fusion.refs_0_, ...), custom_call_target="tpu_custom_call" | custom-call | tf_op jit(solution)/shard_map/mix_time/pallas_call | solution.py:37
  143.2 9.0 %channel_backward.1 = (bf16[512,2048]{1,0:T(8,128)(2,1)S(1)}, f32[512,256]{1,0:T(8,128)S(1)}, f32[512,256]{1,0:T(8,128)S(1)}, f32[512,256]{1,0:T(8,128)S(1)}, f3...) custom-call(s32[5]{0:T(128)S(1)} %pad_add_fusion.refs_0_, ...), custom_call_target="tpu_custom_call" | custom-call | tf_op jit(solution)/shard_map/channel_backward/pallas_call | solution.py:37
  154.8 3.8 %weight_products.5 = (bf16[512,1280]{1,0:T(8,128)(2,1)S(1)}, bf16[512,1280]{1,0:T(8,128)(2,1)S(1)}, bf16[512,1280]{1,0:T(8,128)(2,1)S(1)}, bf16[512,1280]{1,0:T(8,128)(2,1)S(1)}) custom-call(s32[5]{0:T(128)S(1)} %pad_add_fusion.refs_0_, bf16[512,1024]{1,0:T(8,128)(2,1)S(1)} %copy-done.3, bf16[512,1024]{1,0:T(8,128)(2,1)S(1)} %copy-done.5, ...), custom_call_target="tpu_custom_call" | custom-call | tf_op jit(solution)/shard_map/weight_products/pallas_call | solution.py:37
  163.4 2.9 %collective-permute-done.32.refs_9_ = f32[2,1024]{1,0:T(2,128)S(1)} collective-permute-done((f32[2,1024]{1,0:T(2,128)S(1)}, f32[2,1024]{1,0:T(2,128)S(1)}, u32[]{:S(2)}, u32[]{:S(2)}) %collective-permute-start.32) | collective-permute-done | bytes 8224 | tf_op jit(solution)/shard_map/ppermute | solution.py:90
  172.3 6.6 %middle_backward.1 = (bf16[512,1024]{1,0:T(8,128)(2,1)S(1)}, f32[512,512]{1,0:T(8,128)S(1)}, f32[4,512,128]{2,1,0:T(8,128)S(1)}, bf16[512,512]{1,0:T(8,128)(2,1)...) custom-call(s32[5]{0:T(128)S(1)} %pad_add_fusion.refs_0_, f32[512,256]{1,0:T(8,128)S(1)} %get-tuple-element.241.refs_1_, ...), custom_call_target="tpu_custom_call" | custom-call | tf_op jit(solution)/shard_map/middle_backward/pallas_call | solution.py:37
  183.2 2.9 collective-permute-start.35
  196.9 10.7 %time_backward.1 = (bf16[512,512]{1,0:T(8,128)(2,1)S(1)}, bf16[512,512]{1,0:T(8,128)(2,1)S(1)}, f32[512,512]{1,0:T(8,128)S(1)}, f32[512,256]{1,0:T(8,128)S(1)}, ...) custom-call(s32[5]{0:T(128)S(1)} %pad_add_fusion.refs_0_, ...), custom_call_target="tpu_custom_call" | custom-call | tf_op jit(solution)/shard_map/time_backward/pallas_call | solution.py:37
  210.4 2.7 collective-permute-done.39.refs_5_
  214.1 2.7 collective-permute-start.57
  223.4 6.0 %collective-permute-done.57.refs_1_ = bf16[128,2048]{1,0:T(8,128)(2,1)S(1)} collective-permute-done((bf16[128,2048]{1,0:T(8,128)(2,1)S(1)}, bf16[128,2048]{1,0:T(8,128)(2,1)S(1)}, u32[]{:S(2)}, u32[]{:S(2)}) %collective-permute-start.57) | collective-permute-done | bytes 524320 | tf_op jit(solution)/shard_map/ppermute | solution.py:83
  230.2 5.1 %collective-permute-done.49.refs_3_ = bf16[512,512]{1,0:T(8,128)(2,1)S(1)} collective-permute-done((bf16[512,512]{1,0:T(8,128)(2,1)S(1)}, bf16[512,512]{1,0:T(8,128)(2,1)S(1)}, u32[]{:S(2)}, u32[]{:S(2)}) %collective-permute-start.49) | collective-permute-done | bytes 524320 | tf_op jit(solution)/shard_map/ppermute | solution.py:83
  238.3 8.3 %collective-permute-done.54.refs_1_ = bf16[512,512]{1,0:T(8,128)(2,1)S(1)} collective-permute-done((bf16[512,512]{1,0:T(8,128)(2,1)S(1)}, bf16[512,512]{1,0:T(8,128)(2,1)S(1)}, u32[]{:S(2)}, u32[]{:S(2)}) %collective-permute-start.54) | collective-permute-done | bytes 524320 | tf_op jit(solution)/shard_map/ppermute | solution.py:83
  250.8 4.9 %collective-permute-done.51.refs_3_ = bf16[256,512]{1,0:T(8,128)(2,1)S(1)} collective-permute-done((bf16[256,512]{1,0:T(8,128)(2,1)S(1)}, bf16[256,512]{1,0:T(8,128)(2,1)S(1)}, u32[]{:S(2)}, u32[]{:S(2)}) %collective-permute-start.51) | collective-permute-done | bytes 262176 | tf_op jit(solution)/shard_map/ppermute | solution.py:83
  260.9 6.8 %collective-permute-done.52.refs_1_ = bf16[160,1024]{1,0:T(8,128)(2,1)S(1)} collective-permute-done((bf16[160,1024]{1,0:T(8,128)(2,1)S(1)}, bf16[160,1024]{1,0:T(8,128)(2,1)S(1)}, u32[]{:S(2)}, u32[]{:S(2)}) %collective-permute-start.52) | collective-permute-done | bytes 327712 | tf_op jit(solution)/shard_map/ppermute | solution.py:83
  267.8 7.9 %collective-permute-done.61.refs_1_ = bf16[128,1024]{1,0:T(8,128)(2,1)S(1)} collective-permute-done((bf16[128,1024]{1,0:T(8,128)(2,1)S(1)}, bf16[128,1024]{1,0:T(8,128)(2,1)S(1)}, u32[]{:S(2)}, u32[]{:S(2)}) %collective-permute-start.61) | collective-permute-done | bytes 262176 | tf_op jit(solution)/shard_map/ppermute | solution.py:83
  283.0 7.4 %collective-permute-done.63.refs_1_ = bf16[64,1024]{1,0:T(8,128)(2,1)S(1)} collective-permute-done((bf16[64,1024]{1,0:T(8,128)(2,1)S(1)}, bf16[64,1024]{1,0:T(8,128)(2,1)S(1)}, u32[]{:S(2)}, u32[]{:S(2)}) %collective-permute-start.63) | collective-permute-done | bytes 131104 | tf_op jit(solution)/shard_map/ppermute | solution.py:83
  (191 shorter events, 107.6 us)
Async XLA Ops:
  2.2 26.2 %collective-permute-start.3 = (bf16[256,2048]{1,0:T(8,128)(2,1)S(1)}, bf16[256,2048]{1,0:T(8,128)(2,1)S(1)}, u32[]{:S(2)}, u32[]{:S(2)}) collective-permute-start(bf16[256,2048]{1,0:T(8,128)(2,1)S(1)} %pack_time.1.refs_5_.refs_8_.refs_22_.refs_20_), channel_id=1, source_target_pairs={{0,8},{8,0},{16,24},{24,16},{1,9},{9,1},{17,25},{25,17},{2,10},{10... | collective-permute-start | bytes 3145736 | tf_op jit(solution)/shard_map/ppermute | solution.py:83
  5.2 24.6 %collective-permute-start.4 = (bf16[256,2048]{1,0:T(8,128)(2,1)S(1)}, bf16[256,2048]{1,0:T(8,128)(2,1)S(1)}, u32[]{:S(2)}, u32[]{:S(2)}) collective-permute-start(bf16[256,2048]{1,0:T(8,128)(2,1)S(1)} %pack_time.1.refs_5_.refs_8_.refs_22_.refs_20_), channel_id=1, source_target_pairs={{0,16},{8,24},{16,0},{24,8},{1,17},{9,25},{17,1},{25,9},{2,18},{10... | collective-permute-start | bytes 3145736 | tf_op jit(solution)/shard_map/ppermute | solution.py:83
  43.8 31.7 %collective-permute-start.10 = (bf16[256,2560]{1,0:T(8,128)(2,1)S(1)}, bf16[256,2560]{1,0:T(8,128)(2,1)S(1)}, u32[]{:S(2)}, u32[]{:S(2)}) collective-permute-start(bf16[256,2560]{1,0:T(8,128)(2,1)S(1)} %pack.1.refs_5_.refs_10_), channel_id=1, source_target_pairs={{0,8},{8,0},{16,24},{24,16},{1,9},{9,1},{17,25},{25,17},{2,10},{10... | collective-permute-start | bytes 3932168 | tf_op jit(solution)/shard_map/ppermute | solution.py:83
  44.4 31.7 %collective-permute-start.11 = (bf16[256,2560]{1,0:T(8,128)(2,1)S(1)}, bf16[256,2560]{1,0:T(8,128)(2,1)S(1)}, u32[]{:S(2)}, u32[]{:S(2)}) collective-permute-start(bf16[256,2560]{1,0:T(8,128)(2,1)S(1)} %pack.1.refs_5_.refs_10_), channel_id=1, source_target_pairs={{0,16},{8,24},{16,0},{24,8},{1,17},{9,25},{17,1},{25,9},{2,18},{10... | collective-permute-start | bytes 3932168 | tf_op jit(solution)/shard_map/ppermute | solution.py:83
  45.0 50.0 %collective-permute-start.16 = (bf16[2048,256]{1,0:T(8,128)(2,1)S(1)}, bf16[2048,256]{1,0:T(8,128)(2,1)S(1)}, u32[]{:S(2)}, u32[]{:S(2)}) collective-permute-start(bf16[2048,256]{1,0:T(8,128)(2,1)S(1)} %copy-done), channel_id=1, source_target_pairs={{0,8},{8,0},{16,24},{24,16},{1,9},{9,1},{17,25},{25,17},{2,10},{10... | collective-permute-start | bytes 3145736 | tf_op jit(solution)/shard_map/ppermute | solution.py:83
  46.3 49.6 %collective-permute-start.17 = (bf16[2048,256]{1,0:T(8,128)(2,1)S(1)}, bf16[2048,256]{1,0:T(8,128)(2,1)S(1)}, u32[]{:S(2)}, u32[]{:S(2)}) collective-permute-start(bf16[2048,256]{1,0:T(8,128)(2,1)S(1)} %copy-done), channel_id=1, source_target_pairs={{0,16},{8,24},{16,0},{24,8},{1,17},{9,25},{17,1},{25,9},{2,18},{10... | collective-permute-start | bytes 3145736 | tf_op jit(solution)/shard_map/ppermute | solution.py:83
  80.9 17.0 %collective-permute-start.12 = (f32[512,256]{1,0:T(8,128)S(1)}, f32[512,256]{1,0:T(8,128)S(1)}, u32[]{:S(2)}, u32[]{:S(2)}) collective-permute-start(f32[512,256]{1,0:T(8,128)S(1)} %get-tuple-element.214.refs_4_), channel_id=1, source_target_pairs={{0,1},{1,0},{2,3},{3,2},{4,5},{5,4},{6,7},{7,6},{8,9},{9,8},{10,11... | collective-permute-start | bytes 1572872 | tf_op jit(solution)/shard_map/ppermute | solution.py:83
  81.0 17.1 %collective-permute-start.13 = (f32[512,256]{1,0:T(8,128)S(1)}, f32[512,256]{1,0:T(8,128)S(1)}, u32[]{:S(2)}, u32[]{:S(2)}) collective-permute-start(f32[512,256]{1,0:T(8,128)S(1)} %get-tuple-element.215.refs_5_), channel_id=1, source_target_pairs={{0,1},{1,0},{2,3},{3,2},{4,5},{5,4},{6,7},{7,6},{8,9},{9,8},{10,11... | collective-permute-start | bytes 1572872 | tf_op jit(solution)/shard_map/ppermute | solution.py:83
  81.5 16.7 %collective-permute-start.14 = (f32[512,256]{1,0:T(8,128)S(1)}, f32[512,256]{1,0:T(8,128)S(1)}, u32[]{:S(2)}, u32[]{:S(2)}) collective-permute-start(f32[512,256]{1,0:T(8,128)S(1)} %get-tuple-element.212.refs_2_), channel_id=1, source_target_pairs={{0,1},{1,0},{2,3},{3,2},{4,5},{5,4},{6,7},{7,6},{8,9},{9,8},{10,11... | collective-permute-start | bytes 1572872 | tf_op jit(solution)/shard_map/ppermute | solution.py:83
  95.0 17.7 %collective-permute-start.19 = (bf16[256,1280]{1,0:T(8,128)(2,1)S(1)}, bf16[256,1280]{1,0:T(8,128)(2,1)S(1)}, u32[]{:S(2)}, u32[]{:S(2)}) collective-permute-start(bf16[256,1280]{1,0:T(8,128)(2,1)S(1)} %slice.34.refs_13_), channel_id=1, source_target_pairs={{0,16},{8,24},{16,0},{24,8},{1,17},{9,25},{17,1},{25,9},{2,18},{10... | collective-permute-start | bytes 1966088 | tf_op jit(solution)/shard_map/ppermute | solution.py:83
  96.0 17.7 %collective-permute-start.20 = (bf16[256,1280]{1,0:T(8,128)(2,1)S(1)}, bf16[256,1280]{1,0:T(8,128)(2,1)S(1)}, u32[]{:S(2)}, u32[]{:S(2)}) collective-permute-start(bf16[256,1280]{1,0:T(8,128)(2,1)S(1)} %slice.35.refs_14_), channel_id=1, source_target_pairs={{0,8},{8,0},{16,24},{24,16},{1,9},{9,1},{17,25},{25,17},{2,10},{10... | collective-permute-start | bytes 1966088 | tf_op jit(solution)/shard_map/ppermute | solution.py:83
  98.1 22.0 %collective-permute-start.21 = (bf16[1024,256]{1,0:T(8,128)(2,1)S(1)}, bf16[1024,256]{1,0:T(8,128)(2,1)S(1)}, u32[]{:S(2)}, u32[]{:S(2)}) collective-permute-start(bf16[1024,256]{1,0:T(8,128)(2,1)S(1)} %slice.41.refs_10_), channel_id=1, source_target_pairs={{0,16},{8,24},{16,0},{24,8},{1,17},{9,25},{17,1},{25,9},{2,18},{10... | collective-permute-start | bytes 1572872 | tf_op jit(solution)/shard_map/ppermute | solution.py:83
  98.1 21.9 %collective-permute-start.22 = (bf16[1024,256]{1,0:T(8,128)(2,1)S(1)}, bf16[1024,256]{1,0:T(8,128)(2,1)S(1)}, u32[]{:S(2)}, u32[]{:S(2)}) collective-permute-start(bf16[1024,256]{1,0:T(8,128)(2,1)S(1)} %slice.42.refs_11_), channel_id=1, source_target_pairs={{0,8},{8,0},{16,24},{24,16},{1,9},{9,1},{17,25},{25,17},{2,10},{10... | collective-permute-start | bytes 1572872 | tf_op jit(solution)/shard_map/ppermute | solution.py:83
  133.4 27.5 %collective-permute-start.26 = (bf16[512,1024]{1,0:T(8,128)(2,1)S(1)}, bf16[512,1024]{1,0:T(8,128)(2,1)S(1)}, u32[]{:S(2)}, u32[]{:S(2)}) collective-permute-start(bf16[512,1024]{1,0:T(8,128)(2,1)S(1)} %get-tuple-element.232.refs_20_), channel_id=1, source_target_pairs={{0,8},{8,0},{16,24},{24,16},{1,9},{9,1},{17,25},{25,17},{2,10},{10... | collective-permute-start | bytes 3145736 | tf_op jit(solution)/shard_map/ppermute | solution.py:83
  134.7 26.1 %collective-permute-start.27 = (bf16[512,1024]{1,0:T(8,128)(2,1)}, bf16[512,1024]{1,0:T(8,128)(2,1)}, u32[]{:S(2)}, u32[]{:S(2)}) collective-permute-start(bf16[512,1024]{1,0:T(8,128)(2,1)} %get-tuple-element.240), channel_id=1, source_target_pairs={{0,16},{8,24},{16,0},{24,8},{1,17},{9,25},{17,1},{25,9},{2,18},{10... | collective-permute-start | bytes 3145736 | tf_op jit(solution)/shard_map/ppermute | solution.py:83
  158.6 31.8 %collective-permute-start.44 = (bf16[512,1280]{1,0:T(8,128)(2,1)S(1)}, bf16[512,1280]{1,0:T(8,128)(2,1)S(1)}, u32[]{:S(2)}, u32[]{:S(2)}) collective-permute-start(bf16[512,1280]{1,0:T(8,128)(2,1)S(1)} %get-tuple-element.294), channel_id=1, source_target_pairs={{0,8},{8,0},{16,24},{24,16},{1,9},{9,1},{17,25},{25,17},{2,10},{10... | collective-permute-start | bytes 3932168 | tf_op jit(solution)/shard_map/ppermute | solution.py:83
  159.6 31.7 %collective-permute-start.45 = (bf16[512,1280]{1,0:T(8,128)(2,1)S(1)}, bf16[512,1280]{1,0:T(8,128)(2,1)S(1)}, u32[]{:S(2)}, u32[]{:S(2)}) collective-permute-start(bf16[512,1280]{1,0:T(8,128)(2,1)S(1)} %get-tuple-element.296), channel_id=1, source_target_pairs={{0,16},{8,24},{16,0},{24,8},{1,17},{9,25},{17,1},{25,9},{2,18},{10... | collective-permute-start | bytes 3932168 | tf_op jit(solution)/shard_map/ppermute | solution.py:83
  170.3 38.5 %collective-permute-start.42 = (bf16[256,1024]{1,0:T(8,128)(2,1)S(1)}, bf16[256,1024]{1,0:T(8,128)(2,1)S(1)}, u32[]{:S(2)}, u32[]{:S(2)}) collective-permute-start(bf16[256,1024]{1,0:T(8,128)(2,1)S(1)} %get-tuple-element.264.refs_28_), channel_id=1, source_target_pairs={{0,16},{8,24},{16,0},{24,8},{1,17},{9,25},{17,1},{25,9},{2,18},{10... | collective-permute-start | bytes 1572872 | tf_op jit(solution)/shard_map/ppermute | solution.py:83
  171.2 39.2 %collective-permute-start.43 = (bf16[256,1024]{1,0:T(8,128)(2,1)S(1)}, bf16[256,1024]{1,0:T(8,128)(2,1)S(1)}, u32[]{:S(2)}, u32[]{:S(2)}) collective-permute-start(bf16[256,1024]{1,0:T(8,128)(2,1)S(1)} %get-tuple-element.265.refs_29_), channel_id=1, source_target_pairs={{0,8},{8,0},{16,24},{24,16},{1,9},{9,1},{17,25},{25,17},{2,10},{10... | collective-permute-start | bytes 1572872 | tf_op jit(solution)/shard_map/ppermute | solution.py:83
  192.0 26.1 %collective-permute-start.46 = (bf16[256,1280]{1,0:T(8,128)(2,1)S(1)}, bf16[256,1280]{1,0:T(8,128)(2,1)S(1)}, u32[]{:S(2)}, u32[]{:S(2)}) collective-permute-start(bf16[256,1280]{1,0:T(8,128)(2,1)S(1)} %get-tuple-element.301), channel_id=1, source_target_pairs={{0,16},{8,24},{16,0},{24,8},{1,17},{9,25},{17,1},{25,9},{2,18},{10... | collective-permute-start | bytes 1966088 | tf_op jit(solution)/shard_map/ppermute | solution.py:83
  193.2 24.9 %collective-permute-start.47 = (bf16[256,1280]{1,0:T(8,128)(2,1)S(1)}, bf16[256,1280]{1,0:T(8,128)(2,1)S(1)}, u32[]{:S(2)}, u32[]{:S(2)}) collective-permute-start(bf16[256,1280]{1,0:T(8,128)(2,1)S(1)} %get-tuple-element.302), channel_id=1, source_target_pairs={{0,8},{8,0},{16,24},{24,16},{1,9},{9,1},{17,25},{25,17},{2,10},{10... | collective-permute-start | bytes 1966088 | tf_op jit(solution)/shard_map/ppermute | solution.py:83
  214.1 15.4 %collective-permute-start.57 = (bf16[128,2048]{1,0:T(8,128)(2,1)S(1)}, bf16[128,2048]{1,0:T(8,128)(2,1)S(1)}, u32[]{:S(2)}, u32[]{:S(2)}) collective-permute-start(bf16[128,2048]{1,0:T(8,128)(2,1)S(1)} %get-tuple-element.339), channel_id=1, source_target_pairs={{0,2},{2,0},{4,6},{6,4},{1,3},{3,1},{5,7},{7,5},{8,10},{10,8},{12,... | collective-permute-start | bytes 1572872 | tf_op jit(solution)/shard_map/ppermute | solution.py:83
  221.0 15.5 %collective-permute-start.48 = (bf16[544,512]{1,0:T(8,128)(2,1)S(1)}, bf16[544,512]{1,0:T(8,128)(2,1)S(1)}, u32[]{:S(2)}, u32[]{:S(2)}) collective-permute-start(bf16[544,512]{1,0:T(8,128)(2,1)S(1)} %get-tuple-element.304), channel_id=1, source_target_pairs={{0,8},{8,0},{16,24},{24,16},{1,9},{9,1},{17,25},{25,17},{2,10},{10... | collective-permute-start | bytes 1671176 | tf_op jit(solution)/shard_map/ppermute | solution.py:83
  222.3 26.5 %collective-permute-start.56 = (bf16[128,2560]{1,0:T(8,128)(2,1)S(1)}, bf16[128,2560]{1,0:T(8,128)(2,1)S(1)}, u32[]{:S(2)}, u32[]{:S(2)}) collective-permute-start(bf16[128,2560]{1,0:T(8,128)(2,1)S(1)} %get-tuple-element.331), channel_id=1, source_target_pairs={{0,2},{2,0},{4,6},{6,4},{1,3},{3,1},{5,7},{7,5},{8,10},{10,8},{12,... | collective-permute-start | bytes 1966088 | tf_op jit(solution)/shard_map/ppermute | solution.py:83
  222.4 24.2 %collective-permute-start.54 = (bf16[512,512]{1,0:T(8,128)(2,1)S(1)}, bf16[512,512]{1,0:T(8,128)(2,1)S(1)}, u32[]{:S(2)}, u32[]{:S(2)}) collective-permute-start(bf16[512,512]{1,0:T(8,128)(2,1)S(1)} %get-tuple-element.326), channel_id=1, source_target_pairs={{0,8},{8,0},{16,24},{24,16},{1,9},{9,1},{17,25},{25,17},{2,10},{10... | collective-permute-start | bytes 1572872 | tf_op jit(solution)/shard_map/ppermute | solution.py:83
  229.5 18.1 %collective-permute-start.55 = (bf16[512,512]{1,0:T(8,128)(2,1)S(1)}, bf16[512,512]{1,0:T(8,128)(2,1)S(1)}, u32[]{:S(2)}, u32[]{:S(2)}) collective-permute-start(bf16[512,512]{1,0:T(8,128)(2,1)S(1)} %get-tuple-element.328), channel_id=1, source_target_pairs={{0,16},{8,24},{16,0},{24,8},{1,17},{9,25},{17,1},{25,9},{2,18},{10... | collective-permute-start | bytes 1572872 | tf_op jit(solution)/shard_map/ppermute | solution.py:83
  236.7 19.0 %collective-permute-start.50 = (bf16[288,512]{1,0:T(8,128)(2,1)S(1)}, bf16[288,512]{1,0:T(8,128)(2,1)S(1)}, u32[]{:S(2)}, u32[]{:S(2)}) collective-permute-start(bf16[288,512]{1,0:T(8,128)(2,1)S(1)} %get-tuple-element.309), channel_id=1, source_target_pairs={{0,16},{8,24},{16,0},{24,8},{1,17},{9,25},{17,1},{25,9},{2,18},{10... | collective-permute-start | bytes 884744 | tf_op jit(solution)/shard_map/ppermute | solution.py:83
  256.0 22.7 %collective-permute-start.36 = (f32[512,256]{1,0:T(8,128)S(1)}, f32[512,256]{1,0:T(8,128)S(1)}, u32[]{:S(2)}, u32[]{:S(2)}) collective-permute-start(f32[512,256]{1,0:T(8,128)S(1)} %get-tuple-element.283), channel_id=1, source_target_pairs={{0,1},{1,0},{2,3},{3,2},{4,5},{5,4},{6,7},{7,6},{8,9},{9,8},{10,11... | collective-permute-start | bytes 1572872 | tf_op jit(solution)/shard_map/ppermute | solution.py:83
  256.0 22.7 %collective-permute-start.37 = (f32[512,256]{1,0:T(8,128)S(1)}, f32[512,256]{1,0:T(8,128)S(1)}, u32[]{:S(2)}, u32[]{:S(2)}) collective-permute-start(f32[512,256]{1,0:T(8,128)S(1)} %get-tuple-element.284), channel_id=1, source_target_pairs={{0,1},{1,0},{2,3},{3,2},{4,5},{5,4},{6,7},{7,6},{8,9},{9,8},{10,11... | collective-permute-start | bytes 1572872 | tf_op jit(solution)/shard_map/ppermute | solution.py:83
  257.6 19.3 %collective-permute-start.62 = (bf16[64,2560]{1,0:T(8,128)(2,1)S(1)}, bf16[64,2560]{1,0:T(8,128)(2,1)S(1)}, u32[]{:S(2)}, u32[]{:S(2)}) collective-permute-start(bf16[64,2560]{1,0:T(8,128)(2,1)S(1)} %get-tuple-element.358), channel_id=1, source_target_pairs={{0,4},{2,6},{4,0},{6,2},{1,5},{3,7},{5,1},{7,3},{8,12},{10,14},{12... | collective-permute-start | bytes 983048 | tf_op jit(solution)/shard_map/ppermute | solution.py:83
  260.0 15.6 %collective-permute-start.61 = (bf16[128,1024]{1,0:T(8,128)(2,1)S(1)}, bf16[128,1024]{1,0:T(8,128)(2,1)S(1)}, u32[]{:S(2)}, u32[]{:S(2)}) collective-permute-start(bf16[128,1024]{1,0:T(8,128)(2,1)S(1)} %get-tuple-element.354), channel_id=1, source_target_pairs={{0,2},{2,0},{4,6},{6,4},{1,3},{3,1},{5,7},{7,5},{8,10},{10,8},{12,... | collective-permute-start | bytes 786440 | tf_op jit(solution)/shard_map/ppermute | solution.py:83
  275.6 15.5 %collective-permute-start.53 = (bf16[96,1024]{1,0:T(8,128)(2,1)S(1)}, bf16[96,1024]{1,0:T(8,128)(2,1)S(1)}, u32[]{:S(2)}, u32[]{:S(2)}) collective-permute-start(bf16[96,1024]{1,0:T(8,128)(2,1)S(1)} %get-tuple-element.317), channel_id=1, source_target_pairs={{0,4},{2,6},{4,0},{6,2},{1,5},{3,7},{5,1},{7,3},{8,12},{10,14},{12... | collective-permute-start | bytes 589832 | tf_op jit(solution)/shard_map/ppermute | solution.py:83
  (52 other events, 361.2 us)
